TPU v7x, 32 devices: a whole 2x2x4 slice. The times are simulated.
32 devices in a mesh: dp: 8 (over y, x, core), tensor: 4 (over z).
Axes of the slice: x: 2, y: 2, z: 4, core: 2. Of those that a mesh axis runs over, the one named last changes fastest.
Arguments:
- layer_in: bfloat16 [8192, 2048], P(('dp', 'tensor')), may hold values from -6 to 6
- w_query: bfloat16 [2048, 2048], P('dp', 'tensor'), may hold values from -0.125 to 0.125
- w_key: bfloat16 [2048, 1024], P('dp', 'tensor'), may hold values from -0.125 to 0.125
- w_value: bfloat16 [2048, 1024], P('dp', 'tensor'), may hold values from -0.125 to 0.125
- w_output: bfloat16 [2048, 2048], P('tensor', 'dp'), may hold values from -1 to 1
- w_gate_up: bfloat16 [2048, 2, 6144], P('dp', None, 'tensor'), may hold values from -0.125 to 0.125
- w_down: bfloat16 [6144, 2048], P('tensor', 'dp'), may hold values from -0.15625 to 0.15625
- pre_gain: bfloat16 [2048], P('dp'), may hold values from 0.5 to 2
- mid_gain: bfloat16 [2048], P('dp'), may hold values from 0.5 to 2
- query_gain: bfloat16 [128], P('dp'), may hold values from 0.5 to 2.5
- key_gain: bfloat16 [128], P('dp'), may hold values from 0.5 to 2.5
- out_grad: bfloat16 [8192, 2048], P(('dp', 'tensor')), may hold values from -6 to 6
Outputs:
- layer_out: bfloat16 [8192, 2048], P(('dp', 'tensor'))
- in_grad: bfloat16 [8192, 2048], P(('dp', 'tensor'))
- grad_query: float32 [2048, 2048], P('dp', 'tensor')
- grad_key: float32 [2048, 1024], P('dp', 'tensor')
- grad_value: float32 [2048, 1024], P('dp', 'tensor')
- grad_output: float32 [2048, 2048], P('tensor', 'dp')
- grad_gate_up: float32 [2048, 2, 6144], P('dp', None, 'tensor')
- grad_down: float32 [6144, 2048], P('tensor', 'dp')
- grad_pre: float32 [2048], P('dp')
- grad_mid: float32 [2048], P('dp')
- grad_qgain: float32 [128], P('dp')
- grad_kgain: float32 [128], P('dp')
All inputs are finite; a program needn't handle non-finite values.
Results may differ from a plain program's by a relative error of at most 0.035.
Values may be sent and summed in bfloat16 or wider, within the bound.
No kernel may reach another device: no remote copies, remote signals or barrier semaphores. Data moves between devices by JAX's collectives and lax.ppermute only.
A program may use at most 256 MiB of HBM per device.

v0:
```python
import jax
import jax.numpy as jnp
from jax import lax
from jax.sharding import PartitionSpec as P

L = 1024


EPS = 1e-06
THETA = 1000000.0


def contract_rows(left, right):
    return lax.dot_general(
        left, right, (((0,), (0,)), ((), ())), preferred_element_type=jnp.float32
    )


def contract_cols(left, right):
    return lax.dot_general(
        left, right, (((1,), (1,)), ((), ())), preferred_element_type=jnp.float32
    )


def rope_tables(positions, head_size):
    half = head_size // 2
    freq = THETA ** (-(jnp.arange(half, dtype=jnp.float32) * 2.0) / head_size)
    angle = positions.astype(jnp.float32)[:, None] * freq[None, :]
    cosine = jnp.concatenate([jnp.cos(angle), jnp.cos(angle)], axis=1)[:, None, :]
    sine = jnp.concatenate([jnp.sin(angle), jnp.sin(angle)], axis=1)[:, None, :]
    return (cosine, sine)


def rotate(values, cosine, sine):
    half = values.shape[-1] // 2
    turned = jnp.concatenate([-values[..., half:], values[..., :half]], axis=-1)
    return values * cosine + turned * sine


def unrotate(grads, cosine, sine):
    half = grads.shape[-1] // 2
    scaled = grads * sine
    back = jnp.concatenate([scaled[..., half:], -scaled[..., :half]], axis=-1)
    return grads * cosine + back


def rms_forward(values, gain):
    scale = lax.rsqrt(jnp.mean(values * values, axis=-1, keepdims=True) + EPS)
    return (values * scale * gain, scale)


def rms_back(values, scale, gain, grads):
    normal = values * scale
    scaled = grads * gain
    inner = jnp.mean(scaled * normal, axis=-1, keepdims=True)
    back = scale * (scaled - normal * inner)
    gain_part = jnp.sum((grads * normal).reshape(-1, values.shape[-1]), axis=0)
    return (back, gain_part)


def masked_scores(query, key):
    length = query.shape[0]
    scores = contract_cols(query, key) * query.shape[1] ** (-0.5)
    causal = jnp.arange(length)[:, None] >= jnp.arange(length)[None, :]
    return jnp.where(causal, scores, -1e30)


def head_forward(items):
    query, key, value = items
    scores = masked_scores(query, key)
    total = jax.nn.logsumexp(scores, axis=-1)
    probs = jnp.exp(scores - total[:, None]).astype(jnp.bfloat16)
    mixed = jnp.dot(probs, value, preferred_element_type=jnp.float32).astype(jnp.bfloat16)
    return (mixed, total)


def head_backward(items):
    query, key, value, total, grad_mixed = items
    scores = masked_scores(query, key)
    probs = jnp.exp(scores - total[:, None])
    grad_value = contract_rows(probs.astype(jnp.bfloat16), grad_mixed)
    grad_probs = contract_cols(grad_mixed, value)
    inner = jnp.sum(probs * grad_probs, axis=-1, keepdims=True)
    grad_scores = (probs * (grad_probs - inner) * query.shape[1] ** (-0.5)).astype(jnp.bfloat16)
    grad_query = jnp.dot(grad_scores, key, preferred_element_type=jnp.float32)
    grad_key = contract_rows(grad_scores, query)
    return (grad_query, grad_key, grad_value)


def to_items(array, seqs):
    rows, heads, size = array.shape
    return (
        array.reshape(seqs, rows // seqs, heads, size)
        .transpose(0, 2, 1, 3)
        .reshape(seqs * heads, rows // seqs, size)
    )


def from_items(array, seqs):
    items, length, size = array.shape
    heads = items // seqs
    return (
        array.reshape(seqs, heads, length, size)
        .transpose(0, 2, 1, 3)
        .reshape(seqs * length, heads * size)
    )


def on_device(
    layer_in,
    w_query,
    w_key,
    w_value,
    w_output,
    w_gate_up,
    w_down,
    pre_gain,
    mid_gain,
    query_gain,
    key_gain,
    out_grad,
):
    gathered = (
        lax.all_gather(w_query, "dp", axis=0, tiled=True),
        lax.all_gather(w_key, "dp", axis=0, tiled=True),
        lax.all_gather(w_value, "dp", axis=0, tiled=True),
        lax.all_gather(w_output, "dp", axis=1, tiled=True),
        lax.all_gather(w_gate_up, "dp", axis=0, tiled=True),
        lax.all_gather(w_down, "dp", axis=1, tiled=True),
        lax.all_gather(pre_gain, "dp", axis=0, tiled=True),
        lax.all_gather(mid_gain, "dp", axis=0, tiled=True),
        lax.all_gather(query_gain, "dp", axis=0, tiled=True),
        lax.all_gather(key_gain, "dp", axis=0, tiled=True),
    )
    (
        query_w,
        key_w,
        value_w,
        output_w,
        gate_up_w,
        down_w,
        pre_full,
        mid_full,
        gain_query,
        gain_key,
    ) = gathered
    width = layer_in.shape[1]
    head_size = gain_query.shape[0]
    query_heads = query_w.shape[1] // head_size
    value_heads = key_w.shape[1] // head_size
    group = query_heads // value_heads
    hidden_units = down_w.shape[0]
    inputs_wide = layer_in.astype(jnp.float32)
    normed_pre, scale_pre = rms_forward(inputs_wide, pre_full)
    normed_pre = normed_pre.astype(jnp.bfloat16)
    normed_full = lax.all_gather(normed_pre, "tensor", axis=0, tiled=True)
    all_rows = normed_full.shape[0]
    seqs = all_rows // L
    cosine, sine = rope_tables(jnp.arange(all_rows) % L, head_size)
    query = jnp.dot(normed_full, query_w, preferred_element_type=jnp.float32).reshape(
        all_rows, query_heads, head_size
    )
    keys = jnp.dot(normed_full, key_w, preferred_element_type=jnp.float32).reshape(
        all_rows, value_heads, head_size
    )
    values = (
        jnp.dot(normed_full, value_w, preferred_element_type=jnp.float32)
        .astype(jnp.bfloat16)
        .reshape(all_rows, value_heads, head_size)
    )
    query_normed, query_scale = rms_forward(query, gain_query)
    keys_normed, keys_scale = rms_forward(keys, gain_key)
    query_items = to_items(rotate(query_normed, cosine, sine).astype(jnp.bfloat16), seqs)
    keys_items = to_items(
        jnp.repeat(rotate(keys_normed, cosine, sine).astype(jnp.bfloat16), group, axis=1), seqs
    )
    value_items = to_items(jnp.repeat(values, group, axis=1), seqs)
    mixed, totals = lax.map(head_forward, (query_items, keys_items, value_items))
    attention = from_items(mixed, seqs)
    resid = inputs_wide + lax.psum_scatter(
        jnp.dot(attention, output_w, preferred_element_type=jnp.float32).astype(jnp.bfloat16),
        "tensor",
        scatter_dimension=0,
        tiled=True,
    ).astype(jnp.float32)
    normed_mid, scale_mid = rms_forward(resid, mid_full)
    normed_mid = normed_mid.astype(jnp.bfloat16)
    mid_rows = lax.all_gather(normed_mid, "tensor", axis=0, tiled=True)
    gate_up_flat = gate_up_w.reshape(width, 2 * hidden_units)
    gate_up = jnp.dot(mid_rows, gate_up_flat, preferred_element_type=jnp.float32).reshape(
        all_rows, 2, hidden_units
    )
    gate = gate_up[:, 0]
    upper = gate_up[:, 1]
    sigma = jax.nn.sigmoid(gate)
    silu = gate * sigma
    hidden = (silu * upper).astype(jnp.bfloat16)
    layer_out = (
        resid
        + lax.psum_scatter(
            jnp.dot(hidden, down_w, preferred_element_type=jnp.float32).astype(jnp.bfloat16),
            "tensor",
            scatter_dimension=0,
            tiled=True,
        ).astype(jnp.float32)
    ).astype(jnp.bfloat16)
    again = (
        lax.all_gather(w_query, "dp", axis=0, tiled=True),
        lax.all_gather(w_key, "dp", axis=0, tiled=True),
        lax.all_gather(w_value, "dp", axis=0, tiled=True),
        lax.all_gather(w_output, "dp", axis=1, tiled=True),
        lax.all_gather(w_gate_up, "dp", axis=0, tiled=True),
        lax.all_gather(w_down, "dp", axis=1, tiled=True),
        lax.all_gather(pre_gain, "dp", axis=0, tiled=True),
        lax.all_gather(mid_gain, "dp", axis=0, tiled=True),
        lax.all_gather(query_gain, "dp", axis=0, tiled=True),
        lax.all_gather(key_gain, "dp", axis=0, tiled=True),
    )
    (
        query_w,
        key_w,
        value_w,
        output_w,
        gate_up_w,
        down_w,
        pre_full,
        mid_full,
        gain_query,
        gain_key,
    ) = again
    gate_up_flat = gate_up_w.reshape(width, 2 * hidden_units)
    cot_full = lax.all_gather(out_grad, "tensor", axis=0, tiled=True)
    grad_hidden = contract_cols(cot_full, down_w)
    part_down = contract_rows(hidden, cot_full)
    grad_gate = grad_hidden * upper * sigma * (1.0 + gate * (1.0 - sigma))
    grad_up = grad_hidden * silu
    grad_flat = (
        jnp.stack([grad_gate, grad_up], axis=1)
        .astype(jnp.bfloat16)
        .reshape(all_rows, 2 * hidden_units)
    )
    part_gate_up = contract_rows(mid_rows, grad_flat).reshape(width, 2, hidden_units)
    grad_mid_in = lax.psum_scatter(
        contract_cols(grad_flat, gate_up_flat).astype(jnp.bfloat16),
        "tensor",
        scatter_dimension=0,
        tiled=True,
    ).astype(jnp.float32)
    back_mid, part_mid = rms_back(resid, scale_mid, mid_full, grad_mid_in)
    grad_resid = out_grad.astype(jnp.float32) + back_mid
    grad_resid_b = grad_resid.astype(jnp.bfloat16)
    resid_full = lax.all_gather(grad_resid_b, "tensor", axis=0, tiled=True)
    part_output = contract_rows(attention, resid_full)
    grad_attn = contract_cols(resid_full, output_w).astype(jnp.bfloat16)
    grad_items = to_items(grad_attn.reshape(all_rows, query_heads, head_size), seqs)
    grad_q, grad_k, grad_v = lax.map(
        head_backward, (query_items, keys_items, value_items, totals, grad_items)
    )
    grad_q = from_items(grad_q, seqs).reshape(all_rows, query_heads, head_size)
    grad_k = from_items(grad_k, seqs).reshape(all_rows, value_heads, group, head_size).sum(axis=2)
    grad_v = from_items(grad_v, seqs).reshape(all_rows, value_heads, group, head_size).sum(axis=2)
    back_query, part_qgain = rms_back(
        query, query_scale, gain_query, unrotate(grad_q, cosine, sine)
    )
    back_keys, part_kgain = rms_back(keys, keys_scale, gain_key, unrotate(grad_k, cosine, sine))
    query_b = back_query.reshape(all_rows, query_heads * head_size).astype(jnp.bfloat16)
    keys_b = back_keys.reshape(all_rows, value_heads * head_size).astype(jnp.bfloat16)
    values_b = grad_v.reshape(all_rows, value_heads * head_size).astype(jnp.bfloat16)
    part_query = contract_rows(normed_full, query_b)
    part_key = contract_rows(normed_full, keys_b)
    part_value = contract_rows(normed_full, values_b)
    first = contract_cols(query_b, query_w)
    second = contract_cols(keys_b, key_w)
    third = contract_cols(values_b, value_w)
    grad_pre_in = lax.psum_scatter(
        (first + second + third).astype(jnp.bfloat16), "tensor", scatter_dimension=0, tiled=True
    ).astype(jnp.float32)
    back_pre, part_pre = rms_back(inputs_wide, scale_pre, pre_full, grad_pre_in)
    in_grad = (grad_resid + back_pre).astype(jnp.bfloat16)
    (
        summed_query,
        summed_key,
        summed_value,
        summed_output,
        summed_gate_up,
        summed_down,
        summed_pre,
        summed_mid,
        summed_qgain,
        summed_kgain,
    ) = (
        lax.psum_scatter(
            part_query.astype(jnp.bfloat16), "dp", scatter_dimension=0, tiled=True
        ).astype(jnp.float32),
        lax.psum_scatter(
            part_key.astype(jnp.bfloat16), "dp", scatter_dimension=0, tiled=True
        ).astype(jnp.float32),
        lax.psum_scatter(
            part_value.astype(jnp.bfloat16), "dp", scatter_dimension=0, tiled=True
        ).astype(jnp.float32),
        lax.psum_scatter(
            part_output.astype(jnp.bfloat16), "dp", scatter_dimension=1, tiled=True
        ).astype(jnp.float32),
        lax.psum_scatter(
            part_gate_up.astype(jnp.bfloat16), "dp", scatter_dimension=0, tiled=True
        ).astype(jnp.float32),
        lax.psum_scatter(
            part_down.astype(jnp.bfloat16), "dp", scatter_dimension=1, tiled=True
        ).astype(jnp.float32),
        lax.psum_scatter(
            part_pre.astype(jnp.bfloat16), "dp", scatter_dimension=0, tiled=True
        ).astype(jnp.float32),
        lax.psum_scatter(
            part_mid.astype(jnp.bfloat16), "dp", scatter_dimension=0, tiled=True
        ).astype(jnp.float32),
        lax.psum_scatter(
            part_qgain.astype(jnp.bfloat16), "dp", scatter_dimension=0, tiled=True
        ).astype(jnp.float32),
        lax.psum_scatter(
            part_kgain.astype(jnp.bfloat16), "dp", scatter_dimension=0, tiled=True
        ).astype(jnp.float32),
    )
    grad_pre, grad_mid, grad_qgain, grad_kgain = lax.psum(
        (summed_pre, summed_mid, summed_qgain, summed_kgain), "tensor"
    )
    return (
        layer_out,
        in_grad,
        summed_query,
        summed_key,
        summed_value,
        summed_output,
        summed_gate_up,
        summed_down,
        grad_pre,
        grad_mid,
        grad_qgain,
        grad_kgain,
    )


def solution(mesh):
    placed = (
        P(("dp", "tensor"), None),
        P("dp", "tensor"),
        P("dp", "tensor"),
        P("dp", "tensor"),
        P("tensor", "dp"),
        P("dp", None, "tensor"),
        P("tensor", "dp"),
        P("dp"),
        P("dp"),
        P("dp"),
        P("dp"),
        P(("dp", "tensor"), None),
    )
    return jax.shard_map(
        on_device,
        mesh=mesh,
        in_specs=placed,
        out_specs=(
            P(("dp", "tensor"), None),
            P(("dp", "tensor"), None),
            P("dp", "tensor"),
            P("dp", "tensor"),
            P("dp", "tensor"),
            P("tensor", "dp"),
            P("dp", None, "tensor"),
            P("tensor", "dp"),
            P("dp"),
            P("dp"),
            P("dp"),
            P("dp"),
        ),
        check_vma=False,
    )
```

profile of v0, /device:TPU:0, one launch (start us, length us, event | category | flops | bytes accessed | tf_op | source)
XLA Modules:
  0.0 1276.3 jit_solution(18362501459463488901)
XLA Ops:
  8.6 10.4 all-gather
  27.5 13.6 %all-reduce.8 = (bf16[128]{0:T(256)(128)(2,1)S(1)}, bf16[128]{0:T(256)(128)(2,1)S(1)}) all-reduce(bf16[128]{0:T(256)(128)(2,1)S(1)} %dynamic-update-slice, bf16[128]{0:T(256)(128)(2,1)S(1)} %dynamic-update-slice.1), channel_id=1, replica_groups=mesh['dp'=8,'tensor'=4] {'dp'}, use_global_device_ids=true, to_apply=%add | all-reduce | flops 256 | bytes 1024
  43.4 80.0 %all-gather.13.cloned.1.call-done = bf16[1024,2048]{1,0:T(8,128)(2,1)} async-done(((bf16[256,2048]{1,0:T(8,128)(2,1)}), bf16[1024,2048]{1,0:T(8,128)(2,1)}) %all-gather.13.cloned.1.call-update) | async-done | bytes 4194320 | tf_op jit(solution)/shard_map/all_gather | solution.py:156
  137.3 9.9 all-gather.17.cloned.1.call-done
  154.1 18.3 %all-gather.19.cloned.1.call-done = bf16[2048,256]{1,0:T(8,128)(2,1)} async-done(((bf16[256,256]{1,0:T(8,128)(2,1)}), bf16[2048,256]{1,0:T(8,128)(2,1)}) %all-gather.19.cloned.1.call-update) | async-done | bytes 1048592 | tf_op jit(solution)/shard_map/all_gather | solution.py:126
  185.5 26.9 %while.26 = (s32[]{:T(128)}, bf16[4,1024,128]{1,2,0:T(8,128)(2,1)}, f32[4,1024]{1,0:T(4,128)S(1)}, bf16[4,1024,128]{2,1,0:T(8,128)(2,1)S(1)}, bf16[4,1024,128]{2...) while((s32[]{:T(128)}, bf16[4,1024,128]{1,2,0:T(8,128)(2,1)}, ...), condition=%wide.region_6.7_spmd, body=%wide.region_3.6_spmd.sunk | while | flops 551689216 | bytes 31520884 | solution.py:178
  212.4 7.0 convolution_convert_fusion.3
  222.2 8.8 all-gather.1
  231.1 65.3 %reduce-scatter.11.cloned.1.call-done = bf16[256,2048]{1,0:T(8,128)(2,1)} async-done(((bf16[1024,2048]{1,0:T(8,128)(2,1)}), bf16[256,2048]{1,0:T(8,128)(2,1)}) %reduce-scatter.11.cloned.1.call-update) | async-done | bytes 1048592 | tf_op jit(solution)/shard_map/reduce_scatter | solution.py:180
  301.0 70.4 %all-gather.25.cloned.1.call-done = bf16[2048,2,1536]{2,0,1:T(8,128)(2,1)} async-done(((bf16[256,2,1536]{2,0,1:T(8,128)(2,1)}), bf16[2048,2,1536]{2,0,1:T(8,128)(2,1)}) %all-gather.25.cloned.1.call-update) | async-done | bytes 12582928 | tf_op jit(solution)/shard_map/all_gather | solution.py:128
  371.4 16.9 %copy.96 = bf16[2048,2,1536]{0,2,1:T(8,128)(2,1)} copy(bf16[2048,2,1536]{2,0,1:T(8,128)(2,1)} %all-gather.25.cloned.1.call-done) | data formatting | bytes 25165824 | tf_op jit(solution)/shard_map/all_gather | solution.py:128
  388.2 66.1 %all-gather.23.cloned.1.call-done = bf16[1024,2048]{1,0:T(8,128)(2,1)} async-done(((bf16[256,2048]{1,0:T(8,128)(2,1)}), bf16[1024,2048]{1,0:T(8,128)(2,1)}) %all-gather.23.cloned.1.call-update) | async-done | bytes 4194320 | tf_op jit(solution)/shard_map/all_gather | solution.py:188
  454.3 19.2 %fusion.47 = f32[1024,2,1536]{2,0,1:T(8,128)} fusion(bf16[2048,2,1536]{0,2,1:T(8,128)(2,1)} %copy.96, bf16[1024,2048]{1,0:T(8,128)(2,1)} %all-gather.23.cloned.1.call-done), kind=kOutput, calls=%fused_computation.59 | convolution fusion | flops 12884901888 | bytes 29360128 | tf_op jit(solution)/shard_map/dot_general | solution.py:190
  473.5 61.6 %all-gather.29.cloned.1.call-done = bf16[1024,2048]{1,0:T(8,128)(2,1)} async-done(((bf16[256,2048]{1,0:T(8,128)(2,1)}), bf16[1024,2048]{1,0:T(8,128)(2,1)}) %all-gather.29.cloned.1.call-update) | async-done | bytes 4194320 | tf_op jit(solution)/shard_map/all_gather | solution.py:232
  535.1 46.8 %all-gather.27.cloned.1.call-done = bf16[1536,2048]{1,0:T(8,128)(2,1)} async-done(((bf16[1536,256]{1,0:T(8,128)(2,1)}), bf16[1536,2048]{1,0:T(8,128)(2,1)}) %all-gather.27.cloned.1.call-update) | async-done | bytes 6291472 | tf_op jit(solution)/shard_map/all_gather | solution.py:129
  581.9 14.3 %multiply_bitcast_fusion.1 = (bf16[1024,1,1536]{2,0,1:T(8,128)(2,1)S(1)}, bf16[1024,1,1536]{2,0,1:T(8,128)(2,1)S(1)}) fusion(f32[1024,2,1536]{2,0,1:T(8,128)} %fusion.47, bf16[1024,2048]{1,0:T(8,128)(2,1)} %all-gather.29.cloned.1.call-done, bf16[1536,2048]{1,0:T(8,128)(2,1)} %all-gather.27.cloned.1.call-done), kind=kOutput, calls=%fused_computation.69 | convolution fusion | flops 6462898176 | bytes 29360128 | tf_op jit(solution)/shard_map/dot_general | solution.py:20
  598.9 17.7 %bitcast_convert_fusion = bf16[1024,2048]{1,0:T(8,128)(2,1)} fusion(bf16[2048,2,1536]{2,0,1:T(8,128)(2,1)} %all-gather.25.cloned.1.call-done, bf16[1024,1,1536]{2,0,1:T(8,128)(2,1)S(1)} %get-tuple-element.214, bf16[1024,1,1536]{2,0,1:T(8,128)(2,1)S(1)} %get-tuple-element.213), kind=kOutput, calls=%fused_computation.62 | convolution fusion | flops 12890144768 | bytes 23068672 | tf_op jit(solution)/shard_map/dot_general | solution.py:20
  616.6 11.7 all-gather.31.cloned.1.call-start
  628.4 65.2 %reduce-scatter.15.cloned.1.call-done = bf16[256,2048]{1,0:T(8,128)(2,1)} async-done(((bf16[1024,2048]{1,0:T(8,128)(2,1)}), bf16[256,2048]{1,0:T(8,128)(2,1)}) %reduce-scatter.15.cloned.1.call-update) | async-done | bytes 1048592 | tf_op jit(solution)/shard_map/reduce_scatter | solution.py:243
  706.0 8.8 convolution_convert_fusion.1
  714.8 65.1 %all-gather.31.cloned.1.call-done = bf16[1024,2048]{1,0:T(8,128)(2,1)} async-done(((bf16[256,2048]{1,0:T(8,128)(2,1)}), bf16[1024,2048]{1,0:T(8,128)(2,1)}) %all-gather.31.cloned.1.call-update) | async-done | bytes 4194320 | tf_op jit(solution)/shard_map/all_gather | solution.py:252
  788.6 35.8 %while.27 = (s32[]{:T(128)}, f32[4,1024,128]{2,1,0:T(8,128)S(1)}, f32[4,1024,128]{2,1,0:T(8,128)}, f32[4,1024,128]{2,1,0:T(8,128)}, bf16[4,1024,128]{2,1,0:T(8,1...) while((s32[]{:T(128)}, f32[4,1024,128]{2,1,0:T(8,128)S(1)}, ...), condition=%wide.region_14.15_spmd, body=%wide.region_12.14_spmd.sunk | while | flops 1353710592 | bytes 39085188 | solution.py:256
  862.6 8.7 copy.105
  890.5 19.8 %convolution_convert_fusion = bf16[2048,2,1536]{2,0,1:T(8,128)(2,1)} fusion(bf16[1024,2,1536]{0,2,1:T(8,128)(2,1)} %copy.105, bf16[1024,2048]{1,0:T(8,128)(2,1)} %all-gather.23.cloned.1.call-done), kind=kOutput, calls=%fused_computation.61 | convolution fusion | flops 12891193344 | bytes 23068672 | tf_op jit(solution)/shard_map/dot_general | solution.py:14
  920.3 11.2 convolution_convert_fusion.2
  941.6 24.1 %reduce-scatter.25.cloned.1.call-done = bf16[512,256]{1,0:T(8,128)(2,1)} async-done(((bf16[512,2048]{1,0:T(8,128)(2,1)}), bf16[512,256]{1,0:T(8,128)(2,1)}) %reduce-scatter.25.cloned.1.call-update) | async-done | bytes 262160 | tf_op jit(solution)/shard_map/reduce_scatter | solution.py:301
  967.5 42.5 %reduce-scatter.19.cloned.1.call-done = bf16[256,512]{1,0:T(8,128)(2,1)} async-done(((bf16[2048,512]{1,0:T(8,128)(2,1)}), bf16[256,512]{1,0:T(8,128)(2,1)}) %reduce-scatter.19.cloned.1.call-update) | async-done | bytes 262160 | tf_op jit(solution)/shard_map/reduce_scatter | solution.py:292
  1011.8 93.7 %reduce-scatter.27.cloned.1.call-done = bf16[256,2,1536]{2,0,1:T(8,128)(2,1)} async-done(((bf16[2048,2,1536]{2,0,1:T(8,128)(2,1)}), bf16[256,2,1536]{2,0,1:T(8,128)(2,1)}) %reduce-scatter.27.cloned.1.call-update) | async-done | bytes 1572880 | tf_op jit(solution)/shard_map/reduce_scatter | solution.py:304
  1110.2 74.4 %reduce-scatter.17.cloned.1.call-done = bf16[256,2048]{1,0:T(8,128)(2,1)} async-done(((bf16[1024,2048]{1,0:T(8,128)(2,1)}), bf16[256,2048]{1,0:T(8,128)(2,1)}) %reduce-scatter.17.cloned.1.call-update) | async-done | bytes 1048592 | tf_op jit(solution)/shard_map/reduce_scatter | solution.py:275
  1186.7 13.9 %all-reduce.7 = (bf16[2048]{0:T(1024)(128)(2,1)S(1)}, bf16[2048]{0:T(1024)(128)(2,1)S(1)}, bf16[128]{0:T(256)(128)(2,1)S(1)}, bf16[128]{0:T(256)(128)(2,1)S(1)}) all-reduce(bf16[2048]{0:T(1024)(128)(2,1)S(1)} %get-tuple-element.161, bf16[2048]{0:T(1024)(128)(2,1)S(1)} %copy-done.47, ...), channel_id=12, replica_groups=mesh['dp'=8,'tensor'=4] {'dp'}, use_global_device_ids=true, to_apply=%region_28.29.clone | all-reduce | flops 4352 | bytes 17408
  1200.9 12.6 all-reduce.6
  1213.4 50.9 %reduce-scatter.13.cloned.1.call-done = bf16[256,2048]{1,0:T(8,128)(2,1)} async-done(((bf16[1024,2048]{1,0:T(8,128)(2,1)}), bf16[256,2048]{1,0:T(8,128)(2,1)}) %reduce-scatter.13.cloned.1.call-update) | async-done | bytes 1048592 | tf_op jit(solution)/shard_map/reduce_scatter | solution.py:200
  (334 shorter events, 229.8 us)
Async XLA Ops:
  7.2 36.3 %all-gather.15.cloned.1.call-start = ((), (), s32[]{:S(2)}) async-start(), calls=%async_computation.11 | async-start | bytes 2359296 | tf_op jit(solution)/shard_map/all_gather | solution.py:124
  7.9 115.5 %all-gather.13.cloned.1.call-start = ((), (), s32[]{:S(2)}) async-start(), calls=%async_computation.10 | async-start | bytes 5242880 | tf_op jit(solution)/shard_map/all_gather | solution.py:156
  23.7 123.5 %all-gather.17.cloned.1.call-start = ((), (), s32[]{:S(2)}) async-start(), calls=%async_computation.12 | async-start | bytes 1179648 | tf_op jit(solution)/shard_map/all_gather | solution.py:125
  24.5 147.9 %all-gather.19.cloned.1.call-start = ((), (), s32[]{:S(2)}) async-start(), calls=%async_computation.13 | async-start | bytes 1179648 | tf_op jit(solution)/shard_map/all_gather | solution.py:126
  25.0 187.4 %all-gather.21.cloned.1.call-start = ((), (), s32[]{:S(2)}) async-start(), calls=%async_computation.14 | async-start | bytes 2359296 | tf_op jit(solution)/shard_map/all_gather | solution.py:127
  25.6 270.7 %reduce-scatter.11.cloned.1.call-start = ((), (), s32[]{:S(2)}) async-start(), calls=%async_computation.15 | async-start | bytes 5242880 | tf_op jit(solution)/shard_map/reduce_scatter | solution.py:180
  41.1 139.9 %copy-start.52 = (f32[128]{0:T(128)}, f32[128]{0:T(128)S(1)}, u32[]{:S(2)}) copy-start(f32[128]{0:T(128)S(1)} %convert_element_type.190) | copy-start | bytes 1540
  43.4 137.6 %copy-start.5 = (f32[1024,128]{1,0:T(8,128)}, f32[1024,128]{1,0:T(8,128)S(1)}, u32[]{:S(2)}) copy-start(f32[1024,128]{1,0:T(8,128)S(1)} %get-tuple-element.237) | copy-start | bytes 1572868
  219.5 151.9 %all-gather.25.cloned.1.call-start = ((), (), s32[]{:S(2)}) async-start(), calls=%async_computation.17 | async-start | bytes 14155776 | tf_op jit(solution)/shard_map/all_gather | solution.py:128
  222.2 232.1 %all-gather.23.cloned.1.call-start = ((), (), s32[]{:S(2)}) async-start(), calls=%async_computation.16 | async-start | bytes 5242880 | tf_op jit(solution)/shard_map/all_gather | solution.py:188
  231.1 465.3 %copy-start.41 = (f32[8,1,256]{2,1,0:T(1,128)}, f32[8,1,256]{2,1,0:T(1,128)S(1)}, u32[]{:S(2)}) copy-start(f32[8,1,256]{2,1,0:T(1,128)S(1)} %convert_element_type.239) | copy-start | bytes 24580
  298.1 398.3 %copy-start.45 = (f32[256]{0:T(256)}, f32[256]{0:T(256)S(1)}, u32[]{:S(2)}) copy-start(f32[256]{0:T(256)S(1)} %add_rsqrt_fusion.2) | copy-start | bytes 3076
  299.6 235.5 %all-gather.29.cloned.1.call-start = ((), (), s32[]{:S(2)}) async-start(), calls=%async_computation.20 | async-start | bytes 5242880 | tf_op jit(solution)/shard_map/all_gather | solution.py:232
  300.4 281.6 %all-gather.27.cloned.1.call-start = ((), (), s32[]{:S(2)}) async-start(), calls=%async_computation.18 | async-start | bytes 7077888 | tf_op jit(solution)/shard_map/all_gather | solution.py:129
  301.0 392.6 %reduce-scatter.15.cloned.1.call-start = ((), (), s32[]{:S(2)}) async-start(), calls=%async_computation.21 | async-start | bytes 5242880 | tf_op jit(solution)/shard_map/reduce_scatter | solution.py:243
  616.6 163.2 %all-gather.31.cloned.1.call-start = ((), (), s32[]{:S(2)}) async-start(), calls=%async_computation.22 | async-start | bytes 5242880 | tf_op jit(solution)/shard_map/all_gather | solution.py:252
  698.5 234.3 %reduce-scatter.29.cloned.1.call-start = ((), (), s32[]{:S(2)}) async-start(), calls=%async_computation.29 | async-start | bytes 7077888 | tf_op jit(solution)/shard_map/reduce_scatter | solution.py:307
  714.8 223.6 %reduce-scatter.21.cloned.1.call-start = ((), (), s32[]{:S(2)}) async-start(), calls=%async_computation.25 | async-start | bytes 1179648 | tf_op jit(solution)/shard_map/reduce_scatter | solution.py:295
  839.2 100.8 %reduce-scatter.23.cloned.1.call-start = ((), (), s32[]{:S(2)}) async-start(), calls=%async_computation.26 | async-start | bytes 1179648 | tf_op jit(solution)/shard_map/reduce_scatter | solution.py:298
  849.0 116.7 %reduce-scatter.25.cloned.1.call-start = ((), (), s32[]{:S(2)}) async-start(), calls=%async_computation.27 | async-start | bytes 2359296 | tf_op jit(solution)/shard_map/reduce_scatter | solution.py:301
  855.4 154.6 %reduce-scatter.19.cloned.1.call-start = ((), (), s32[]{:S(2)}) async-start(), calls=%async_computation.24 | async-start | bytes 2359296 | tf_op jit(solution)/shard_map/reduce_scatter | solution.py:292
  890.3 215.2 %reduce-scatter.27.cloned.1.call-start = ((), (), s32[]{:S(2)}) async-start(), calls=%async_computation.28 | async-start | bytes 14155776 | tf_op jit(solution)/shard_map/reduce_scatter | solution.py:304
  910.3 274.3 %reduce-scatter.17.cloned.1.call-start = ((), (), s32[]{:S(2)}) async-start(), calls=%async_computation.23 | async-start | bytes 5242880 | tf_op jit(solution)/shard_map/reduce_scatter | solution.py:275
  920.0 344.4 %reduce-scatter.13.cloned.1.call-start = ((), (), s32[]{:S(2)}) async-start(), calls=%async_computation.19 | async-start | bytes 5242880 | tf_op jit(solution)/shard_map/reduce_scatter | solution.py:200
  1011.8 172.8 %copy-start.2 = (bf16[256,2048]{1,0:T(8,128)(2,1)S(1)}, bf16[256,2048]{1,0:T(8,128)(2,1)}, u32[]{:S(2)}) copy-start(bf16[256,2048]{1,0:T(8,128)(2,1)} %param.16) | copy-start | bytes 3145732
  1011.8 172.8 %copy-start.44 = (f32[8,1,256]{2,1,0:T(1,128)S(1)}, f32[8,1,256]{2,1,0:T(1,128)}, u32[]{:S(2)}) copy-start(f32[8,1,256]{2,1,0:T(1,128)} %copy-done.43) | copy-start | bytes 24580
  1011.8 172.8 %copy-start.49 = (f32[256]{0:T(256)S(1)}, f32[256]{0:T(256)}, u32[]{:S(2)}) copy-start(f32[256]{0:T(256)} %copy-done.48) | copy-start | bytes 3076
  1110.2 154.2 %copy-start.4 = (bf16[256,2048]{1,0:T(8,128)(2,1)S(1)}, bf16[256,2048]{1,0:T(8,128)(2,1)}, u32[]{:S(2)}) copy-start(bf16[256,2048]{1,0:T(8,128)(2,1)} %reduce-scatter.11.cloned.1.call-done) | copy-start | bytes 3145732
  1110.2 154.2 %copy-start.20 = (bf16[256,2048]{1,0:T(8,128)(2,1)S(1)}, bf16[256,2048]{1,0:T(8,128)(2,1)}, u32[]{:S(2)}) copy-start(bf16[256,2048]{1,0:T(8,128)(2,1)} %param.27) | copy-start | bytes 3145732
  1110.2 154.2 %copy-start.42 = (f32[8,1,256]{2,1,0:T(1,128)S(1)}, f32[8,1,256]{2,1,0:T(1,128)}, u32[]{:S(2)}) copy-start(f32[8,1,256]{2,1,0:T(1,128)} %copy-done.41) | copy-start | bytes 24580
  1110.2 154.2 %copy-start.46 = (f32[256]{0:T(256)S(1)}, f32[256]{0:T(256)}, u32[]{:S(2)}) copy-start(f32[256]{0:T(256)} %copy-done.45) | copy-start | bytes 3076
  1110.2 154.2 %copy-start.51 = (f32[256]{0:T(256)S(1)}, f32[256]{0:T(256)}, u32[]{:S(2)}) copy-start(f32[256]{0:T(256)} %copy-done.50) | copy-start | bytes 3076
  (55 other events, 628.9 us)
Sparse Core Ops, SparseCore 0:
  9.9 30.5 all-gather.14
  42.7 80.7 all-gather.12
  125.3 21.8 all-gather.16
  149.0 23.3 all-gather.18
  174.1 28.0 all-gather.20
  219.6 76.7 reduce-scatter.10
  298.8 72.4 all-gather.24
  373.5 80.7 all-gather.22
  455.8 79.2 all-gather.28
  536.8 45.0 all-gather.26
  616.7 76.7 reduce-scatter.14
  698.6 81.2 all-gather.30
  783.2 60.0 reduce-scatter.28
  846.4 35.9 reduce-scatter.20
  885.4 35.9 reduce-scatter.22
  924.6 41.0 reduce-scatter.24
  968.8 41.1 reduce-scatter.18
  1013.3 92.1 reduce-scatter.26
  1107.8 76.7 reduce-scatter.16
  1186.8 77.5 reduce-scatter.12
where the time goes:
time: 1290 us; the launch traced here: 1280 us
  waiting for transfers between devices  838 us (65%)
  matrix products  191 us (15%)
  other arithmetic  81.9 us (6%)
  local copies, waits for them, and re-layouts  74.5 us (6%)
  blocking collectives  59.2 us (5%)
  between operations  17.3 us (1%)
  starting transfers between devices  13.3 us (1%)
    reduce_scatter x1, waiting for transfers between devices, on_device(): lax.psum_scatter(part_gate_up.astype(jnp.bfloat16), 'dp', scatter_dimensi...  93.7 us
    all_gather x1, waiting for transfers between devices, on_device(): normed_full = lax.all_gather(normed_pre, 'tensor', axis=0, tiled=True)  80 us
    reduce_scatter x1, waiting for transfers between devices, on_device(): lax.psum_scatter((first + second + third).astype(jnp.bfloat16), 'tensor',...  74.4 us
    all_gather x1, waiting for transfers between devices, on_device(): lax.all_gather(w_gate_up, 'dp', axis=0, tiled=True)  70.4 us
    all_gather x1, waiting for transfers between devices, on_device(): mid_rows = lax.all_gather(normed_mid, 'tensor', axis=0, tiled=True)  66.1 us
    reduce_scatter x1, waiting for transfers between devices, on_device(): lax.psum_scatter(jnp.dot(attention, output_w, preferred_element_type=jnp....  65.3 us
    reduce_scatter x1, waiting for transfers between devices, on_device(): lax.psum_scatter(contract_cols(grad_flat, gate_up_flat).astype(jnp.bfloat...  65.2 us
    all_gather x1, waiting for transfers between devices, on_device(): resid_full = lax.all_gather(grad_resid_b, 'tensor', axis=0, tiled=True)  65.1 us
  transfers between devices with their start and end apart: 20, of which 15 were waited for; matrix products, arithmetic and copies ran while one was open for 22% of the time, Pallas kernels for 0%

commit v1 on v0

v1 whole, which is shorter than its diff:
```python
import functools

import jax
import jax.numpy as jnp
from jax import lax
from jax.experimental import pallas as pl
from jax.experimental.pallas import tpu as pltpu
from jax.sharding import PartitionSpec as P

L = 1024


EPS = 1e-06
THETA = 1000000.0
F32 = jnp.float32
BF16 = jnp.bfloat16
BLOCK = 256


barrier = lax.optimization_barrier


def dot(left, right):
    return jnp.dot(left, right, preferred_element_type=F32)


def contract_rows(left, right):
    return lax.dot_general(left, right, (((0,), (0,)), ((), ())), preferred_element_type=F32)


def contract_cols(left, right):
    return lax.dot_general(left, right, (((1,), (1,)), ((), ())), preferred_element_type=F32)


def rope_tables(head_size):
    half = head_size // 2
    freq = THETA ** (-(jnp.arange(half, dtype=F32) * 2.0) / head_size)
    angle = jnp.arange(L).astype(F32)[:, None] * freq[None, :]
    cosine, sine = jnp.cos(angle), jnp.sin(angle)
    return (
        jnp.concatenate([cosine, cosine], axis=1),
        jnp.concatenate([-sine, sine], axis=1),
    )


def rms_scale(values):
    return lax.rsqrt(jnp.mean(values * values, axis=-1, keepdims=True) + EPS)


def rms_back(normal, scale, gain, grads):
    scaled = grads * gain
    inner = jnp.mean(scaled * normal, axis=-1, keepdims=True)
    return scale * (scaled - normal * inner)


def turn(values):
    return pltpu.roll(values, values.shape[-1] // 2, 1)


def causal_block(scores_t):
    keys = lax.broadcasted_iota(jnp.int32, scores_t.shape, 0)
    queries = lax.broadcasted_iota(jnp.int32, scores_t.shape, 1)
    return keys <= queries


def attention_forward(group, size, q_ref, k_ref, v_ref, cos_ref, sin_ref, gq_ref, gk_ref, out_ref, lse_ref):
    cosine, sine = cos_ref[...], sin_ref[...]
    factor = size ** (-0.5)
    keys = k_ref[...]
    keys = keys * rms_scale(keys) * gk_ref[...]
    keys = (keys * cosine + turn(keys) * sine).astype(BF16)
    values_t = v_ref[...].T.astype(BF16)
    for h in range(group):
        query = q_ref[:, h * size : (h + 1) * size]
        query = query * rms_scale(query) * gq_ref[...]
        query = (query * cosine + turn(query) * sine).astype(BF16)
        for b in range(L // BLOCK):
            lo, hi = b * BLOCK, (b + 1) * BLOCK
            scores = contract_cols(keys[:hi], query[lo:hi]) * factor
            powers = jnp.exp(scores)
            last = jnp.where(causal_block(powers[lo:]), powers[lo:], 0.0)
            powers = jnp.concatenate([powers[:lo], last], axis=0) if lo else last
            total = jnp.sum(powers, axis=0, keepdims=True)
            probs = (powers * (1.0 / total)).astype(BF16)
            mixed_t = dot(values_t[:, :hi], probs)
            out_ref[lo:hi, h * size : (h + 1) * size] = mixed_t.T.astype(BF16)
            lse_ref[0, h : h + 1, lo:hi] = jnp.log(total)


def attention_backward(
    group, size, heads, kv_heads, q_ref, k_ref, v_ref, grad_ref, lse_ref, cos_ref, sin_ref, gq_ref, gk_ref,
    out_ref, gain_ref, dk_ref, dv_ref, dq_ref,
):
    first = (pl.program_id(0) == 0) & (pl.program_id(1) == 0)

    @pl.when(first)
    def _():
        gain_ref[...] = jnp.zeros_like(gain_ref)

    at = pl.program_id(1)
    cosine, sine = cos_ref[...], sin_ref[...]
    factor = size ** (-0.5)
    raw_k = k_ref[...]
    scale_k = rms_scale(raw_k)
    normal_k = raw_k * scale_k
    keys = normal_k * gk_ref[...]
    keys = keys * cosine + turn(keys) * sine
    keys_t = keys.T.astype(BF16)
    keys = keys.astype(BF16)
    values = v_ref[...].astype(BF16)
    dk_ref[...] = jnp.zeros_like(dk_ref)
    dv_ref[...] = jnp.zeros_like(dv_ref)
    for h in range(group):
        cols = slice(h * size, (h + 1) * size)
        raw_q = q_ref[:, cols]
        scale_q = rms_scale(raw_q)
        normal_q = raw_q * scale_q
        query = normal_q * gq_ref[...]
        query = (query * cosine + turn(query) * sine).astype(BF16)
        grad = grad_ref[:, cols]
        for b in range(L // BLOCK):
            lo, hi = b * BLOCK, (b + 1) * BLOCK
            q_b, g_b = query[lo:hi], grad[lo:hi]
            scores = contract_cols(keys[:hi], q_b) * factor
            probs = jnp.exp(scores - lse_ref[0, h : h + 1, lo:hi])
            last = jnp.where(causal_block(probs[lo:]), probs[lo:], 0.0)
            probs = jnp.concatenate([probs[:lo], last], axis=0) if lo else last
            dv_ref[:hi] += dot(probs.astype(BF16), g_b)
            grad_probs = contract_cols(values[:hi], g_b)
            inner = jnp.sum(probs * grad_probs, axis=0, keepdims=True)
            grad_scores = (probs * (grad_probs - inner) * factor).astype(BF16)
            dk_ref[:hi] += dot(grad_scores, q_b)
            dq_ref[lo:hi] = dot(keys_t[:, :hi], grad_scores).T
        dq = dq_ref[...]
        dqn = dq * cosine - turn(dq) * sine
        gain_ref[0:1] += jnp.sum(dqn * normal_q, axis=0, keepdims=True)
        back = rms_back(normal_q, scale_q, gq_ref[...], dqn)
        out_ref[:, pl.ds(pl.multiple_of((at * group + h) * size, size), size)] = back.astype(BF16)
    dk = dk_ref[...]
    dkn = dk * cosine - turn(dk) * sine
    gain_ref[1:2] += jnp.sum(dkn * normal_k, axis=0, keepdims=True)
    back = rms_back(normal_k, scale_k, gk_ref[...], dkn)
    out_ref[:, pl.ds(pl.multiple_of((heads + at) * size, size), size)] = back.astype(BF16)
    out_ref[:, pl.ds(pl.multiple_of((heads + kv_heads + at) * size, size), size)] = dv_ref[...].astype(BF16)


def hidden_kernel(
    mid_ref, og_ref, gate_ref, up_ref, down_ref, hidden_ref, grad_gate_ref, grad_up_ref, back_ref, out_ref
):
    mid, gate_w, up_w, down_w = mid_ref[...], gate_ref[0], up_ref[0], down_ref[...]
    gate = dot(mid, gate_w)
    upper = dot(mid, up_w)
    grad_hidden = contract_cols(og_ref[...], down_w)
    sigma = 1.0 / (1.0 + jnp.exp(-gate))
    silu = gate * sigma
    hidden = (silu * upper).astype(BF16)
    grad_gate = (grad_hidden * upper * sigma * (1.0 + gate * (1.0 - sigma))).astype(BF16)
    grad_up = (grad_hidden * silu).astype(BF16)
    hidden_ref[...] = hidden
    grad_gate_ref[...] = grad_gate
    grad_up_ref[...] = grad_up
    back = contract_cols(grad_gate, gate_w) + contract_cols(grad_up, up_w)
    out = dot(hidden, down_w)

    @pl.when(pl.program_id(0) == 0)
    def _():
        back_ref[...] = back
        out_ref[...] = out

    @pl.when(pl.program_id(0) > 0)
    def _():
        back_ref[...] += back
        out_ref[...] += out


def hidden_piece(mid, og, gate_up_w, down_w):
    rows, width = mid.shape
    units = down_w.shape[0]
    tile = min(512, units)
    whole = pl.BlockSpec((rows, width), lambda j: (0, 0))
    out = pl.BlockSpec((rows, tile), lambda j: (0, j))
    return pl.pallas_call(
        hidden_kernel,
        grid=(units // tile,),
        in_specs=[
            whole,
            whole,
            pl.BlockSpec((1, width, tile), lambda j: (0, 0, j)),
            pl.BlockSpec((1, width, tile), lambda j: (1, 0, j)),
            pl.BlockSpec((tile, width), lambda j: (j, 0)),
        ],
        out_specs=(out, out, out, whole, whole),
        out_shape=tuple(jax.ShapeDtypeStruct((rows, units), BF16) for _ in range(3))
        + tuple(jax.ShapeDtypeStruct((rows, width), F32) for _ in range(2)),
        cost_estimate=pl.CostEstimate(
            flops=12 * rows * width * units,
            transcendentals=rows * units,
            bytes_accessed=6 * width * units + 12 * rows * width + 6 * rows * units,
        ),
        name="hidden_piece",
    )(mid, og, gate_up_w, gate_up_w, down_w)


def qkv_specs(group, size, heads, kv_heads):
    return [
        pl.BlockSpec((L, group * size), lambda s, g: (s, g)),
        pl.BlockSpec((L, size), lambda s, g: (s, heads + g)),
        pl.BlockSpec((L, size), lambda s, g: (s, heads + kv_heads + g)),
    ]


def forward_heads(qkv, cosine, sine, gain_q, gain_k, heads, kv_heads):
    rows, size, group = qkv.shape[0], cosine.shape[1], heads // kv_heads
    fixed = pl.BlockSpec((L, size), lambda s, g: (0, 0))
    gain = pl.BlockSpec((1, size), lambda s, g: (0, 0))
    return pl.pallas_call(
        functools.partial(attention_forward, group, size),
        grid=(rows // L, kv_heads),
        in_specs=qkv_specs(group, size, heads, kv_heads) + [fixed, fixed, gain, gain],
        out_specs=(
            pl.BlockSpec((L, group * size), lambda s, g: (s, g)),
            pl.BlockSpec((1, group, L), lambda s, g: (s * kv_heads + g, 0, 0)),
        ),
        out_shape=(
            jax.ShapeDtypeStruct((rows, heads * size), BF16),
            jax.ShapeDtypeStruct((rows // L * kv_heads, group, L), F32),
        ),
        cost_estimate=pl.CostEstimate(
            flops=4 * heads * rows * L * size,
            transcendentals=heads * rows * L,
            bytes_accessed=rows * (heads + 2 * kv_heads) * size * 4 + rows * heads * size * 2,
        ),
        name="attention_forward",
    )(qkv, qkv, qkv, cosine, sine, gain_q, gain_k)


def backward_heads(qkv, grad, lse, cosine, sine, gain_q, gain_k, heads, kv_heads):
    rows, size, group = qkv.shape[0], cosine.shape[1], heads // kv_heads
    width = (heads + 2 * kv_heads) * size
    fixed = pl.BlockSpec((L, size), lambda s, g: (0, 0))
    gain = pl.BlockSpec((1, size), lambda s, g: (0, 0))
    return pl.pallas_call(
        functools.partial(attention_backward, group, size, heads, kv_heads),
        grid=(rows // L, kv_heads),
        in_specs=qkv_specs(group, size, heads, kv_heads)
        + [
            pl.BlockSpec((L, group * size), lambda s, g: (s, g)),
            pl.BlockSpec((1, group, L), lambda s, g: (s * kv_heads + g, 0, 0)),
            fixed,
            fixed,
            gain,
            gain,
        ],
        out_specs=(
            pl.BlockSpec((L, width), lambda s, g: (s, 0)),
            pl.BlockSpec((2, size), lambda s, g: (0, 0)),
        ),
        out_shape=(
            jax.ShapeDtypeStruct((rows, width), BF16),
            jax.ShapeDtypeStruct((2, size), F32),
        ),
        scratch_shapes=[pltpu.VMEM((L, size), F32)] * 3,
        cost_estimate=pl.CostEstimate(
            flops=10 * heads * rows * L * size,
            transcendentals=heads * rows * L,
            bytes_accessed=rows * width * 6 + rows * heads * size * 2,
        ),
        name="attention_backward",
    )(qkv, qkv, qkv, grad, lse, cosine, sine, gain_q, gain_k)


def on_device(
    devices,
    layer_in,
    w_query,
    w_key,
    w_value,
    w_output,
    w_gate_up,
    w_down,
    pre_gain,
    mid_gain,
    query_gain,
    key_gain,
    out_grad,
):
    dp, parts = devices
    ring = [(i, (i + 1) % parts) for i in range(parts)]
    me = lax.axis_index("tensor")
    mine = lax.axis_index("dp")
    rows, width = layer_in.shape
    all_rows = rows * parts
    head_size = query_gain.shape[0] * dp
    heads = w_query.shape[1] // head_size
    kv_heads = w_key.shape[1] // head_size

    def place(k):
        return (me + parts - k) % parts

    def around(block):
        return lax.ppermute(block, "tensor", ring)

    def gather_ring(block):
        blocks = [block]
        for _ in range(parts - 1):
            blocks.append(around(blocks[-1]))
        return blocks

    def scatter_ring(part, fillers=()):
        order = list(range(1, parts)) + [0]
        made = []
        total = part(order[0])
        for j, k in enumerate(order[1:]):
            moving = around(total.astype(BF16))
            new = fillers[j]() if j < len(fillers) else ()
            moving, ahead, new = barrier((moving, part(k), new))
            total = ahead + moving.astype(F32)
            made.append(new)
        return total, made

    def scattered(part, axis):
        return lax.psum_scatter(part, "dp", scatter_dimension=axis, tiled=True)

    bits = dp.bit_length() - 1

    def halve(block, left, bit):
        axis, own = left.index(bit), (mine >> bit) & 1
        keep, give = (lax.dynamic_index_in_dim(block, at, axis, keepdims=False) for at in (own, 1 - own))
        took = lax.ppermute(give, "dp", [(i, i ^ (1 << bit)) for i in range(dp)])
        return (keep.astype(F32) + took.astype(F32)).astype(BF16), [b for b in left if b != bit]

    def halves_start(part):
        block = part.reshape((2,) * bits + (part.shape[0] // dp, part.shape[1]))
        return halve(block, list(range(bits))[::-1], 0)

    def halves_split(state):
        block, left = state
        cut = block.shape[-1] // 2
        rest = sorted(left)
        return [(block[..., :cut], left, rest), (block[..., cut:], left, rest[::-1])]

    def halves_step(states):
        return [(*halve(block, left, order[0]), order[1:]) for block, left, order in states]

    def halves_end(states):
        while states[0][2]:
            states = halves_step(states)
        return jnp.concatenate([block for block, _, _ in states], axis=-1)

    def butterfly(values):
        for axis, size in (("dp", dp), ("tensor", parts)):
            for bit in range(size.bit_length() - 1):
                values = values + lax.ppermute(values, axis, [(i, i ^ (1 << bit)) for i in range(size)])
        return values

    sizes = (pre_gain.shape[0], mid_gain.shape[0], query_gain.shape[0], key_gain.shape[0])
    used = sum(sizes)
    packed = jnp.concatenate([pre_gain, mid_gain, query_gain, key_gain])
    packed = jnp.pad(packed, (0, -used % 128)).reshape(1, -1)
    output_w = lax.all_gather(w_output, "tensor", axis=0, tiled=True)
    w_qkv = lax.all_gather(jnp.concatenate([w_query, w_key, w_value], axis=1), "dp", axis=0, tiled=True)
    gate_up_w = lax.all_gather(w_gate_up.transpose(1, 0, 2), "dp", axis=1, tiled=True)
    down_w = lax.all_gather(w_down, "dp", axis=1, tiled=True)

    xs = [layer_in, around(layer_in)]
    output_w, packed, _ = barrier((output_w, packed, xs[1]))
    output_w = lax.all_gather(output_w, "dp", axis=1, tiled=True)
    gains = lax.all_gather(packed, "dp", axis=0, tiled=True).astype(F32)
    starts = [sum(sizes[:i]) for i in range(5)]
    pre_full, mid_full, gain_query, gain_key = (
        gains[:, lo:hi].reshape(1, -1) for lo, hi in zip(starts, starts[1:])
    )
    cosine, sine = rope_tables(head_size)

    normals = []
    qkv = jnp.zeros((all_rows, w_qkv.shape[1]), F32)
    normed_full = jnp.zeros((all_rows, width), BF16)
    for k in range(parts):
        if 0 < k < parts - 1:
            xs.append(around(xs[k]))
        wide = xs[k].astype(F32)
        scale = rms_scale(wide)
        normals.append((wide, scale))
        normed = (wide * scale * pre_full).astype(BF16)
        at = (place(k) * rows, 0)
        normed_full = lax.dynamic_update_slice(normed_full, normed, at)
        qkv = lax.dynamic_update_slice(qkv, dot(normed, w_qkv), at)
        if k == parts - 2:
            qkv, normed_full, xs[-1] = barrier((qkv, normed_full, xs[-1]))

    first_og, _ = barrier((out_grad, xs[-1]))
    ogs = [out_grad, around(first_og)]
    attention, lse = forward_heads(qkv, cosine, sine, gain_query, gain_key, heads, kv_heads)
    attention, ogs[1] = barrier((attention, ogs[1]))
    ogs.append(around(ogs[1]))
    mixed = lax.all_to_all(
        attention.reshape(parts, rows, heads * head_size), "tensor", 0, 0, tiled=True
    )
    mixed = mixed.transpose(1, 0, 2).reshape(rows, parts * heads * head_size)
    mixed, ogs[-1] = barrier((mixed, ogs[-1]))
    for k in range(2, parts - 1):
        ogs.append(around(ogs[k]))
    inputs_wide = normals[0][0]
    resid = inputs_wide + dot(mixed, output_w)
    scale_mid = rms_scale(resid)
    normal_mid = resid * scale_mid
    mids = gather_ring((normal_mid * mid_full).astype(BF16))

    pieces = {}

    def back_part(k):
        pieces[k] = hidden_piece(mids[k], ogs[k], gate_up_w, down_w)
        return pieces[k][3]

    def rows_of(blocks):
        return jnp.concatenate(blocks, axis=0)

    def column(i):
        return [pieces[k][i] for k in range(parts)]

    def all_pieces():
        for k in range(2, parts):
            back_part(k)
        back_part(0)
        return ()

    back_part(1)
    grad_mid_in, (_, part_gate, (part_up, part_down)) = scatter_ring(
        lambda k: pieces[k][3],
        (
            all_pieces,
            lambda: contract_rows(rows_of(mids), rows_of(column(1))).astype(BF16),
            lambda: (
                contract_rows(rows_of(mids), rows_of(column(2))).astype(BF16),
                contract_rows(rows_of(column(0)), rows_of(ogs)).astype(BF16),
            ),
        ),
    )
    summed_gate, summed_down = scattered(part_gate, 0), scattered(part_down, 1)
    grad_resid = out_grad.astype(F32) + rms_back(normal_mid, scale_mid, mid_full, grad_mid_in)
    part_mid = jnp.sum(grad_mid_in * normal_mid, axis=0)
    grad_resid_b = grad_resid.astype(BF16)

    late = barrier((column(4), grad_resid_b))[0]
    down_move = around(late[1].astype(BF16))
    grad_mixed = contract_cols(grad_resid_b, output_w).astype(BF16)
    grad_mixed = grad_mixed.reshape(rows, parts, heads * head_size).transpose(1, 0, 2)
    grad_attn = lax.all_to_all(grad_mixed, "tensor", 0, 0, tiled=True).reshape(all_rows, heads * head_size)
    up_state = halves_step(halves_split(halves_start(part_up)))
    part_output = contract_rows(grad_resid_b, mixed).astype(BF16)
    grad_attn, down_move, part_output, up_blocks = barrier(
        (grad_attn, down_move, part_output, [u[0] for u in up_state])
    )
    up_state = [(block, *u[1:]) for block, u in zip(up_blocks, up_state)]
    down_move = around((late[2] + down_move.astype(F32)).astype(BF16))
    out_block, out_left = halves_start(part_output)

    grad_qkv, gain_parts = backward_heads(
        qkv, grad_attn, lse, cosine, sine, gain_query, gain_key, heads, kv_heads
    )
    grad_qkv, down_move, out_block, summed_up, summed_gate = barrier(
        (grad_qkv, down_move, out_block, halves_end(up_state), summed_gate)
    )
    for k in range(3, parts):
        down_move = around((late[k] + down_move.astype(F32)).astype(BF16))
    layer_out = (resid + late[0] + down_move.astype(F32)).astype(BF16)

    grads_in, part_pre = [], 0.0
    for k in range(parts):
        block = lax.dynamic_slice(grad_qkv, (place(k) * rows, 0), (rows, grad_qkv.shape[1]))
        grads_in.append(contract_cols(block, w_qkv))
        wide, scale = normals[k]
        part_pre = part_pre + jnp.sum(grads_in[k] * (wide * scale), axis=0)

    def gain_filler():
        packed = jnp.concatenate([part_pre, part_mid, gain_parts[0], gain_parts[1]])
        return butterfly(packed.reshape(-1, 128)).reshape(-1), summed_down

    grad_pre_in, ((part_qkv, out_rows), (gain_sums, summed_down), _) = scatter_ring(
        lambda k: grads_in[k],
        (
            lambda: (
                contract_rows(normed_full, grad_qkv).astype(BF16),
                halves_end(halves_split((out_block, out_left))),
            ),
            gain_filler,
        ),
    )
    summed_qkv = scattered(part_qkv, 0).astype(F32)
    out_cols = out_rows.shape[1] // parts
    summed_output, _ = scatter_ring(
        lambda k: lax.dynamic_slice(
            out_rows, (0, place(k) * out_cols), (out_rows.shape[0], out_cols)
        ).astype(F32)
    )
    summed_output = summed_output.T
    scale_pre = normals[0][1]
    back_pre = rms_back(inputs_wide * scale_pre, scale_pre, pre_full, grad_pre_in)
    in_grad = (grad_resid + back_pre).astype(BF16)

    summed_down = summed_down.astype(F32)
    summed_gate_up = jnp.stack([summed_gate.astype(F32), summed_up.astype(F32)], axis=1)
    cuts = [w_query.shape[1], w_query.shape[1] + w_key.shape[1]]
    summed_query, summed_key, summed_value = jnp.split(summed_qkv, cuts, axis=1)

    outs, at = [], 0
    for full, size in zip((width, width, head_size, head_size), sizes):
        outs.append(lax.dynamic_slice(gain_sums, (at + mine * size,), (size,)))
        at += full
    return (
        layer_out,
        in_grad,
        summed_query,
        summed_key,
        summed_value,
        summed_output,
        summed_gate_up,
        summed_down,
        *outs,
    )


def solution(mesh):
    placed = (
        P(("dp", "tensor"), None),
        P("dp", "tensor"),
        P("dp", "tensor"),
        P("dp", "tensor"),
        P("tensor", "dp"),
        P("dp", None, "tensor"),
        P("tensor", "dp"),
        P("dp"),
        P("dp"),
        P("dp"),
        P("dp"),
        P(("dp", "tensor"), None),
    )
    return jax.shard_map(
        functools.partial(on_device, (mesh.shape["dp"], mesh.shape["tensor"])),
        mesh=mesh,
        in_specs=placed,
        out_specs=(
            P(("dp", "tensor"), None),
            P(("dp", "tensor"), None),
            P("dp", "tensor"),
            P("dp", "tensor"),
            P("dp", "tensor"),
            P("tensor", "dp"),
            P("dp", None, "tensor"),
            P("tensor", "dp"),
            P("dp"),
            P("dp"),
            P("dp"),
            P("dp"),
        ),
        check_vma=False,
    )
```

time: 1290 us -> 739 us (0.57)
  waiting for transfers between devices: 838 us -> 338 us
  Pallas kernels: 0 us -> 103 us
  matrix products: 191 us -> 89.8 us
  blocking collectives: 59.2 us -> 9.28 us
  starting transfers between devices: 13.3 us -> 37.2 us
    reduce_scatter x10 -> x3, waiting for transfers between devices: 416 us -> 0.01 us  [scattered(): return lax.psum_scatter(part, 'dp', scatter_dimension=axis, tiled=True)]
    all_gather x10 -> x5, waiting for transfers between devices: 418 us -> 21.3 us  [the longest x1 17.3 us: on_device(): lax.all_gather(w_gate_up.transpose(1, 0, 2), 'dp', axis=1, tiled=True)]
    ppermute x0 -> x36, waiting for transfers between devices: none -> 306 us  [the longest x21 253 us: around(): return lax.ppermute(block, 'tensor', ring)]
    pallas_call x0 -> x6, Pallas kernels: none -> 103 us  [the longest x4 73.2 us: hidden_piece(): pl.pallas_call(hidden_kernel, grid=(units // tile,), in_specs=[whole, who...]
    dot_general x14 -> x5, matrix products: 66 us -> 18 us  [dot(): return jnp.dot(left, right, preferred_element_type=F32)]
    dot_general x18 -> x5, matrix products: 61.6 us -> 20.6 us  [contract_cols(): lax.dot_general(left, right, (((1,), (1,)), ((), ())), preferred_element_...]
    ppermute x0 -> x36, starting transfers between devices: none -> 29 us  [the longest x21 16.1 us: around(): return lax.ppermute(block, 'tensor', ring)]
    unnamed x2 -> x0, blocking collectives: 27.5 us -> none
  transfers between devices with their start and end apart: 20 -> 46, of which waited for: 15 -> 27; matrix products, arithmetic and copies ran while one was open for 22% -> 29% of each run, Pallas kernels for 0% -> 14%
where the time goes in v1:
time: 739 us; the launch traced here: 732 us
  waiting for transfers between devices  338 us (46%)
  Pallas kernels  103 us (14%)
  matrix products  89.8 us (12%)
  other arithmetic  70.3 us (10%)
  local copies, waits for them, and re-layouts  68.2 us (9%)
  starting transfers between devices  37.2 us (5%)
  between operations  15.3 us (2%)
  blocking collectives  9.28 us (1%)
    ppermute x21, waiting for transfers between devices, around(): return lax.ppermute(block, 'tensor', ring)  253 us
    pallas_call x4, Pallas kernels, hidden_piece(): pl.pallas_call(hidden_kernel, grid=(units // tile,), in_specs=[whole, who...  73.2 us
    dot_general x5, matrix products, contract_rows(): lax.dot_general(left, right, (((0,), (0,)), ((), ())), preferred_element_...  51.2 us
    ppermute x5, waiting for transfers between devices, butterfly(): lax.ppermute(values, axis, [(i, i ^ 1 << bit) for i in range(size)])  28.2 us
    ppermute x10, waiting for transfers between devices, halve(): took = lax.ppermute(give, 'dp', [(i, i ^ 1 << bit) for i in range(dp)])  25.6 us
    unnamed x125, local copies, waits for them, and re-layouts  22.4 us
    dot_general x5, matrix products, contract_cols(): lax.dot_general(left, right, (((1,), (1,)), ((), ())), preferred_element_...  20.6 us
    convert_element_type x10, other arithmetic, halve(): (keep.astype(F32) + took.astype(F32)).astype(BF16)  20.3 us
  transfers between devices with their start and end apart: 46, of which 27 were waited for; matrix products, arithmetic and copies ran while one was open for 29% of the time, Pallas kernels for 14%

profile of v1, /device:TPU:0, one launch (start us, length us, event | category | flops | bytes accessed | tf_op | source)
XLA Modules:
  0.0 731.6 jit_solution(7553437177124728425)
XLA Ops:
  13.9 39.6 %collective-permute-done = bf16[256,2048]{1,0:T(8,128)(2,1)S(1)} collective-permute-done((bf16[256,2048]{1,0:T(8,128)(2,1)}, bf16[256,2048]{1,0:T(8,128)(2,1)S(1)}, u32[]{:S(2)}, u32[]{:S(2)}) %collective-permute-start) | collective-permute-done | bytes 1048608 | tf_op jit(solution)/shard_map/ppermute | solution.py:301
  63.1 9.3 %all-gather = bf16[8,1,640]{2,1,0:T(2,128)(2,1)S(1)} all-gather(bf16[1,1,640]{2,1,0:T(2,128)(2,1)S(1)} %bitcast.136), channel_id=1, replica_groups=mesh['dp'=8,'tensor'=4] {'dp'}, dimensions={0}, use_global_device_ids=true | all-gather | bytes 11520 | tf_op jit(solution)/shard_map/all_gather | solution.py:368
  77.7 12.0 %collective-permute-done.1 = bf16[256,2048]{1,0:T(8,128)(2,1)S(1)} collective-permute-done((bf16[256,2048]{1,0:T(8,128)(2,1)S(1)}, bf16[256,2048]{1,0:T(8,128)(2,1)S(1)}, u32[]{:S(2)}, u32[]{:S(2)}) %collective-permute-start.1) | collective-permute-done | bytes 1048608 | tf_op jit(solution)/shard_map/ppermute | solution.py:301
  103.8 11.9 %collective-permute-done.2 = bf16[256,2048]{1,0:T(8,128)(2,1)S(1)} collective-permute-done((bf16[256,2048]{1,0:T(8,128)(2,1)S(1)}, bf16[256,2048]{1,0:T(8,128)(2,1)S(1)}, u32[]{:S(2)}, u32[]{:S(2)}) %collective-permute-start.2) | collective-permute-done | bytes 1048608 | tf_op jit(solution)/shard_map/ppermute | solution.py:301
  122.2 11.7 %attention_forward.1 = (bf16[1024,512]{1,0:T(8,128)(2,1)}, f32[2,2,1024]{2,1,0:T(2,128)}) custom-call(f32[1024,1024]{1,0:T(8,128)} %convolution_dynamic-update-slice_fusion.q_ref.k_ref.v_ref, f32[1024,1024]{1,0:T(8,128)} %convolution_dynamic-update-slice_fusion.q_ref.k_ref.v_ref, f32[1024,1024]{1,0:T(8,128)} %convolution_dynamic-update-slice_fusion.q_ref.k_ref.v_ref, ...), custom_call_target="tpu_custom_call" | custom-call | flops 2147483648 | bytes 5242880 | tf_op jit(solution)/shard_map/attention_forward/pallas_call | solution.py:216
  133.9 7.6 %collective-permute-done.3.og_ref = bf16[256,2048]{1,0:T(8,128)(2,1)S(1)} collective-permute-done((bf16[256,2048]{1,0:T(8,128)(2,1)}, bf16[256,2048]{1,0:T(8,128)(2,1)S(1)}, u32[]{:S(2)}, u32[]{:S(2)}) %collective-permute-start.3) | collective-permute-done | bytes 1048608 | tf_op jit(solution)/shard_map/ppermute | solution.py:301
  149.6 39.5 %collective-permute-done.4.og_ref = bf16[256,2048]{1,0:T(8,128)(2,1)} collective-permute-done((bf16[256,2048]{1,0:T(8,128)(2,1)S(1)}, bf16[256,2048]{1,0:T(8,128)(2,1)}, u32[]{:S(2)}, u32[]{:S(2)}) %collective-permute-start.4) | collective-permute-done | bytes 1048608 | tf_op jit(solution)/shard_map/ppermute | solution.py:301
  194.7 6.6 multiply_reduce_fusion.2
  202.5 25.9 %collective-permute-done.5.mid_ref = bf16[256,2048]{1,0:T(8,128)(2,1)S(1)} collective-permute-done((bf16[256,2048]{1,0:T(8,128)(2,1)S(1)}, bf16[256,2048]{1,0:T(8,128)(2,1)S(1)}, u32[]{:S(2)}, u32[]{:S(2)}) %collective-permute-start.5) | collective-permute-done | bytes 1048608 | tf_op jit(solution)/shard_map/ppermute | solution.py:301
  228.4 27.9 %collective-permute-done.6.mid_ref = bf16[256,2048]{1,0:T(8,128)(2,1)} collective-permute-done((bf16[256,2048]{1,0:T(8,128)(2,1)S(1)}, bf16[256,2048]{1,0:T(8,128)(2,1)}, u32[]{:S(2)}, u32[]{:S(2)}) %collective-permute-start.6) | collective-permute-done | bytes 1048608 | tf_op jit(solution)/shard_map/ppermute | solution.py:301
  256.3 17.3 %all-gather.13.cloned.1.call-done.gate_ref.up_ref = bf16[2,2048,1536]{2,1,0:T(8,128)(2,1)} async-done(((bf16[2,256,1536]{2,1,0:T(8,128)(2,1)}), bf16[2,2048,1536]{2,1,0:T(8,128)(2,1)}) %all-gather.13.cloned.1.call-update) | async-done | bytes 12582928 | tf_op jit(solution)/shard_map/all_gather | solution.py:362
  273.6 18.3 %hidden_piece.5 = (bf16[256,1536]{1,0:T(8,128)(2,1)}, bf16[256,1536]{1,0:T(8,128)(2,1)}, bf16[256,1536]{1,0:T(8,128)(2,1)}, f32[256,2048]{1,0:T(8,128)}, f32[256,2048]{1,0:T(8,128)}) custom-call(bf16[256,2048]{1,0:T(8,128)(2,1)} %copy-done.51, bf16[256,2048]{1,0:T(8,128)(2,1)} %copy-done.49, ...), custom_call_target="tpu_custom_call" | custom-call | flops 9663676416 | bytes 27525120 | tf_op jit(solution)/shard_map/hidden_piece/pallas_call | solution.py:182
  295.3 18.3 %hidden_piece.6 = (bf16[256,1536]{1,0:T(8,128)(2,1)}, bf16[256,1536]{1,0:T(8,128)(2,1)}, bf16[256,1536]{1,0:T(8,128)(2,1)}, f32[256,2048]{1,0:T(8,128)}, f32[256,2048]{1,0:T(8,128)}) custom-call(bf16[256,2048]{1,0:T(8,128)(2,1)} %collective-permute-done.6.mid_ref, bf16[256,2048]{1,0:T(8,128)(2,1)} %collective-permute-done.4.og_ref, ...), custom_call_target="tpu_custom_call" | custom-call | flops 9663676416 | bytes 27525120 | tf_op jit(solution)/shard_map/hidden_piece/pallas_call | solution.py:182
  313.6 18.3 %hidden_piece.4 = (bf16[256,1536]{1,0:T(8,128)(2,1)}, bf16[256,1536]{1,0:T(8,128)(2,1)}, bf16[256,1536]{1,0:T(8,128)(2,1)}, f32[256,2048]{1,0:T(8,128)}, f32[256,2048]{1,0:T(8,128)}) custom-call(bf16[256,2048]{1,0:T(8,128)(2,1)} %copy-done.33, bf16[256,2048]{1,0:T(8,128)(2,1)} %og_ref.1, ...), custom_call_target="tpu_custom_call" | custom-call | flops 9663676416 | bytes 27525120 | tf_op jit(solution)/shard_map/hidden_piece/pallas_call | solution.py:182
  331.9 18.3 %hidden_piece.7 = (bf16[256,1536]{1,0:T(8,128)(2,1)}, bf16[256,1536]{1,0:T(8,128)(2,1)}, bf16[256,1536]{1,0:T(8,128)(2,1)}, f32[256,2048]{1,0:T(8,128)}, f32[256,2048]{1,0:T(8,128)}) custom-call(bf16[256,2048]{1,0:T(8,128)(2,1)} %collective-permute-done.7.mid_ref, bf16[256,2048]{1,0:T(8,128)(2,1)} %collective-permute-done.8.og_ref, ...), custom_call_target="tpu_custom_call" | custom-call | flops 9663676416 | bytes 27525120 | tf_op jit(solution)/shard_map/hidden_piece/pallas_call | solution.py:182
  355.3 11.4 %convolution_convert_fusion.3 = bf16[2048,1536]{1,0:T(8,128)(2,1)} fusion(bf16[256,1536]{1,0:T(8,128)(2,1)} %get-tuple-element.107, bf16[256,1536]{1,0:T(8,128)(2,1)S(1)} %copy-done.58, bf16[256,1536]{1,0:T(8,128)(2,1)S(1)} %copy-done.57, bf16[256,1536]{1,0:T(8,128)(2,1)} %get-tuple-element.104, bf16[256,2048]{1,0:T(8,128)(2,1)} %collective-permute-done.7.mid_ref, ...), kind=kOutput, calls=%fused_computation.5 | convolution fusion | flops 6474956800 | bytes 13631488 | tf_op jit(solution)/shard_map/dot_general | solution.py:28
  366.7 14.2 %collective-permute-done.10 = bf16[256,2048]{1,0:T(8,128)(2,1)} collective-permute-done((bf16[256,2048]{1,0:T(8,128)(2,1)}, bf16[256,2048]{1,0:T(8,128)(2,1)}, u32[]{:S(2)}, u32[]{:S(2)}) %collective-permute-start.10) | collective-permute-done | bytes 1048608 | tf_op jit(solution)/shard_map/ppermute | solution.py:301
  381.0 12.9 %convolution_convert_fusion.2 = bf16[2048,1536]{1,0:T(8,128)(2,1)} fusion(bf16[256,1536]{1,0:T(8,128)(2,1)} %get-tuple-element.114, bf16[256,1536]{1,0:T(8,128)(2,1)} %get-tuple-element.113, bf16[256,1536]{1,0:T(8,128)(2,1)} %get-tuple-element.112, bf16[256,1536]{1,0:T(8,128)(2,1)} %get-tuple-element.111, ...), kind=kOutput, calls=%fused_computation.4 | convolution fusion | flops 6474956800 | bytes 13631488 | tf_op jit(solution)/shard_map/dot_general | solution.py:28
  396.6 11.4 %convolution_convert_fusion.1 = bf16[1536,2048]{1,0:T(8,128)(2,1)} fusion(bf16[256,2048]{1,0:T(8,128)(2,1)} %collective-permute-done.8.og_ref, bf16[256,2048]{1,0:T(8,128)(2,1)} %collective-permute-done.4.og_ref, bf16[256,2048]{1,0:T(8,128)(2,1)S(1)} %copy-done.50, bf16[256,2048]{1,0:T(8,128)(2,1)} %og_ref.1, bf16[256,1536]{1,0:T(8,128)(2,1)S(1)} %copy-done.56, ...), kind=kOutput, calls=%fused_computation.3 | convolution fusion | flops 6474956800 | bytes 13631488 | tf_op jit(solution)/shard_map/dot_general | solution.py:28
  408.0 14.9 %collective-permute-done.11 = bf16[256,2048]{1,0:T(8,128)(2,1)S(1)} collective-permute-done((bf16[256,2048]{1,0:T(8,128)(2,1)}, bf16[256,2048]{1,0:T(8,128)(2,1)S(1)}, u32[]{:S(2)}, u32[]{:S(2)}) %collective-permute-start.11) | collective-permute-done | bytes 1048608 | tf_op jit(solution)/shard_map/ppermute | solution.py:301
  460.6 7.1 convolution_convert_fusion
  476.9 11.9 %collective-permute-done.12 = bf16[256,2048]{1,0:T(8,128)(2,1)} collective-permute-done((bf16[256,2048]{1,0:T(8,128)(2,1)}, bf16[256,2048]{1,0:T(8,128)(2,1)}, u32[]{:S(2)}, u32[]{:S(2)}) %collective-permute-start.12) | collective-permute-done | bytes 1048608 | tf_op jit(solution)/shard_map/ppermute | solution.py:301
  493.4 8.5 %constant_dynamic-slice_fusion.2 = (bf16[2,2,1,256,2048]{4,3,2,1,0:T(8,128)(2,1)}, bf16[2,2,1,256,2048]{4,3,2,1,0:T(8,128)(2,1)}) fusion(bf16[2,2,2,256,2048]{4,3,2,1,0:T(8,128)(2,1)} %bitcast.110, s32[]{:T(128)S(6)} %select_n.127, s32[]{:T(128)S(6)} %select_n.128), kind=kLoop, calls=%fused_computation.156 | loop fusion | bytes 16777224 | tf_op jit(solution)/shard_map/jit(dynamic_index_in_dim)/dynamic_slice | solution.py:328
  514.2 6.6 copy.45
  524.3 18.4 %attention_backward.1 = (bf16[1024,1024]{1,0:T(8,128)(2,1)}, f32[2,128]{1,0:T(2,128)}) custom-call(f32[1024,1024]{1,0:T(8,128)} %convolution_dynamic-update-slice_fusion.q_ref.k_ref.v_ref, f32[1024,1024]{1,0:T(8,128)} %convolution_dynamic-update-slice_fusion.q_ref.k_ref.v_ref, f32[1024,1024]{1,0:T(8,128)} %convolution_dynamic-update-slice_fusion.q_ref.k_ref.v_ref, ...), custom_call_target="tpu_custom_call" | custom-call | flops 5368709120 | bytes 7340032 | tf_op jit(solution)/shard_map/attention_backward/pallas_call | solution.py:242
  547.2 6.6 fusion
  560.7 8.5 %convolution_convert_fusion.4 = bf16[2048,1024]{1,0:T(8,128)(2,1)} fusion(bf16[1024,2048]{1,0:T(8,128)(2,1)} %fusion.79, bf16[1024,1024]{1,0:T(8,128)(2,1)S(1)} %copy-done.31), kind=kOutput, calls=%fused_computation.16 | convolution fusion | flops 4297064448 | bytes 10485760 | tf_op jit(solution)/shard_map/dot_general | solution.py:28
  577.7 11.0 %collective-permute-done.22 = bf16[2,256,1024]{1,2,0:T(8,128)(2,1)} collective-permute-done((bf16[2,256,1024]{1,2,0:T(8,128)(2,1)}, bf16[2,256,1024]{1,2,0:T(8,128)(2,1)}, u32[]{:S(2)}, u32[]{:S(2)}) %collective-permute-start.22) | collective-permute-done | bytes 1048608 | tf_op jit(solution)/shard_map/ppermute | solution.py:329
  596.6 6.9 collective-permute-done.23
  635.1 27.5 %collective-permute-done.33 = bf16[256,512]{0,1:T(8,128)(2,1)S(1)} collective-permute-done((bf16[256,512]{0,1:T(8,128)(2,1)S(1)}, bf16[256,512]{0,1:T(8,128)(2,1)S(1)}, u32[]{:S(2)}, u32[]{:S(2)}) %collective-permute-start.33) | collective-permute-done | bytes 262176 | tf_op jit(solution)/shard_map/ppermute | solution.py:301
  667.1 20.3 %collective-permute-done.31 = f32[34,128]{1,0:T(8,128)S(1)} collective-permute-done((f32[34,128]{1,0:T(8,128)S(1)}, f32[34,128]{1,0:T(8,128)S(1)}, u32[]{:S(2)}, u32[]{:S(2)}) %collective-permute-start.31) | collective-permute-done | bytes 17440 | tf_op jit(solution)/shard_map/ppermute | solution.py:353
  702.7 14.7 %collective-permute-done.32 = bf16[256,2048]{1,0:T(8,128)(2,1)S(1)} collective-permute-done((bf16[256,2048]{1,0:T(8,128)(2,1)S(1)}, bf16[256,2048]{1,0:T(8,128)(2,1)S(1)}, u32[]{:S(2)}, u32[]{:S(2)}) %collective-permute-start.32) | collective-permute-done | bytes 1048608 | tf_op jit(solution)/shard_map/ppermute | solution.py:301
  (301 shorter events, 221.1 us)
Async XLA Ops:
  7.2 48.5 %all-gather.7.cloned.1.call-start = ((), (), s32[]{:S(2)}) async-start(), calls=%async_computation.5 | async-start | bytes 1310720 | tf_op jit(solution)/shard_map/all_gather | solution.py:360
  7.9 85.2 %all-gather.9.cloned.1.call-start = ((), (), s32[]{:S(2)}) async-start(), calls=%async_computation.6 | async-start | bytes 4718592 | tf_op jit(solution)/shard_map/all_gather | solution.py:361
  9.9 184.7 %all-gather.11.cloned.1.call-start = ((), (), s32[]{:S(2)}) async-start(), calls=%async_computation.7 | async-start | bytes 9437184 | tf_op jit(solution)/shard_map/all_gather | solution.py:367
  10.0 43.5 %collective-permute-start = (bf16[256,2048]{1,0:T(8,128)(2,1)}, bf16[256,2048]{1,0:T(8,128)(2,1)S(1)}, u32[]{:S(2)}, u32[]{:S(2)}) collective-permute-start(bf16[256,2048]{1,0:T(8,128)(2,1)} %param.12), channel_id=1, source_target_pairs={{0,1},{1,2},{2,3},{3,0},{4,5},{5,6},{6,7},{7,4},{8,9},{9,10},{10,1... | collective-permute-start | bytes 3145736 | tf_op jit(solution)/shard_map/ppermute | solution.py:301
  55.7 200.5 %all-gather.15.cloned.1.call-start = ((), (), s32[]{:S(2)}) async-start(), calls=%async_computation.9 | async-start | bytes 7077888 | tf_op jit(solution)/shard_map/all_gather | solution.py:363
  56.3 217.2 %all-gather.13.cloned.1.call-start = ((), (), s32[]{:S(2)}) async-start(), calls=%async_computation.8 | async-start | bytes 14155776 | tf_op jit(solution)/shard_map/all_gather | solution.py:362
  62.8 26.9 %collective-permute-start.1 = (bf16[256,2048]{1,0:T(8,128)(2,1)S(1)}, bf16[256,2048]{1,0:T(8,128)(2,1)S(1)}, u32[]{:S(2)}, u32[]{:S(2)}) collective-permute-start(bf16[256,2048]{1,0:T(8,128)(2,1)S(1)} %collective-permute-done), channel_id=1, source_target_pairs={{0,1},{1,2},{2,3},{3,0},{4,5},{5,6},{6,7},{7,4},{8,9},{9,10},{10,1... | collective-permute-start | bytes 3145736 | tf_op jit(solution)/shard_map/ppermute | solution.py:301
  144.1 49.6 %all-to-all-start = ((bf16[4,256,512]{1,2,0:T(8,128)(2,1)}), bf16[4,256,512]{1,2,0:T(8,128)(2,1)S(1)}, u32[]{:S(2)}, u32[]{:S(2)}) async-start(bf16[4,256,512]{1,2,0:T(8,128)(2,1)} %copy.36), calls=%async_computation | async-start | bytes 2097152 | tf_op jit(solution)/shard_map/all_to_all | solution.py:396
  147.6 406.2 %reduce-scatter.4.cloned.1.call-start = ((), (), s32[]{:S(2)}) async-start(), calls=%async_computation.10 | async-start | bytes 7077888 | tf_op jit(solution)/shard_map/reduce_scatter | solution.py:322
  147.7 41.5 %collective-permute-start.4 = (bf16[256,2048]{1,0:T(8,128)(2,1)S(1)}, bf16[256,2048]{1,0:T(8,128)(2,1)}, u32[]{:S(2)}, u32[]{:S(2)}) collective-permute-start(bf16[256,2048]{1,0:T(8,128)(2,1)S(1)} %collective-permute-done.3.og_ref), channel_id=1, source_target_pairs={{0,1},{1,2},{2,3},{3,0},{4,5},{5,6},{6,7},{7,4},{8,9},{9,10},{10,1... | collective-permute-start | bytes 3145736 | tf_op jit(solution)/shard_map/ppermute | solution.py:301
  228.3 27.9 %collective-permute-start.6 = (bf16[256,2048]{1,0:T(8,128)(2,1)S(1)}, bf16[256,2048]{1,0:T(8,128)(2,1)}, u32[]{:S(2)}, u32[]{:S(2)}) collective-permute-start(bf16[256,2048]{1,0:T(8,128)(2,1)S(1)} %collective-permute-done.5.mid_ref), channel_id=1, source_target_pairs={{0,1},{1,2},{2,3},{3,0},{4,5},{5,6},{6,7},{7,4},{8,9},{9,10},{10,1... | collective-permute-start | bytes 3145736 | tf_op jit(solution)/shard_map/ppermute | solution.py:301
  228.3 103.6 %collective-permute-start.8 = (bf16[256,2048]{1,0:T(8,128)(2,1)}, bf16[256,2048]{1,0:T(8,128)(2,1)}, u32[]{:S(2)}, u32[]{:S(2)}) collective-permute-start(bf16[256,2048]{1,0:T(8,128)(2,1)} %collective-permute-done.4.og_ref), channel_id=1, source_target_pairs={{0,1},{1,2},{2,3},{3,0},{4,5},{5,6},{6,7},{7,4},{8,9},{9,10},{10,1... | collective-permute-start | bytes 3145736 | tf_op jit(solution)/shard_map/ppermute | solution.py:301
  256.3 75.6 %collective-permute-start.7 = (bf16[256,2048]{1,0:T(8,128)(2,1)}, bf16[256,2048]{1,0:T(8,128)(2,1)}, u32[]{:S(2)}, u32[]{:S(2)}) collective-permute-start(bf16[256,2048]{1,0:T(8,128)(2,1)} %collective-permute-done.6.mid_ref), channel_id=1, source_target_pairs={{0,1},{1,2},{2,3},{3,0},{4,5},{5,6},{6,7},{7,4},{8,9},{9,10},{10,1... | collective-permute-start | bytes 3145736 | tf_op jit(solution)/shard_map/ppermute | solution.py:301
  293.6 56.6 %collective-permute-start.9 = (bf16[256,2048]{1,0:T(8,128)(2,1)S(1)}, bf16[256,2048]{1,0:T(8,128)(2,1)}, u32[]{:S(2)}, u32[]{:S(2)}) collective-permute-start(bf16[256,2048]{1,0:T(8,128)(2,1)S(1)} %convert_element_type.295), channel_id=1, source_target_pairs={{0,1},{1,2},{2,3},{3,0},{4,5},{5,6},{6,7},{7,4},{8,9},{9,10},{10,1... | collective-permute-start | bytes 3145736 | tf_op jit(solution)/shard_map/ppermute | solution.py:301
  353.6 27.3 %collective-permute-start.10 = (bf16[256,2048]{1,0:T(8,128)(2,1)}, bf16[256,2048]{1,0:T(8,128)(2,1)}, u32[]{:S(2)}, u32[]{:S(2)}) collective-permute-start(bf16[256,2048]{1,0:T(8,128)(2,1)} %add_convert_fusion.6), channel_id=1, source_target_pairs={{0,1},{1,2},{2,3},{3,0},{4,5},{5,6},{6,7},{7,4},{8,9},{9,10},{10,1... | collective-permute-start | bytes 3145736 | tf_op jit(solution)/shard_map/ppermute | solution.py:301
  396.6 26.3 %collective-permute-start.11 = (bf16[256,2048]{1,0:T(8,128)(2,1)}, bf16[256,2048]{1,0:T(8,128)(2,1)S(1)}, u32[]{:S(2)}, u32[]{:S(2)}) collective-permute-start(bf16[256,2048]{1,0:T(8,128)(2,1)} %add_convert_fusion.5), channel_id=1, source_target_pairs={{0,1},{1,2},{2,3},{3,0},{4,5},{5,6},{6,7},{7,4},{8,9},{9,10},{10,1... | collective-permute-start | bytes 3145736 | tf_op jit(solution)/shard_map/ppermute | solution.py:301
  440.0 53.4 %all-to-all-start.1 = ((bf16[4,256,512]{2,1,0:T(8,128)(2,1)}), bf16[4,256,512]{2,1,0:T(8,128)(2,1)}, u32[]{:S(2)}, u32[]{:S(2)}) async-start(bf16[4,256,512]{2,1,0:T(8,128)(2,1)} %bitcast.108), calls=%async_computation.1 | async-start | bytes 2097152 | tf_op jit(solution)/shard_map/all_to_all | solution.py:448
  444.2 243.9 %reduce-scatter.6.cloned.1.call-start = ((), (), s32[]{:S(2)}) async-start(), calls=%async_computation.11 | async-start | bytes 7077888 | tf_op jit(solution)/shard_map/reduce_scatter | solution.py:322
  458.6 30.2 %collective-permute-start.12 = (bf16[256,2048]{1,0:T(8,128)(2,1)}, bf16[256,2048]{1,0:T(8,128)(2,1)}, u32[]{:S(2)}, u32[]{:S(2)}) collective-permute-start(bf16[256,2048]{1,0:T(8,128)(2,1)} %convert_element_type.306), channel_id=1, source_target_pairs={{0,1},{1,2},{2,3},{3,0},{4,5},{5,6},{6,7},{7,4},{8,9},{9,10},{10,1... | collective-permute-start | bytes 3145736 | tf_op jit(solution)/shard_map/ppermute | solution.py:301
  508.2 39.1 %collective-permute-start.17 = (bf16[2,2,256,2048]{2,3,1,0:T(8,128)(2,1)}, bf16[2,2,256,2048]{2,3,1,0:T(8,128)(2,1)}, u32[]{:S(2)}, u32[]{:S(2)}) collective-permute-start(bf16[2,2,256,2048]{2,3,1,0:T(8,128)(2,1)} %bitcast.116), channel_id=1, source_target_pairs={{0,4},{4,0},{8,12},{12,8},{16,20},{20,16},{24,28},{28,24},{1,5},{5... | collective-permute-start | bytes 12582920 | tf_op jit(solution)/shard_map/ppermute | solution.py:329
  508.2 212.5 %reduce-scatter.8.cloned.1.call-start = ((), (), s32[]{:S(2)}) async-start(), calls=%async_computation.12 | async-start | bytes 4718592 | tf_op jit(solution)/shard_map/reduce_scatter | solution.py:322
  511.4 32.5 %collective-permute-start.18 = (bf16[256,768]{1,0:T(8,128)(2,1)}, bf16[256,768]{1,0:T(8,128)(2,1)}, u32[]{:S(2)}, u32[]{:S(2)}) collective-permute-start(bf16[256,768]{1,0:T(8,128)(2,1)} %dynamic-slice_bitcast_fusion.8), channel_id=1, source_target_pairs={{0,16},{4,20},{8,24},{12,28},{16,0},{20,4},{24,8},{28,12},{1,17},{... | collective-permute-start | bytes 1179656 | tf_op jit(solution)/shard_map/ppermute | solution.py:329
  513.1 32.0 %collective-permute-start.19 = (bf16[256,768]{1,0:T(8,128)(2,1)}, bf16[256,768]{1,0:T(8,128)(2,1)S(1)}, u32[]{:S(2)}, u32[]{:S(2)}) collective-permute-start(bf16[256,768]{1,0:T(8,128)(2,1)} %dynamic-slice_bitcast_fusion.7), channel_id=1, source_target_pairs={{0,8},{4,12},{8,0},{12,4},{16,24},{20,28},{24,16},{28,20},{1,9},{5... | collective-permute-start | bytes 1179656 | tf_op jit(solution)/shard_map/ppermute | solution.py:329
  524.1 29.7 %collective-permute-start.16 = (bf16[256,2048]{1,0:T(8,128)(2,1)}, bf16[256,2048]{1,0:T(8,128)(2,1)}, u32[]{:S(2)}, u32[]{:S(2)}) collective-permute-start(bf16[256,2048]{1,0:T(8,128)(2,1)} %add_convert_fusion.4), channel_id=1, source_target_pairs={{0,1},{1,2},{2,3},{3,0},{4,5},{5,6},{6,7},{7,4},{8,9},{9,10},{10,1... | collective-permute-start | bytes 3145736 | tf_op jit(solution)/shard_map/ppermute | solution.py:301
  557.7 30.9 %collective-permute-start.22 = (bf16[2,256,1024]{1,2,0:T(8,128)(2,1)}, bf16[2,256,1024]{1,2,0:T(8,128)(2,1)}, u32[]{:S(2)}, u32[]{:S(2)}) collective-permute-start(bf16[2,256,1024]{1,2,0:T(8,128)(2,1)} %dynamic-slice_bitcast_fusion.2), channel_id=1, source_target_pairs={{0,8},{4,12},{8,0},{12,4},{16,24},{20,28},{24,16},{28,20},{1,9},{5... | collective-permute-start | bytes 3145736 | tf_op jit(solution)/shard_map/ppermute | solution.py:329
  559.5 32.3 %collective-permute-start.24 = (bf16[2,256,1024]{1,2,0:T(8,128)(2,1)}, bf16[2,256,1024]{1,2,0:T(8,128)(2,1)}, u32[]{:S(2)}, u32[]{:S(2)}) collective-permute-start(bf16[2,256,1024]{1,2,0:T(8,128)(2,1)} %dynamic-slice_bitcast_fusion.1), channel_id=1, source_target_pairs={{0,16},{4,20},{8,24},{12,28},{16,0},{20,4},{24,8},{28,12},{1,17},{... | collective-permute-start | bytes 3145736 | tf_op jit(solution)/shard_map/ppermute | solution.py:329
  573.4 34.3 %collective-permute-start.21 = (bf16[256,2048]{1,0:T(8,128)(2,1)S(1)}, bf16[256,2048]{1,0:T(8,128)(2,1)S(1)}, u32[]{:S(2)}, u32[]{:S(2)}) collective-permute-start(bf16[256,2048]{1,0:T(8,128)(2,1)S(1)} %get-tuple-element.205), channel_id=1, source_target_pairs={{0,1},{1,2},{2,3},{3,0},{4,5},{5,6},{6,7},{7,4},{8,9},{9,10},{10,1... | collective-permute-start | bytes 3145736 | tf_op jit(solution)/shard_map/ppermute | solution.py:301
  628.4 63.4 %collective-permute-start.20 = (bf16[256,2048]{1,0:T(8,128)(2,1)}, bf16[256,2048]{1,0:T(8,128)(2,1)}, u32[]{:S(2)}, u32[]{:S(2)}) collective-permute-start(bf16[256,2048]{1,0:T(8,128)(2,1)} %add_convert_fusion.3), channel_id=1, source_target_pairs={{0,1},{1,2},{2,3},{3,0},{4,5},{5,6},{6,7},{7,4},{8,9},{9,10},{10,1... | collective-permute-start | bytes 3145736 | tf_op jit(solution)/shard_map/ppermute | solution.py:301
  629.1 58.3 %collective-permute-start.31 = (f32[34,128]{1,0:T(8,128)S(1)}, f32[34,128]{1,0:T(8,128)S(1)}, u32[]{:S(2)}, u32[]{:S(2)}) collective-permute-start(f32[34,128]{1,0:T(8,128)S(1)} %add.336), channel_id=1, source_target_pairs={{0,2},{1,3},{2,0},{3,1},{4,6},{5,7},{6,4},{7,5},{8,10},{9,11},{10,... | collective-permute-start | bytes 52232 | tf_op jit(solution)/shard_map/ppermute | solution.py:353
  632.5 30.1 %collective-permute-start.33 = (bf16[256,512]{0,1:T(8,128)(2,1)S(1)}, bf16[256,512]{0,1:T(8,128)(2,1)S(1)}, u32[]{:S(2)}, u32[]{:S(2)}) collective-permute-start(bf16[256,512]{0,1:T(8,128)(2,1)S(1)} %get-tuple-element.209), channel_id=1, source_target_pairs={{0,1},{1,2},{2,3},{3,0},{4,5},{5,6},{6,7},{7,4},{8,9},{9,10},{10,1... | collective-permute-start | bytes 786440 | tf_op jit(solution)/shard_map/ppermute | solution.py:301
  635.1 53.1 %collective-permute-start.26 = (bf16[256,2048]{1,0:T(8,128)(2,1)}, bf16[256,2048]{1,0:T(8,128)(2,1)}, u32[]{:S(2)}, u32[]{:S(2)}) collective-permute-start(bf16[256,2048]{1,0:T(8,128)(2,1)} %add_convert_fusion.1), channel_id=1, source_target_pairs={{0,1},{1,2},{2,3},{3,0},{4,5},{5,6},{6,7},{7,4},{8,9},{9,10},{10,1... | collective-permute-start | bytes 3145736 | tf_op jit(solution)/shard_map/ppermute | solution.py:301
  690.6 26.9 %collective-permute-start.32 = (bf16[256,2048]{1,0:T(8,128)(2,1)S(1)}, bf16[256,2048]{1,0:T(8,128)(2,1)S(1)}, u32[]{:S(2)}, u32[]{:S(2)}) collective-permute-start(bf16[256,2048]{1,0:T(8,128)(2,1)S(1)} %add_convert_fusion), channel_id=1, source_target_pairs={{0,1},{1,2},{2,3},{3,0},{4,5},{5,6},{6,7},{7,4},{8,9},{9,10},{10,1... | collective-permute-start | bytes 3145736 | tf_op jit(solution)/shard_map/ppermute | solution.py:301
  (73 other events, 1093.5 us)
Sparse Core Ops, SparseCore 0:
  9.6 46.1 all-gather.6
  58.2 34.8 all-gather.8
  95.0 55.8 all-gather.10
  152.6 46.5 all-gather.14
  201.5 71.9 all-gather.12
  381.1 59.0 reduce-scatter.3
  508.3 65.5 reduce-scatter.5
  608.8 50.1 reduce-scatter.7

commit v2 on v1

--- a/solution.py
+++ b/solution.py
@@ -144,10 +144,12 @@
     out_ref[:, pl.ds(pl.multiple_of((heads + kv_heads + at) * size, size), size)] = dv_ref[...].astype(BF16)
 
 
-def hidden_kernel(
-    mid_ref, og_ref, gate_ref, up_ref, down_ref, hidden_ref, grad_gate_ref, grad_up_ref, back_ref, out_ref
-):
-    mid, gate_w, up_w, down_w = mid_ref[...], gate_ref[0], up_ref[0], down_ref[...]
+def hidden_kernel(blocks, *refs):
+    gate_refs, up_refs = refs[:blocks], refs[blocks : 2 * blocks]
+    mid_ref, og_ref, down_ref, hidden_ref, grad_gate_ref, grad_up_ref, back_ref, out_ref = refs[2 * blocks :]
+    gate_w = jnp.concatenate([ref[...] for ref in gate_refs], axis=0)
+    up_w = jnp.concatenate([ref[...] for ref in up_refs], axis=0)
+    mid, down_w = mid_ref[...], down_ref[...]
     gate = dot(mid, gate_w)
     upper = dot(mid, up_w)
     grad_hidden = contract_cols(og_ref[...], down_w)
@@ -173,22 +175,18 @@
         out_ref[...] += out
 
 
-def hidden_piece(mid, og, gate_up_w, down_w):
+def hidden_piece(mid, og, gate_blocks, up_blocks, down_w):
     rows, width = mid.shape
     units = down_w.shape[0]
+    blocks = len(gate_blocks)
     tile = min(512, units)
     whole = pl.BlockSpec((rows, width), lambda j: (0, 0))
     out = pl.BlockSpec((rows, tile), lambda j: (0, j))
+    block = pl.BlockSpec((width // blocks, tile), lambda j: (0, j))
     return pl.pallas_call(
-        hidden_kernel,
+        functools.partial(hidden_kernel, blocks),
         grid=(units // tile,),
-        in_specs=[
-            whole,
-            whole,
-            pl.BlockSpec((1, width, tile), lambda j: (0, 0, j)),
-            pl.BlockSpec((1, width, tile), lambda j: (1, 0, j)),
-            pl.BlockSpec((tile, width), lambda j: (j, 0)),
-        ],
+        in_specs=[block] * (2 * blocks) + [whole, whole, pl.BlockSpec((tile, width), lambda j: (j, 0))],
         out_specs=(out, out, out, whole, whole),
         out_shape=tuple(jax.ShapeDtypeStruct((rows, units), BF16) for _ in range(3))
         + tuple(jax.ShapeDtypeStruct((rows, width), F32) for _ in range(2)),
@@ -198,7 +196,32 @@
             bytes_accessed=6 * width * units + 12 * rows * width + 6 * rows * units,
         ),
         name="hidden_piece",
-    )(mid, og, gate_up_w, gate_up_w, down_w)
+    )(*gate_blocks, *up_blocks, mid, og, down_w)
+
+
+def shuffle_kernel(size, order_ref, in_ref, out_ref):
+    for i in range(in_ref.shape[1] // size):
+        at = pl.multiple_of(order_ref[i] * size, size)
+        out_ref[:, i * size : (i + 1) * size] = in_ref[:, pl.ds(at, size)]
+
+
+def shuffled(values, order):
+    size = values.shape[1] // order.shape[0]
+    if size % 128:
+        cut = values.reshape(values.shape[0], order.shape[0], size)
+        return cut[:, order].reshape(values.shape)
+    whole = pl.BlockSpec(values.shape, lambda i, order: (0, 0))
+    return pl.pallas_call(
+        functools.partial(shuffle_kernel, size),
+        grid_spec=pltpu.PrefetchScalarGridSpec(
+            num_scalar_prefetch=1, grid=(1,), in_specs=[whole], out_specs=whole
+        ),
+        out_shape=jax.ShapeDtypeStruct(values.shape, values.dtype),
+        cost_estimate=pl.CostEstimate(
+            flops=0, transcendentals=0, bytes_accessed=2 * values.size * values.dtype.itemsize
+        ),
+        name="shuffled",
+    )(order, values)
 
 
 def qkv_specs(group, size, heads, kv_heads):
@@ -312,8 +335,9 @@
         total = part(order[0])
         for j, k in enumerate(order[1:]):
             moving = around(total.astype(BF16))
+            ahead = part(k)
             new = fillers[j]() if j < len(fillers) else ()
-            moving, ahead, new = barrier((moving, part(k), new))
+            moving, ahead, new = barrier((moving, ahead, new))
             total = ahead + moving.astype(F32)
             made.append(new)
         return total, made
@@ -323,29 +347,32 @@
 
     bits = dp.bit_length() - 1
 
-    def halve(block, left, bit):
-        axis, own = left.index(bit), (mine >> bit) & 1
-        keep, give = (lax.dynamic_index_in_dim(block, at, axis, keepdims=False) for at in (own, 1 - own))
-        took = lax.ppermute(give, "dp", [(i, i ^ (1 << bit)) for i in range(dp)])
-        return (keep.astype(F32) + took.astype(F32)).astype(BF16), [b for b in left if b != bit]
-
-    def halves_start(part):
-        block = part.reshape((2,) * bits + (part.shape[0] // dp, part.shape[1]))
-        return halve(block, list(range(bits))[::-1], 0)
-
-    def halves_split(state):
-        block, left = state
-        cut = block.shape[-1] // 2
-        rest = sorted(left)
-        return [(block[..., :cut], left, rest), (block[..., cut:], left, rest[::-1])]
-
-    def halves_step(states):
-        return [(*halve(block, left, order[0]), order[1:]) for block, left, order in states]
-
-    def halves_end(states):
-        while states[0][2]:
-            states = halves_step(states)
-        return jnp.concatenate([block for block, _, _ in states], axis=-1)
+    def swap(block, bit):
+        return lax.ppermute(block, "dp", [(i, i ^ (1 << bit)) for i in range(dp)])
+
+    near_last = list(range(1, bits)) + [0]
+    relative = [0]
+    for bit in near_last:
+        relative = relative + [r | (1 << bit) for r in relative]
+
+    def doubling_step(held, bit):
+        return {**held, **{r | (1 << bit): swap(block, bit) for r, block in held.items()}}
+
+    def halving_step(keep, give, bit):
+        return (keep.astype(F32) + swap(give, bit).astype(F32)).astype(BF16)
+
+    def halve(held, bit):
+        keep = [r for r in held if not (r >> bit) & 1]
+        far = swap(jnp.concatenate([held[r | (1 << bit)] for r in keep], axis=0), bit)
+        size = far.shape[0] // len(keep)
+        return {
+            r: (held[r].astype(F32) + far[i * size : (i + 1) * size].astype(F32)).astype(BF16)
+            for i, r in enumerate(keep)
+        }
+
+    def by_name(block, names):
+        size = block.shape[0] // len(names)
+        return {r: block[i * size : (i + 1) * size] for i, r in enumerate(names)}
 
     def butterfly(values):
         for axis, size in (("dp", dp), ("tensor", parts)):
@@ -357,14 +384,21 @@
     used = sum(sizes)
     packed = jnp.concatenate([pre_gain, mid_gain, query_gain, key_gain])
     packed = jnp.pad(packed, (0, -used % 128)).reshape(1, -1)
+    w_qkv = lax.all_gather(jnp.concatenate([w_query, w_key, w_value], axis=1), "dp", axis=0, tiled=True)
+    xs = [layer_in, around(layer_in)]
+    steps = list(zip(near_last, near_last[:-1][::-1] + near_last[-1:]))
+    blocks = [{0: w_gate_up[:, 0]}, {0: w_gate_up[:, 1]}]
+
+    def double(hop):
+        if steps:
+            for i, bit in enumerate(steps.pop(0)):
+                blocks[i] = doubling_step(blocks[i], bit)
+            blocks[:], hop = barrier((blocks, hop))
+        return hop
+
+    xs[1] = double(xs[1])
+    w_output, packed, _ = barrier((w_output, packed, xs[1]))
     output_w = lax.all_gather(w_output, "tensor", axis=0, tiled=True)
-    w_qkv = lax.all_gather(jnp.concatenate([w_query, w_key, w_value], axis=1), "dp", axis=0, tiled=True)
-    gate_up_w = lax.all_gather(w_gate_up.transpose(1, 0, 2), "dp", axis=1, tiled=True)
-    down_w = lax.all_gather(w_down, "dp", axis=1, tiled=True)
-
-    xs = [layer_in, around(layer_in)]
-    output_w, packed, _ = barrier((output_w, packed, xs[1]))
-    output_w = lax.all_gather(output_w, "dp", axis=1, tiled=True)
     gains = lax.all_gather(packed, "dp", axis=0, tiled=True).astype(F32)
     starts = [sum(sizes[:i]) for i in range(5)]
     pre_full, mid_full, gain_query, gain_key = (
@@ -386,11 +420,18 @@
         normed_full = lax.dynamic_update_slice(normed_full, normed, at)
         qkv = lax.dynamic_update_slice(qkv, dot(normed, w_qkv), at)
         if k == parts - 2:
-            qkv, normed_full, xs[-1] = barrier((qkv, normed_full, xs[-1]))
-
+            xs[-1] = double(xs[-1])
+            qkv, normed_full, xs[-1], output_w = barrier((qkv, normed_full, xs[-1], output_w))
+            output_w = lax.all_gather(output_w, "dp", axis=1, tiled=True)
+
+    down_w = lax.all_gather(w_down, "dp", axis=1, tiled=True)
     first_og, _ = barrier((out_grad, xs[-1]))
     ogs = [out_grad, around(first_og)]
     attention, lse = forward_heads(qkv, cosine, sine, gain_query, gain_key, heads, kv_heads)
+    ogs[1] = double(ogs[1])
+    while steps:
+        ogs[1] = double(ogs[1])
+    gate_blocks, up_blocks = ([held[r] for r in relative] for held in blocks)
     attention, ogs[1] = barrier((attention, ogs[1]))
     ogs.append(around(ogs[1]))
     mixed = lax.all_to_all(
@@ -404,63 +445,67 @@
     resid = inputs_wide + dot(mixed, output_w)
     scale_mid = rms_scale(resid)
     normal_mid = resid * scale_mid
-    mids = gather_ring((normal_mid * mid_full).astype(BF16))
-
+    mids = gather_ring(
+        shuffled((normal_mid * mid_full).astype(BF16), mine ^ jnp.asarray(relative, jnp.int32))
+    )
     pieces = {}
 
-    def back_part(k):
-        pieces[k] = hidden_piece(mids[k], ogs[k], gate_up_w, down_w)
+    def piece(k):
+        pieces[k] = hidden_piece(mids[k], ogs[k], gate_blocks, up_blocks, down_w)
         return pieces[k][3]
 
     def rows_of(blocks):
         return jnp.concatenate(blocks, axis=0)
 
     def column(i):
-        return [pieces[k][i] for k in range(parts)]
-
-    def all_pieces():
-        for k in range(2, parts):
-            back_part(k)
-        back_part(0)
-        return ()
-
-    back_part(1)
-    grad_mid_in, (_, part_gate, (part_up, part_down)) = scatter_ring(
-        lambda k: pieces[k][3],
-        (
-            all_pieces,
-            lambda: contract_rows(rows_of(mids), rows_of(column(1))).astype(BF16),
-            lambda: (
-                contract_rows(rows_of(mids), rows_of(column(2))).astype(BF16),
-                contract_rows(rows_of(column(0)), rows_of(ogs)).astype(BF16),
-            ),
-        ),
-    )
-    summed_gate, summed_down = scattered(part_gate, 0), scattered(part_down, 1)
+        return rows_of([pieces[k][i] for k in range(parts)])
+
+    half = width // 2
+    piece(1)
+    grad_mid_in, made = scatter_ring(
+        piece, [tuple] * (parts - 2) + [lambda: contract_rows(column(0), rows_of(ogs)).astype(BF16)]
+    )
+    part_down = made[-1]
+    mid_rows, grad_gates, grad_ups = rows_of(mids), column(1), column(2)
+    give_gate, give_up = (contract_rows(mid_rows[:, half:], g).astype(BF16) for g in (grad_gates, grad_ups))
+    grad_mid_in, give_gate, give_up = barrier((grad_mid_in, give_gate, give_up))
+    summed_down = scattered(part_down, 1)
+    back_order = [relative.index(r) for r in range(dp)]
+    grad_mid_in = shuffled(
+        grad_mid_in, jnp.asarray(back_order, jnp.int32)[mine ^ jnp.arange(dp, dtype=jnp.int32)]
+    )
     grad_resid = out_grad.astype(F32) + rms_back(normal_mid, scale_mid, mid_full, grad_mid_in)
     part_mid = jnp.sum(grad_mid_in * normal_mid, axis=0)
     grad_resid_b = grad_resid.astype(BF16)
 
-    late = barrier((column(4), grad_resid_b))[0]
+    late = barrier(([pieces[k][4] for k in range(parts)], grad_resid_b))[0]
     down_move = around(late[1].astype(BF16))
     grad_mixed = contract_cols(grad_resid_b, output_w).astype(BF16)
     grad_mixed = grad_mixed.reshape(rows, parts, heads * head_size).transpose(1, 0, 2)
     grad_attn = lax.all_to_all(grad_mixed, "tensor", 0, 0, tiled=True).reshape(all_rows, heads * head_size)
-    up_state = halves_step(halves_split(halves_start(part_up)))
-    part_output = contract_rows(grad_resid_b, mixed).astype(BF16)
-    grad_attn, down_move, part_output, up_blocks = barrier(
-        (grad_attn, down_move, part_output, [u[0] for u in up_state])
-    )
-    up_state = [(block, *u[1:]) for block, u in zip(up_blocks, up_state)]
+    part_output = contract_rows(mixed, grad_resid_b).astype(BF16)
+    gate_held = by_name(
+        halving_step(contract_rows(mid_rows[:, :half], grad_gates).astype(BF16), give_gate, 0), relative[: dp // 2]
+    )
+    up_held = by_name(
+        halving_step(contract_rows(mid_rows[:, :half], grad_ups).astype(BF16), give_up, 0), relative[: dp // 2]
+    )
+    for at in range(bits - 2):
+        gate_held, up_held = halve(gate_held, bits - 1 - at), halve(up_held, 1 + at)
+    grad_attn, down_move, part_output, gate_held, up_held = barrier(
+        (grad_attn, down_move, part_output, gate_held, up_held)
+    )
+    summed_output = scattered(part_output, 1)
     down_move = around((late[2] + down_move.astype(F32)).astype(BF16))
-    out_block, out_left = halves_start(part_output)
+    gate_held, up_held = halve(gate_held, 1), halve(up_held, bits - 1)
 
     grad_qkv, gain_parts = backward_heads(
         qkv, grad_attn, lse, cosine, sine, gain_query, gain_key, heads, kv_heads
     )
-    grad_qkv, down_move, out_block, summed_up, summed_gate = barrier(
-        (grad_qkv, down_move, out_block, halves_end(up_state), summed_gate)
-    )
+    grad_qkv, down_move, gate_held, up_held, summed_down = barrier(
+        (grad_qkv, down_move, gate_held, up_held, summed_down)
+    )
+    summed_gate, summed_up = gate_held[0], up_held[0]
     for k in range(3, parts):
         down_move = around((late[k] + down_move.astype(F32)).astype(BF16))
     layer_out = (resid + late[0] + down_move.astype(F32)).astype(BF16)
@@ -474,26 +519,19 @@
 
     def gain_filler():
         packed = jnp.concatenate([part_pre, part_mid, gain_parts[0], gain_parts[1]])
-        return butterfly(packed.reshape(-1, 128)).reshape(-1), summed_down
-
-    grad_pre_in, ((part_qkv, out_rows), (gain_sums, summed_down), _) = scatter_ring(
+        return butterfly(packed.reshape(-1, 128)).reshape(-1)
+
+    grad_pre_in, (part_qkv, (gain_sums, summed_output), _) = scatter_ring(
         lambda k: grads_in[k],
         (
-            lambda: (
-                contract_rows(normed_full, grad_qkv).astype(BF16),
-                halves_end(halves_split((out_block, out_left))),
-            ),
-            gain_filler,
+            lambda: contract_rows(normed_full, grad_qkv).astype(BF16),
+            lambda: (gain_filler(), summed_output),
         ),
     )
     summed_qkv = scattered(part_qkv, 0).astype(F32)
-    out_cols = out_rows.shape[1] // parts
-    summed_output, _ = scatter_ring(
-        lambda k: lax.dynamic_slice(
-            out_rows, (0, place(k) * out_cols), (out_rows.shape[0], out_cols)
-        ).astype(F32)
-    )
-    summed_output = summed_output.T
+    summed_output = lax.psum_scatter(
+        summed_output, "tensor", scatter_dimension=0, tiled=True
+    ).astype(F32)
     scale_pre = normals[0][1]
     back_pre = rms_back(inputs_wide * scale_pre, scale_pre, pre_full, grad_pre_in)
     in_grad = (grad_resid + back_pre).astype(BF16)

time: 739 us -> 672 us (0.909)
  waiting for transfers between devices: 338 us -> 295 us
  local copies, waits for them, and re-layouts: 68.2 us -> 40.3 us
    ppermute x21 -> x18, waiting for transfers between devices: 253 us -> 179 us  [around(): return lax.ppermute(block, 'tensor', ring)]
    ppermute x10 -> x20, waiting for transfers between devices: 25.6 us -> 71.3 us  [swap(): return lax.ppermute(block, 'dp', [(i, i ^ 1 << bit) for i in range(dp)])]
    all_gather x1 -> x0, waiting for transfers between devices: 17.3 us -> none  [on_device(): lax.all_gather(w_gate_up.transpose(1, 0, 2), 'dp', axis=1, tiled=True)]
    dynamic_slice x2 -> x0, local copies, waits for them, and re-layouts: 14.7 us -> none  [halve(): lax.dynamic_index_in_dim(block, at, axis, keepdims=False)]
    squeeze x9 -> x0, local copies, waits for them, and re-layouts: 10.6 us -> none  [halve(): lax.dynamic_index_in_dim(block, at, axis, keepdims=False)]
    convert_element_type x13 -> x6, other arithmetic: 24.2 us -> 14.1 us  [the longest x4 11.1 us: halve(): (held[r].astype(F32) + far[i * size:(i + 1) * size].astype(F32)).astype(B...]
    pallas_call x4 -> x6, Pallas kernels: 73.2 us -> 78.1 us  [the longest x4 71.3 us: hidden_piece(): pl.pallas_call(functools.partial(hidden_kernel, blocks), grid=(units // t...]
    ppermute x21 -> x18, starting transfers between devices: 16.1 us -> 12.6 us  [around(): return lax.ppermute(block, 'tensor', ring)]
  transfers between devices with their start and end apart: 46 -> 53, of which waited for: 27 -> 30; matrix products, arithmetic and copies ran while one was open for 29% -> 27% of each run, Pallas kernels for 14% -> 16%
where the time goes in v2:
time: 672 us; the launch traced here: 664 us
  waiting for transfers between devices  295 us (44%)
  Pallas kernels  108 us (16%)
  matrix products  86.9 us (13%)
  other arithmetic  69 us (10%)
  local copies, waits for them, and re-layouts  40.3 us (6%)
  starting transfers between devices  39 us (6%)
  between operations  15 us (2%)
  blocking collectives  10.2 us (2%)
    ppermute x18, waiting for transfers between devices, around(): return lax.ppermute(block, 'tensor', ring)  179 us
    pallas_call x4, Pallas kernels, hidden_piece(): pl.pallas_call(functools.partial(hidden_kernel, blocks), grid=(units // t...  71.3 us
    ppermute x20, waiting for transfers between devices, swap(): return lax.ppermute(block, 'dp', [(i, i ^ 1 << bit) for i in range(dp)])  71.3 us
    dot_general x7, matrix products, contract_rows(): lax.dot_general(left, right, (((0,), (0,)), ((), ())), preferred_element_...  48.5 us
    ppermute x5, waiting for transfers between devices, butterfly(): lax.ppermute(values, axis, [(i, i ^ 1 << bit) for i in range(size)])  25.6 us
    unnamed x129, local copies, waits for them, and re-layouts  21 us
    dot_general x5, matrix products, contract_cols(): lax.dot_general(left, right, (((1,), (1,)), ((), ())), preferred_element_...  19.4 us
    pallas_call x1, Pallas kernels, backward_heads(): pl.pallas_call(functools.partial(attention_backward, group, size, heads,...  19.4 us
  transfers between devices with their start and end apart: 53, of which 30 were waited for; matrix products, arithmetic and copies ran while one was open for 27% of the time, Pallas kernels for 16%

profile of v2, /device:TPU:0, one launch (start us, length us, event | category | flops | bytes accessed | tf_op | source)
XLA Modules:
  0.0 663.8 jit_solution(16444545559135143370)
XLA Ops:
  20.2 20.5 %collective-permute-done.refs_1_ = bf16[256,1536]{1,0:T(8,128)(2,1)} collective-permute-done((bf16[256,1536]{1,0:T(8,128)(2,1)}, bf16[256,1536]{1,0:T(8,128)(2,1)}, u32[]{:S(2)}, u32[]{:S(2)}) %collective-permute-start) | collective-permute-done | bytes 786464 | tf_op jit(solution)/shard_map/ppermute | solution.py:351
  45.9 10.2 %all-gather = bf16[8,1,640]{2,1,0:T(2,128)(2,1)S(1)} all-gather(bf16[1,1,640]{2,1,0:T(2,128)(2,1)S(1)} %bitcast.89), channel_id=1, replica_groups=mesh['dp'=8,'tensor'=4] {'dp'}, dimensions={0}, use_global_device_ids=true | all-gather | bytes 11520 | tf_op jit(solution)/shard_map/all_gather | solution.py:402
  62.7 5.7 collective-permute-done.3
  71.4 5.5 collective-permute-done.4.refs_2_
  76.9 16.2 %collective-permute-done.5.refs_3_ = bf16[256,1536]{1,0:T(8,128)(2,1)} collective-permute-done((bf16[256,1536]{1,0:T(8,128)(2,1)}, bf16[256,1536]{1,0:T(8,128)(2,1)}, u32[]{:S(2)}, u32[]{:S(2)}) %collective-permute-start.5) | collective-permute-done | bytes 786464 | tf_op jit(solution)/shard_map/ppermute | solution.py:351
  94.6 13.3 %collective-permute-done.8 = bf16[256,2048]{1,0:T(8,128)(2,1)S(1)} collective-permute-done((bf16[256,2048]{1,0:T(8,128)(2,1)S(1)}, bf16[256,2048]{1,0:T(8,128)(2,1)S(1)}, u32[]{:S(2)}, u32[]{:S(2)}) %collective-permute-start.8) | collective-permute-done | bytes 1048608 | tf_op jit(solution)/shard_map/ppermute | solution.py:324
  133.0 11.0 %attention_forward.1 = (bf16[1024,512]{1,0:T(8,128)(2,1)}, f32[2,2,1024]{2,1,0:T(2,128)}) custom-call(f32[1024,1024]{1,0:T(8,128)} %convolution_dynamic-update-slice_fusion.q_ref.k_ref.v_ref, f32[1024,1024]{1,0:T(8,128)} %convolution_dynamic-update-slice_fusion.q_ref.k_ref.v_ref, f32[1024,1024]{1,0:T(8,128)} %convolution_dynamic-update-slice_fusion.q_ref.k_ref.v_ref, ...), custom_call_target="tpu_custom_call" | custom-call | flops 2147483648 | bytes 5242880 | tf_op jit(solution)/shard_map/attention_forward/pallas_call | solution.py:239
  144.0 8.7 %collective-permute-done.17.refs_17_ = bf16[256,2048]{1,0:T(8,128)(2,1)} collective-permute-done((bf16[256,2048]{1,0:T(8,128)(2,1)S(1)}, bf16[256,2048]{1,0:T(8,128)(2,1)}, u32[]{:S(2)}, u32[]{:S(2)}) %collective-permute-start.17) | collective-permute-done | bytes 1048608 | tf_op jit(solution)/shard_map/ppermute | solution.py:324
  161.0 40.9 %collective-permute-done.18.refs_17_ = bf16[256,2048]{1,0:T(8,128)(2,1)} collective-permute-done((bf16[256,2048]{1,0:T(8,128)(2,1)}, bf16[256,2048]{1,0:T(8,128)(2,1)}, u32[]{:S(2)}, u32[]{:S(2)}) %collective-permute-start.18) | collective-permute-done | bytes 1048608 | tf_op jit(solution)/shard_map/ppermute | solution.py:324
  207.3 6.2 multiply_reduce_fusion.2
  218.1 5.3 all-gather.12.cloned.1.call-done.refs_18_
  223.3 17.8 %hidden_piece.4 = (bf16[256,1536]{1,0:T(8,128)(2,1)}, bf16[256,1536]{1,0:T(8,128)(2,1)}, bf16[256,1536]{1,0:T(8,128)(2,1)}, f32[256,2048]{1,0:T(8,128)}, f32[256,2048]{1,0:T(8,128)}) custom-call(bf16[256,1536]{1,0:T(8,128)(2,1)} %bitcast.62.refs_0_, bf16[256,1536]{1,0:T(8,128)(2,1)} %collective-permute-done.refs_1_, ...), custom_call_target="tpu_custom_call" | custom-call | flops 9663676416 | bytes 27525120 | tf_op jit(solution)/shard_map/hidden_piece/pallas_call | solution.py:186
  244.2 10.9 %collective-permute-done.19.refs_16_ = bf16[256,2048]{1,0:T(8,128)(2,1)} collective-permute-done((bf16[256,2048]{1,0:T(8,128)(2,1)}, bf16[256,2048]{1,0:T(8,128)(2,1)}, u32[]{:S(2)}, u32[]{:S(2)}) %collective-permute-start.19) | collective-permute-done | bytes 1048608 | tf_op jit(solution)/shard_map/ppermute | solution.py:324
  255.2 17.8 %hidden_piece.5 = (bf16[256,1536]{1,0:T(8,128)(2,1)}, bf16[256,1536]{1,0:T(8,128)(2,1)}, bf16[256,1536]{1,0:T(8,128)(2,1)}, f32[256,2048]{1,0:T(8,128)}, f32[256,2048]{1,0:T(8,128)}) custom-call(bf16[256,1536]{1,0:T(8,128)(2,1)} %bitcast.62.refs_0_, bf16[256,1536]{1,0:T(8,128)(2,1)} %collective-permute-done.refs_1_, ...), custom_call_target="tpu_custom_call" | custom-call | flops 9663676416 | bytes 27525120 | tf_op jit(solution)/shard_map/hidden_piece/pallas_call | solution.py:186
  282.4 17.7 %hidden_piece.6 = (bf16[256,1536]{1,0:T(8,128)(2,1)}, bf16[256,1536]{1,0:T(8,128)(2,1)}, bf16[256,1536]{1,0:T(8,128)(2,1)}, f32[256,2048]{1,0:T(8,128)}, f32[256,2048]{1,0:T(8,128)}) custom-call(bf16[256,1536]{1,0:T(8,128)(2,1)} %bitcast.62.refs_0_, bf16[256,1536]{1,0:T(8,128)(2,1)} %collective-permute-done.refs_1_, ...), custom_call_target="tpu_custom_call" | custom-call | flops 9663676416 | bytes 27525120 | tf_op jit(solution)/shard_map/hidden_piece/pallas_call | solution.py:186
  308.3 23.0 %collective-permute-done.21.refs_16_ = bf16[256,2048]{1,0:T(8,128)(2,1)} collective-permute-done((bf16[256,2048]{1,0:T(8,128)(2,1)}, bf16[256,2048]{1,0:T(8,128)(2,1)}, u32[]{:S(2)}, u32[]{:S(2)}) %collective-permute-start.21) | collective-permute-done | bytes 1048608 | tf_op jit(solution)/shard_map/ppermute | solution.py:324
  331.3 17.9 %hidden_piece.7 = (bf16[256,1536]{1,0:T(8,128)(2,1)}, bf16[256,1536]{1,0:T(8,128)(2,1)}, bf16[256,1536]{1,0:T(8,128)(2,1)}, f32[256,2048]{1,0:T(8,128)}, f32[256,2048]{1,0:T(8,128)}) custom-call(bf16[256,1536]{1,0:T(8,128)(2,1)} %bitcast.62.refs_0_, bf16[256,1536]{1,0:T(8,128)(2,1)} %collective-permute-done.refs_1_, ...), custom_call_target="tpu_custom_call" | custom-call | flops 9663676416 | bytes 27525120 | tf_op jit(solution)/shard_map/hidden_piece/pallas_call | solution.py:186
  358.2 5.1 convolution_convert_fusion.5
  364.3 11.6 %convolution_convert_fusion.1 = bf16[1536,2048]{1,0:T(8,128)(2,1)} fusion(bf16[256,2048]{1,0:T(8,128)(2,1)} %collective-permute-done.22.refs_17_, bf16[256,2048]{1,0:T(8,128)(2,1)} %collective-permute-done.18.refs_17_, bf16[256,2048]{1,0:T(8,128)(2,1)} %collective-permute-done.17.refs_17_, bf16[256,2048]{1,0:T(8,128)(2,1)S(1)} %copy-done.20, ...), kind=kOutput, calls=%fused_computation.2 | convolution fusion | flops 6474956800 | bytes 13631488 | tf_op jit(solution)/shard_map/dot_general | solution.py:28
  379.1 7.8 %convolution_convert_fusion.4 = bf16[1024,1536]{1,0:T(8,128)(2,1)} fusion(bf16[1024,1536]{1,0:T(8,128)(2,1)} %constant_dynamic-update-slice_fusion.4, bf16[1024,2048]{1,0:T(8,128)(2,1)} %copy-done.15), kind=kOutput, calls=%fused_computation.15 | convolution fusion | flops 3222798336 | bytes 8388608 | tf_op jit(solution)/shard_map/dot_general | solution.py:28
  400.7 6.7 %add_convert_fusion.1 = bf16[1024,1536]{1,0:T(8,128)(2,1)S(1)} fusion(bf16[1024,1536]{1,0:T(8,128)(2,1)} %collective-permute-done.27, bf16[1024,1536]{1,0:T(8,128)(2,1)S(1)} %copy-done.44, bf16[1024,2048]{1,0:T(8,128)(2,1)S(1)} %copy-done.16), kind=kOutput, calls=%fused_computation.4 | convolution fusion | flops 3229089792 | bytes 11534336 | tf_op jit(solution)/shard_map/dot_general | solution.py:28
  411.0 5.5 add_convert_fusion
  433.6 5.7 convolution_convert_fusion
  439.4 23.6 %collective-permute-done.28 = bf16[512,1536]{1,0:T(8,128)(2,1)} collective-permute-done((bf16[512,1536]{1,0:T(8,128)(2,1)}, bf16[512,1536]{1,0:T(8,128)(2,1)}, u32[]{:S(2)}, u32[]{:S(2)}) %collective-permute-start.28) | collective-permute-done | bytes 1572896 | tf_op jit(solution)/shard_map/ppermute | solution.py:351
  484.1 19.4 %attention_backward.1 = (bf16[1024,1024]{1,0:T(8,128)(2,1)}, f32[2,128]{1,0:T(2,128)}) custom-call(f32[1024,1024]{1,0:T(8,128)} %convolution_dynamic-update-slice_fusion.q_ref.k_ref.v_ref, f32[1024,1024]{1,0:T(8,128)} %convolution_dynamic-update-slice_fusion.q_ref.k_ref.v_ref, f32[1024,1024]{1,0:T(8,128)} %convolution_dynamic-update-slice_fusion.q_ref.k_ref.v_ref, ...), custom_call_target="tpu_custom_call" | custom-call | flops 5368709120 | bytes 7340032 | tf_op jit(solution)/shard_map/attention_backward/pallas_call | solution.py:265
  509.3 5.1 fusion.29
  517.5 6.1 convolution_convert_fusion.6
  523.6 16.6 %collective-permute-done.35 = bf16[256,2048]{1,0:T(8,128)(2,1)} collective-permute-done((bf16[256,2048]{1,0:T(8,128)(2,1)}, bf16[256,2048]{1,0:T(8,128)(2,1)}, u32[]{:S(2)}, u32[]{:S(2)}) %collective-permute-start.35) | collective-permute-done | bytes 1048608 | tf_op jit(solution)/shard_map/ppermute | solution.py:324
  541.0 5.4 fusion.25
  561.7 15.6 %collective-permute-done.40 = f32[34,128]{1,0:T(8,128)S(1)} collective-permute-done((f32[34,128]{1,0:T(8,128)S(1)}, f32[34,128]{1,0:T(8,128)S(1)}, u32[]{:S(2)}, u32[]{:S(2)}) %collective-permute-start.40) | collective-permute-done | bytes 17440 | tf_op jit(solution)/shard_map/ppermute | solution.py:380
  606.1 7.5 %collective-permute-done.42 = bf16[256,2048]{1,0:T(8,128)(2,1)} collective-permute-done((bf16[256,2048]{1,0:T(8,128)(2,1)}, bf16[256,2048]{1,0:T(8,128)(2,1)}, u32[]{:S(2)}, u32[]{:S(2)}) %collective-permute-start.42) | collective-permute-done | bytes 1048608 | tf_op jit(solution)/shard_map/ppermute | solution.py:324
  615.6 35.2 %collective-permute-done.34 = bf16[256,2048]{1,0:T(8,128)(2,1)} collective-permute-done((bf16[256,2048]{1,0:T(8,128)(2,1)}, bf16[256,2048]{1,0:T(8,128)(2,1)}, u32[]{:S(2)}, u32[]{:S(2)}) %collective-permute-start.34) | collective-permute-done | bytes 1048608 | tf_op jit(solution)/shard_map/ppermute | solution.py:324
  (311 shorter events, 223.2 us)
Async XLA Ops:
  7.2 100.8 %all-gather.6.cloned.1.call-start = ((), (), s32[]{:S(2)}) async-start(), calls=%async_computation.6 | async-start | bytes 4718592 | tf_op jit(solution)/shard_map/all_gather | solution.py:387
  9.3 110.9 %all-gather.8.cloned.1.call-start = ((), (), s32[]{:S(2)}) async-start(), calls=%async_computation.7 | async-start | bytes 1310720 | tf_op jit(solution)/shard_map/all_gather | solution.py:401
  9.4 35.3 %collective-permute-start.2 = (bf16[256,2048]{1,0:T(8,128)(2,1)}, bf16[256,2048]{1,0:T(8,128)(2,1)}, u32[]{:S(2)}, u32[]{:S(2)}) collective-permute-start(bf16[256,2048]{1,0:T(8,128)(2,1)} %param.14), channel_id=1, source_target_pairs={{0,1},{1,2},{2,3},{3,0},{4,5},{5,6},{6,7},{7,4},{8,9},{9,10},{10,1... | collective-permute-start | bytes 3145736 | tf_op jit(solution)/shard_map/ppermute | solution.py:324
  18.2 26.4 %collective-permute-start.1 = (bf16[256,1536]{1,0:T(8,128)(2,1)}, bf16[256,1536]{1,0:T(8,128)(2,1)}, u32[]{:S(2)}, u32[]{:S(2)}) collective-permute-start(bf16[256,1536]{1,0:T(8,128)(2,1)} %bitcast.61.refs_8_), channel_id=1, source_target_pairs={{0,16},{4,20},{8,24},{12,28},{16,0},{20,4},{24,8},{28,12},{1,17},{... | collective-permute-start | bytes 2359304 | tf_op jit(solution)/shard_map/ppermute | solution.py:351
  56.2 37.0 %collective-permute-start.5 = (bf16[256,1536]{1,0:T(8,128)(2,1)}, bf16[256,1536]{1,0:T(8,128)(2,1)}, u32[]{:S(2)}, u32[]{:S(2)}) collective-permute-start(bf16[256,1536]{1,0:T(8,128)(2,1)} %collective-permute-done.refs_1_), channel_id=1, source_target_pairs={{0,16},{4,20},{8,24},{12,28},{16,0},{20,4},{24,8},{28,12},{1,17},{... | collective-permute-start | bytes 2359304 | tf_op jit(solution)/shard_map/ppermute | solution.py:351
  58.2 34.9 %collective-permute-start.6 = (bf16[256,1536]{1,0:T(8,128)(2,1)}, bf16[256,1536]{1,0:T(8,128)(2,1)}, u32[]{:S(2)}, u32[]{:S(2)}) collective-permute-start(bf16[256,1536]{1,0:T(8,128)(2,1)} %bitcast.61.refs_8_), channel_id=1, source_target_pairs={{0,8},{4,12},{8,0},{12,4},{16,24},{20,28},{24,16},{28,20},{1,9},{5... | collective-permute-start | bytes 2359304 | tf_op jit(solution)/shard_map/ppermute | solution.py:351
  58.3 36.3 %collective-permute-start.7 = (bf16[256,1536]{1,0:T(8,128)(2,1)}, bf16[256,1536]{1,0:T(8,128)(2,1)}, u32[]{:S(2)}, u32[]{:S(2)}) collective-permute-start(bf16[256,1536]{1,0:T(8,128)(2,1)} %collective-permute-done.1.refs_10_), channel_id=1, source_target_pairs={{0,8},{4,12},{8,0},{12,4},{16,24},{20,28},{24,16},{28,20},{1,9},{5... | collective-permute-start | bytes 2359304 | tf_op jit(solution)/shard_map/ppermute | solution.py:351
  60.2 147.0 %all-gather.10.cloned.1.call-start = ((), (), s32[]{:S(2)}) async-start(), calls=%async_computation.8 | async-start | bytes 9437184 | tf_op jit(solution)/shard_map/all_gather | solution.py:425
  68.4 39.6 %collective-permute-start.8 = (bf16[256,2048]{1,0:T(8,128)(2,1)S(1)}, bf16[256,2048]{1,0:T(8,128)(2,1)S(1)}, u32[]{:S(2)}, u32[]{:S(2)}) collective-permute-start(bf16[256,2048]{1,0:T(8,128)(2,1)S(1)} %collective-permute-done.3), channel_id=1, source_target_pairs={{0,1},{1,2},{2,3},{3,0},{4,5},{5,6},{6,7},{7,4},{8,9},{9,10},{10,1... | collective-permute-start | bytes 3145736 | tf_op jit(solution)/shard_map/ppermute | solution.py:324
  120.3 103.0 %all-gather.12.cloned.1.call-start = ((), (), s32[]{:S(2)}) async-start(), calls=%async_computation.9 | async-start | bytes 7077888 | tf_op jit(solution)/shard_map/all_gather | solution.py:427
  125.2 27.5 %collective-permute-start.17 = (bf16[256,2048]{1,0:T(8,128)(2,1)S(1)}, bf16[256,2048]{1,0:T(8,128)(2,1)}, u32[]{:S(2)}, u32[]{:S(2)}) collective-permute-start(bf16[256,2048]{1,0:T(8,128)(2,1)S(1)} %copy-done.19), channel_id=1, source_target_pairs={{0,1},{1,2},{2,3},{3,0},{4,5},{5,6},{6,7},{7,4},{8,9},{9,10},{10,1... | collective-permute-start | bytes 3145736 | tf_op jit(solution)/shard_map/ppermute | solution.py:324
  155.0 51.4 %all-to-all-start = ((bf16[4,256,512]{1,2,0:T(8,128)(2,1)}), bf16[4,256,512]{1,2,0:T(8,128)(2,1)S(1)}, u32[]{:S(2)}, u32[]{:S(2)}) async-start(bf16[4,256,512]{1,2,0:T(8,128)(2,1)} %copy.37), calls=%async_computation | async-start | bytes 2097152 | tf_op jit(solution)/shard_map/all_to_all | solution.py:437
  158.5 350.8 %reduce-scatter.5.cloned.1.call-start = ((), (), s32[]{:S(2)}) async-start(), calls=%async_computation.10 | async-start | bytes 7077888 | tf_op jit(solution)/shard_map/reduce_scatter | solution.py:346
  158.5 43.3 %collective-permute-start.18 = (bf16[256,2048]{1,0:T(8,128)(2,1)}, bf16[256,2048]{1,0:T(8,128)(2,1)}, u32[]{:S(2)}, u32[]{:S(2)}) collective-permute-start(bf16[256,2048]{1,0:T(8,128)(2,1)} %collective-permute-done.17.refs_17_), channel_id=1, source_target_pairs={{0,1},{1,2},{2,3},{3,0},{4,5},{5,6},{6,7},{7,4},{8,9},{9,10},{10,1... | collective-permute-start | bytes 3145736 | tf_op jit(solution)/shard_map/ppermute | solution.py:324
  206.3 101.9 %collective-permute-start.22 = (bf16[256,2048]{1,0:T(8,128)(2,1)}, bf16[256,2048]{1,0:T(8,128)(2,1)}, u32[]{:S(2)}, u32[]{:S(2)}) collective-permute-start(bf16[256,2048]{1,0:T(8,128)(2,1)} %collective-permute-done.18.refs_17_), channel_id=1, source_target_pairs={{0,1},{1,2},{2,3},{3,0},{4,5},{5,6},{6,7},{7,4},{8,9},{9,10},{10,1... | collective-permute-start | bytes 3145736 | tf_op jit(solution)/shard_map/ppermute | solution.py:324
  217.7 37.3 %collective-permute-start.19 = (bf16[256,2048]{1,0:T(8,128)(2,1)}, bf16[256,2048]{1,0:T(8,128)(2,1)}, u32[]{:S(2)}, u32[]{:S(2)}) collective-permute-start(bf16[256,2048]{1,0:T(8,128)(2,1)} %shuffled.2.refs_16_), channel_id=1, source_target_pairs={{0,1},{1,2},{2,3},{3,0},{4,5},{5,6},{6,7},{7,4},{8,9},{9,10},{10,1... | collective-permute-start | bytes 3145736 | tf_op jit(solution)/shard_map/ppermute | solution.py:324
  255.1 27.4 %collective-permute-start.20 = (bf16[256,2048]{1,0:T(8,128)(2,1)}, bf16[256,2048]{1,0:T(8,128)(2,1)}, u32[]{:S(2)}, u32[]{:S(2)}) collective-permute-start(bf16[256,2048]{1,0:T(8,128)(2,1)} %collective-permute-done.19.refs_16_), channel_id=1, source_target_pairs={{0,1},{1,2},{2,3},{3,0},{4,5},{5,6},{6,7},{7,4},{8,9},{9,10},{10,1... | collective-permute-start | bytes 3145736 | tf_op jit(solution)/shard_map/ppermute | solution.py:324
  275.9 27.2 %collective-permute-start.23 = (bf16[256,2048]{1,0:T(8,128)(2,1)}, bf16[256,2048]{1,0:T(8,128)(2,1)}, u32[]{:S(2)}, u32[]{:S(2)}) collective-permute-start(bf16[256,2048]{1,0:T(8,128)(2,1)} %convert_element_type.230), channel_id=1, source_target_pairs={{0,1},{1,2},{2,3},{3,0},{4,5},{5,6},{6,7},{7,4},{8,9},{9,10},{10,1... | collective-permute-start | bytes 3145736 | tf_op jit(solution)/shard_map/ppermute | solution.py:324
  303.1 28.1 %collective-permute-start.21 = (bf16[256,2048]{1,0:T(8,128)(2,1)}, bf16[256,2048]{1,0:T(8,128)(2,1)}, u32[]{:S(2)}, u32[]{:S(2)}) collective-permute-start(bf16[256,2048]{1,0:T(8,128)(2,1)} %collective-permute-done.20.refs_16_), channel_id=1, source_target_pairs={{0,1},{1,2},{2,3},{3,0},{4,5},{5,6},{6,7},{7,4},{8,9},{9,10},{10,1... | collective-permute-start | bytes 3145736 | tf_op jit(solution)/shard_map/ppermute | solution.py:324
  306.4 44.7 %collective-permute-start.24 = (bf16[256,2048]{1,0:T(8,128)(2,1)}, bf16[256,2048]{1,0:T(8,128)(2,1)}, u32[]{:S(2)}, u32[]{:S(2)}) collective-permute-start(bf16[256,2048]{1,0:T(8,128)(2,1)} %add_convert_fusion.8), channel_id=1, source_target_pairs={{0,1},{1,2},{2,3},{3,0},{4,5},{5,6},{6,7},{7,4},{8,9},{9,10},{10,1... | collective-permute-start | bytes 3145736 | tf_op jit(solution)/shard_map/ppermute | solution.py:324
  408.7 54.3 %collective-permute-start.28 = (bf16[512,1536]{1,0:T(8,128)(2,1)}, bf16[512,1536]{1,0:T(8,128)(2,1)}, u32[]{:S(2)}, u32[]{:S(2)}) collective-permute-start(bf16[512,1536]{1,0:T(8,128)(2,1)} %concatenate.48), channel_id=1, source_target_pairs={{0,16},{4,20},{8,24},{12,28},{16,0},{20,4},{24,8},{28,12},{1,17},{... | collective-permute-start | bytes 4718600 | tf_op jit(solution)/shard_map/ppermute | solution.py:351
  418.7 47.5 %collective-permute-start.30 = (bf16[512,1536]{1,0:T(8,128)(2,1)}, bf16[512,1536]{1,0:T(8,128)(2,1)}, u32[]{:S(2)}, u32[]{:S(2)}) collective-permute-start(bf16[512,1536]{1,0:T(8,128)(2,1)} %pad_maximum_fusion.1), channel_id=1, source_target_pairs={{0,8},{4,12},{8,0},{12,4},{16,24},{20,28},{24,16},{28,20},{1,9},{5... | collective-permute-start | bytes 4718600 | tf_op jit(solution)/shard_map/ppermute | solution.py:351
  424.4 52.8 %all-to-all-start.1 = ((bf16[4,256,512]{2,1,0:T(8,128)(2,1)}), bf16[4,256,512]{2,1,0:T(8,128)(2,1)}, u32[]{:S(2)}, u32[]{:S(2)}) async-start(bf16[4,256,512]{2,1,0:T(8,128)(2,1)} %bitcast.68), calls=%async_computation.1 | async-start | bytes 2097152 | tf_op jit(solution)/shard_map/all_to_all | solution.py:485
  428.7 153.4 %reduce-scatter.7.cloned.1.call-start = ((), (), s32[]{:S(2)}) async-start(), calls=%async_computation.11 | async-start | bytes 9437184 | tf_op jit(solution)/shard_map/reduce_scatter | solution.py:346
  431.7 41.0 %collective-permute-start.26 = (bf16[256,2048]{1,0:T(8,128)(2,1)}, bf16[256,2048]{1,0:T(8,128)(2,1)}, u32[]{:S(2)}, u32[]{:S(2)}) collective-permute-start(bf16[256,2048]{1,0:T(8,128)(2,1)} %convert_element_type.241), channel_id=1, source_target_pairs={{0,1},{1,2},{2,3},{3,0},{4,5},{5,6},{6,7},{7,4},{8,9},{9,10},{10,1... | collective-permute-start | bytes 3145736 | tf_op jit(solution)/shard_map/ppermute | solution.py:324
  477.3 123.9 %reduce-scatter.9.cloned.1.call-start = ((), (), s32[]{:S(2)}) async-start(), calls=%async_computation.12 | async-start | bytes 4718592 | tf_op jit(solution)/shard_map/reduce_scatter | solution.py:346
  482.8 26.5 %collective-permute-start.31 = (bf16[256,2048]{1,0:T(8,128)(2,1)}, bf16[256,2048]{1,0:T(8,128)(2,1)}, u32[]{:S(2)}, u32[]{:S(2)}) collective-permute-start(bf16[256,2048]{1,0:T(8,128)(2,1)} %add_convert_fusion.6), channel_id=1, source_target_pairs={{0,1},{1,2},{2,3},{3,0},{4,5},{5,6},{6,7},{7,4},{8,9},{9,10},{10,1... | collective-permute-start | bytes 3145736 | tf_op jit(solution)/shard_map/ppermute | solution.py:324
  514.5 25.8 %collective-permute-start.35 = (bf16[256,2048]{1,0:T(8,128)(2,1)}, bf16[256,2048]{1,0:T(8,128)(2,1)}, u32[]{:S(2)}, u32[]{:S(2)}) collective-permute-start(bf16[256,2048]{1,0:T(8,128)(2,1)} %get-tuple-element.261), channel_id=1, source_target_pairs={{0,1},{1,2},{2,3},{3,0},{4,5},{5,6},{6,7},{7,4},{8,9},{9,10},{10,1... | collective-permute-start | bytes 3145736 | tf_op jit(solution)/shard_map/ppermute | solution.py:324
  540.3 114.6 %reduce-scatter.11.cloned.1.call-start = ((), (), s32[]{:S(2)}) async-start(), calls=%async_computation.13 | async-start | bytes 1310720 | tf_op jit(solution)/shard_map/reduce_scatter | solution.py:532
  552.7 29.3 %collective-permute-start.36 = (bf16[256,2048]{1,0:T(8,128)(2,1)}, bf16[256,2048]{1,0:T(8,128)(2,1)}, u32[]{:S(2)}, u32[]{:S(2)}) collective-permute-start(bf16[256,2048]{1,0:T(8,128)(2,1)} %add_convert_fusion.3), channel_id=1, source_target_pairs={{0,1},{1,2},{2,3},{3,0},{4,5},{5,6},{6,7},{7,4},{8,9},{9,10},{10,1... | collective-permute-start | bytes 3145736 | tf_op jit(solution)/shard_map/ppermute | solution.py:324
  585.3 28.3 %collective-permute-start.42 = (bf16[256,2048]{1,0:T(8,128)(2,1)}, bf16[256,2048]{1,0:T(8,128)(2,1)}, u32[]{:S(2)}, u32[]{:S(2)}) collective-permute-start(bf16[256,2048]{1,0:T(8,128)(2,1)} %add_convert_fusion.2), channel_id=1, source_target_pairs={{0,1},{1,2},{2,3},{3,0},{4,5},{5,6},{6,7},{7,4},{8,9},{9,10},{10,1... | collective-permute-start | bytes 3145736 | tf_op jit(solution)/shard_map/ppermute | solution.py:324
  587.8 62.9 %collective-permute-start.34 = (bf16[256,2048]{1,0:T(8,128)(2,1)}, bf16[256,2048]{1,0:T(8,128)(2,1)}, u32[]{:S(2)}, u32[]{:S(2)}) collective-permute-start(bf16[256,2048]{1,0:T(8,128)(2,1)} %add_convert_fusion.5), channel_id=1, source_target_pairs={{0,1},{1,2},{2,3},{3,0},{4,5},{5,6},{6,7},{7,4},{8,9},{9,10},{10,1... | collective-permute-start | bytes 3145736 | tf_op jit(solution)/shard_map/ppermute | solution.py:324
  (79 other events, 844.4 us)
Sparse Core Ops, SparseCore 0:
  10.5 45.2 all-gather.5
  60.4 44.4 all-gather.7
  120.4 54.5 all-gather.9
  176.7 46.5 all-gather.11
  379.2 81.9 reduce-scatter.4
  477.4 69.1 reduce-scatter.6
  550.0 51.1 reduce-scatter.8
  603.4 44.4 reduce-scatter.10

commit v3 on v2

--- a/solution.py
+++ b/solution.py
@@ -6,6 +6,7 @@
 from jax.experimental import pallas as pl
 from jax.experimental.pallas import tpu as pltpu
 from jax.sharding import PartitionSpec as P
+
 
 L = 1024
 
@@ -325,11 +326,11 @@
 
     def gather_ring(block):
         blocks = [block]
-        for _ in range(parts - 1):
+        for _ in range(1, parts):
             blocks.append(around(blocks[-1]))
         return blocks
 
-    def scatter_ring(part, fillers=()):
+    def scatter_ring(part, fillers=(), tied=None):
         order = list(range(1, parts)) + [0]
         made = []
         total = part(order[0])
@@ -340,6 +341,8 @@
             moving, ahead, new = barrier((moving, ahead, new))
             total = ahead + moving.astype(F32)
             made.append(new)
+            if tied is not None and isinstance(new, tuple) and len(new) > 1:
+                tied.append(new[1])
         return total, made
 
     def scattered(part, axis):
@@ -396,7 +399,8 @@
             blocks[:], hop = barrier((blocks, hop))
         return hop
 
-    xs[1] = double(xs[1])
+    cosine, sine = rope_tables(head_size)
+    xs[1], cosine, sine = barrier((xs[1], cosine, sine))
     w_output, packed, _ = barrier((w_output, packed, xs[1]))
     output_w = lax.all_gather(w_output, "tensor", axis=0, tiled=True)
     gains = lax.all_gather(packed, "dp", axis=0, tiled=True).astype(F32)
@@ -404,7 +408,6 @@
     pre_full, mid_full, gain_query, gain_key = (
         gains[:, lo:hi].reshape(1, -1) for lo, hi in zip(starts, starts[1:])
     )
-    cosine, sine = rope_tables(head_size)
 
     normals = []
     qkv = jnp.zeros((all_rows, w_qkv.shape[1]), F32)
@@ -419,8 +422,10 @@
         at = (place(k) * rows, 0)
         normed_full = lax.dynamic_update_slice(normed_full, normed, at)
         qkv = lax.dynamic_update_slice(qkv, dot(normed, w_qkv), at)
+        if k == 1:
+            xs[2] = double(xs[2])
+            qkv, normed_full, xs[2] = barrier((qkv, normed_full, xs[2]))
         if k == parts - 2:
-            xs[-1] = double(xs[-1])
             qkv, normed_full, xs[-1], output_w = barrier((qkv, normed_full, xs[-1], output_w))
             output_w = lax.all_gather(output_w, "dp", axis=1, tiled=True)
 
@@ -428,10 +433,6 @@
     first_og, _ = barrier((out_grad, xs[-1]))
     ogs = [out_grad, around(first_og)]
     attention, lse = forward_heads(qkv, cosine, sine, gain_query, gain_key, heads, kv_heads)
-    ogs[1] = double(ogs[1])
-    while steps:
-        ogs[1] = double(ogs[1])
-    gate_blocks, up_blocks = ([held[r] for r in relative] for held in blocks)
     attention, ogs[1] = barrier((attention, ogs[1]))
     ogs.append(around(ogs[1]))
     mixed = lax.all_to_all(
@@ -439,6 +440,8 @@
     )
     mixed = mixed.transpose(1, 0, 2).reshape(rows, parts * heads * head_size)
     mixed, ogs[-1] = barrier((mixed, ogs[-1]))
+    while len(steps) > 1:
+        mixed = double(mixed)
     for k in range(2, parts - 1):
         ogs.append(around(ogs[k]))
     inputs_wide = normals[0][0]
@@ -448,6 +451,9 @@
     mids = gather_ring(
         shuffled((normal_mid * mid_full).astype(BF16), mine ^ jnp.asarray(relative, jnp.int32))
     )
+    if parts > 1:
+        mids[1] = double(mids[1])
+    gate_blocks, up_blocks = ([held[r] for r in relative] for held in blocks)
     pieces = {}
 
     def piece(k):
@@ -462,14 +468,16 @@
 
     half = width // 2
     piece(1)
-    grad_mid_in, made = scatter_ring(
-        piece, [tuple] * (parts - 2) + [lambda: contract_rows(column(0), rows_of(ogs)).astype(BF16)]
-    )
-    part_down = made[-1]
+    down_parts = []
+
+    def down_filler():
+        down_parts.append(contract_rows(column(0), rows_of(ogs)).astype(BF16))
+        return down_parts[0]
+
+    grad_mid_in, _ = scatter_ring(piece, [tuple] * (parts - 2) + [down_filler])
+    summed_down = scattered(down_parts[0], 1)
     mid_rows, grad_gates, grad_ups = rows_of(mids), column(1), column(2)
-    give_gate, give_up = (contract_rows(mid_rows[:, half:], g).astype(BF16) for g in (grad_gates, grad_ups))
-    grad_mid_in, give_gate, give_up = barrier((grad_mid_in, give_gate, give_up))
-    summed_down = scattered(part_down, 1)
+    gives = [contract_rows(mid_rows[:, half:], grads).astype(BF16) for grads in (grad_gates, grad_ups)]
     back_order = [relative.index(r) for r in range(dp)]
     grad_mid_in = shuffled(
         grad_mid_in, jnp.asarray(back_order, jnp.int32)[mine ^ jnp.arange(dp, dtype=jnp.int32)]
@@ -482,33 +490,24 @@
     down_move = around(late[1].astype(BF16))
     grad_mixed = contract_cols(grad_resid_b, output_w).astype(BF16)
     grad_mixed = grad_mixed.reshape(rows, parts, heads * head_size).transpose(1, 0, 2)
-    grad_attn = lax.all_to_all(grad_mixed, "tensor", 0, 0, tiled=True).reshape(all_rows, heads * head_size)
+    grad_attn = lax.all_to_all(grad_mixed, "tensor", 0, 0, tiled=True)
+    grad_attn = grad_attn.reshape(all_rows, heads * head_size)
+    mixed, grad_resid_b, _ = barrier((mixed, grad_resid_b, grad_mixed))
     part_output = contract_rows(mixed, grad_resid_b).astype(BF16)
-    gate_held = by_name(
-        halving_step(contract_rows(mid_rows[:, :half], grad_gates).astype(BF16), give_gate, 0), relative[: dp // 2]
-    )
-    up_held = by_name(
-        halving_step(contract_rows(mid_rows[:, :half], grad_ups).astype(BF16), give_up, 0), relative[: dp // 2]
-    )
-    for at in range(bits - 2):
-        gate_held, up_held = halve(gate_held, bits - 1 - at), halve(up_held, 1 + at)
-    grad_attn, down_move, part_output, gate_held, up_held = barrier(
-        (grad_attn, down_move, part_output, gate_held, up_held)
-    )
     summed_output = scattered(part_output, 1)
+    mid_rows, grad_gates, grad_ups, _, _ = barrier((mid_rows, grad_gates, grad_ups, grad_mixed, part_output))
+    held = []
+    for give, grads in zip(gives, (grad_gates, grad_ups)):
+        keep = contract_rows(mid_rows[:, :half], grads).astype(BF16)
+        held.append(by_name(halving_step(keep, give, 0), relative[: dp // 2]))
+    grad_attn, down_move, held = barrier((grad_attn, down_move, held))
     down_move = around((late[2] + down_move.astype(F32)).astype(BF16))
-    gate_held, up_held = halve(gate_held, 1), halve(up_held, bits - 1)
+    held = [halve(held[0], bits - 1), halve(held[1], 1)]
 
     grad_qkv, gain_parts = backward_heads(
         qkv, grad_attn, lse, cosine, sine, gain_query, gain_key, heads, kv_heads
     )
-    grad_qkv, down_move, gate_held, up_held, summed_down = barrier(
-        (grad_qkv, down_move, gate_held, up_held, summed_down)
-    )
-    summed_gate, summed_up = gate_held[0], up_held[0]
-    for k in range(3, parts):
-        down_move = around((late[k] + down_move.astype(F32)).astype(BF16))
-    layer_out = (resid + late[0] + down_move.astype(F32)).astype(BF16)
+    grad_qkv, summed_down = barrier((grad_qkv, summed_down))
 
     grads_in, part_pre = [], 0.0
     for k in range(parts):
@@ -521,17 +520,47 @@
         packed = jnp.concatenate([part_pre, part_mid, gain_parts[0], gain_parts[1]])
         return butterfly(packed.reshape(-1, 128)).reshape(-1)
 
-    grad_pre_in, (part_qkv, (gain_sums, summed_output), _) = scatter_ring(
-        lambda k: grads_in[k],
-        (
-            lambda: contract_rows(normed_full, grad_qkv).astype(BF16),
-            lambda: (gain_filler(), summed_output),
-        ),
-    )
-    summed_qkv = scattered(part_qkv, 0).astype(F32)
+    part_qkv = contract_rows(normed_full, grad_qkv).astype(BF16)
+    moves = [down_move, held]
+
+    def first_filler():
+        return part_qkv, moves, summed_output
+
+    def second_filler():
+        return gain_filler(), moves
+
+    def step_moves(last):
+        at = len(moves_done) + 1
+        moves_done.append(last)
+        down_move, held = last
+        if 2 + at < parts:
+            down_move = around((late[2 + at] + down_move.astype(F32)).astype(BF16))
+        if at < bits - 1:
+            held = [halve(held[0], bits - 1 - at), halve(held[1], 1 + at)]
+        return [down_move, held]
+
+    moves_done, tied = [], []
+
+    def filler(make):
+        def run():
+            nonlocal moves
+            if tied:
+                moves = step_moves(tied[-1])
+            return make()
+
+        return run
+
+    grad_pre_in, made = scatter_ring(lambda k: grads_in[k], (filler(first_filler), filler(second_filler)), tied)
+    _, _, summed_output = made[0]
+    gain_sums, (down_move, held) = made[1]
+    for at in range(len(moves_done) + 1, max(bits - 1, parts - 2)):
+        down_move, held = step_moves([down_move, held])
+    summed_gate, summed_up = (h[0] for h in held)
+    layer_out = (resid + late[0] + down_move.astype(F32)).astype(BF16)
     summed_output = lax.psum_scatter(
         summed_output, "tensor", scatter_dimension=0, tiled=True
     ).astype(F32)
+    summed_qkv = scattered(part_qkv, 0).astype(F32)
     scale_pre = normals[0][1]
     back_pre = rms_back(inputs_wide * scale_pre, scale_pre, pre_full, grad_pre_in)
     in_grad = (grad_resid + back_pre).astype(BF16)

time: 672 us -> 782 us (1.16)
  waiting for transfers between devices: 295 us -> 415 us
    ppermute x18, waiting for transfers between devices: 179 us -> 275 us  [around(): return lax.ppermute(block, 'tensor', ring)]
    ppermute x5, waiting for transfers between devices: 25.6 us -> 98.5 us  [butterfly(): lax.ppermute(values, axis, [(i, i ^ 1 << bit) for i in range(size)])]
    ppermute x20, waiting for transfers between devices: 71.3 us -> 17.8 us  [swap(): return lax.ppermute(block, 'dp', [(i, i ^ 1 << bit) for i in range(dp)])]
    all_gather x1, waiting for transfers between devices: 0.01 us -> 13.8 us  [on_device(): output_w = lax.all_gather(w_output, 'tensor', axis=0, tiled=True)]
    convert_element_type x5, other arithmetic: 15 us -> 6.97 us  [scatter_ring(): moving = around(total.astype(BF16))]
    unnamed x129 -> x131, local copies, waits for them, and re-layouts: 21 us -> 14.2 us
  transfers between devices with their start and end apart: 53 -> 53, of which waited for: 30 -> 27; matrix products, arithmetic and copies ran while one was open for 27% -> 21% of each run, Pallas kernels for 16% -> 12%
where the time goes in v3:
time: 782 us; the launch traced here: 774 us
  waiting for transfers between devices  415 us (53%)
  Pallas kernels  108 us (14%)
  matrix products  83.3 us (11%)
  other arithmetic  65.9 us (8%)
  starting transfers between devices  40.1 us (5%)
  local copies, waits for them, and re-layouts  35.7 us (5%)
  between operations  15.3 us (2%)
  blocking collectives  10.4 us (1%)
    ppermute x18, waiting for transfers between devices, around(): return lax.ppermute(block, 'tensor', ring)  275 us
    ppermute x5, waiting for transfers between devices, butterfly(): lax.ppermute(values, axis, [(i, i ^ 1 << bit) for i in range(size)])  98.5 us
    pallas_call x4, Pallas kernels, hidden_piece(): pl.pallas_call(functools.partial(hidden_kernel, blocks), grid=(units // t...  71.9 us
    dot_general x7, matrix products, contract_rows(): lax.dot_general(left, right, (((0,), (0,)), ((), ())), preferred_element_...  46.4 us
    dot_general x5, matrix products, dot(): return jnp.dot(left, right, preferred_element_type=F32)  18.8 us
    pallas_call x1, Pallas kernels, backward_heads(): pl.pallas_call(functools.partial(attention_backward, group, size, heads,...  18.3 us
    dot_general x5, matrix products, contract_cols(): lax.dot_general(left, right, (((1,), (1,)), ((), ())), preferred_element_...  18.2 us
    ppermute x20, waiting for transfers between devices, swap(): return lax.ppermute(block, 'dp', [(i, i ^ 1 << bit) for i in range(dp)])  17.8 us
  transfers between devices with their start and end apart: 53, of which 27 were waited for; matrix products, arithmetic and copies ran while one was open for 21% of the time, Pallas kernels for 12%

profile of v3, /device:TPU:0, one launch (start us, length us, event | category | flops | bytes accessed | tf_op | source)
XLA Modules:
  0.0 773.8 jit_solution(2349379104710550105)
XLA Ops:
  23.4 14.5 %collective-permute-done.2 = bf16[256,2048]{1,0:T(8,128)(2,1)} collective-permute-done((bf16[256,2048]{1,0:T(8,128)(2,1)}, bf16[256,2048]{1,0:T(8,128)(2,1)}, u32[]{:S(2)}, u32[]{:S(2)}) %collective-permute-start.2) | collective-permute-done | bytes 1048608 | tf_op jit(solution)/shard_map/ppermute | solution.py:325
  38.0 10.4 %all-gather = bf16[8,1,640]{2,1,0:T(2,128)(2,1)S(1)} all-gather(bf16[1,1,640]{2,1,0:T(2,128)(2,1)S(1)} %bitcast.87), channel_id=1, replica_groups=mesh['dp'=8,'tensor'=4] {'dp'}, dimensions={0}, use_global_device_ids=true | all-gather | bytes 11520 | tf_op jit(solution)/shard_map/all_gather | solution.py:406
  56.4 7.9 %collective-permute-done.3 = bf16[256,2048]{1,0:T(8,128)(2,1)S(1)} collective-permute-done((bf16[256,2048]{1,0:T(8,128)(2,1)}, bf16[256,2048]{1,0:T(8,128)(2,1)S(1)}, u32[]{:S(2)}, u32[]{:S(2)}) %collective-permute-start.3) | collective-permute-done | bytes 1048608 | tf_op jit(solution)/shard_map/ppermute | solution.py:325
  78.2 13.8 %all-gather.8.cloned.1.call-done = bf16[2048,256]{1,0:T(8,128)(2,1)} async-done(((bf16[512,256]{1,0:T(8,128)(2,1)}), bf16[2048,256]{1,0:T(8,128)(2,1)}) %all-gather.8.cloned.1.call-update) | async-done | bytes 1048592 | tf_op jit(solution)/shard_map/all_gather | solution.py:405
  92.0 16.5 %collective-permute-done.8 = bf16[256,2048]{1,0:T(8,128)(2,1)S(1)} collective-permute-done((bf16[256,2048]{1,0:T(8,128)(2,1)S(1)}, bf16[256,2048]{1,0:T(8,128)(2,1)S(1)}, u32[]{:S(2)}, u32[]{:S(2)}) %collective-permute-start.8) | collective-permute-done | bytes 1048608 | tf_op jit(solution)/shard_map/ppermute | solution.py:325
  115.4 11.2 %attention_forward.1 = (bf16[1024,512]{1,0:T(8,128)(2,1)}, f32[2,2,1024]{2,1,0:T(2,128)}) custom-call(f32[1024,1024]{1,0:T(8,128)} %convolution_dynamic-update-slice_fusion.q_ref.k_ref.v_ref, f32[1024,1024]{1,0:T(8,128)} %convolution_dynamic-update-slice_fusion.q_ref.k_ref.v_ref, f32[1024,1024]{1,0:T(8,128)} %convolution_dynamic-update-slice_fusion.q_ref.k_ref.v_ref, ...), custom_call_target="tpu_custom_call" | custom-call | flops 2147483648 | bytes 5242880 | tf_op jit(solution)/shard_map/attention_forward/pallas_call | solution.py:240
  126.6 9.3 %collective-permute-done.9.refs_17_ = bf16[256,2048]{1,0:T(8,128)(2,1)} collective-permute-done((bf16[256,2048]{1,0:T(8,128)(2,1)}, bf16[256,2048]{1,0:T(8,128)(2,1)}, u32[]{:S(2)}, u32[]{:S(2)}) %collective-permute-start.9) | collective-permute-done | bytes 1048608 | tf_op jit(solution)/shard_map/ppermute | solution.py:325
  148.2 36.2 %collective-permute-done.10.refs_17_ = bf16[256,2048]{1,0:T(8,128)(2,1)S(1)} collective-permute-done((bf16[256,2048]{1,0:T(8,128)(2,1)}, bf16[256,2048]{1,0:T(8,128)(2,1)S(1)}, u32[]{:S(2)}, u32[]{:S(2)}) %collective-permute-start.10) | collective-permute-done | bytes 1048608 | tf_op jit(solution)/shard_map/ppermute | solution.py:325
  189.0 7.2 collective-permute-done.5.refs_3_
  197.9 6.2 multiply_reduce_fusion.2
  210.8 24.7 %collective-permute-done.19.refs_16_ = bf16[256,2048]{1,0:T(8,128)(2,1)} collective-permute-done((bf16[256,2048]{1,0:T(8,128)(2,1)}, bf16[256,2048]{1,0:T(8,128)(2,1)}, u32[]{:S(2)}, u32[]{:S(2)}) %collective-permute-start.19) | collective-permute-done | bytes 1048608 | tf_op jit(solution)/shard_map/ppermute | solution.py:325
  236.7 17.9 %hidden_piece.4 = (bf16[256,1536]{1,0:T(8,128)(2,1)}, bf16[256,1536]{1,0:T(8,128)(2,1)}, bf16[256,1536]{1,0:T(8,128)(2,1)}, f32[256,2048]{1,0:T(8,128)}, f32[256,2048]{1,0:T(8,128)}) custom-call(bf16[256,1536]{1,0:T(8,128)(2,1)} %bitcast.62.refs_0_, bf16[256,1536]{1,0:T(8,128)(2,1)} %collective-permute-done.refs_1_, ...), custom_call_target="tpu_custom_call" | custom-call | flops 9663676416 | bytes 27525120 | tf_op jit(solution)/shard_map/hidden_piece/pallas_call | solution.py:187
  254.6 9.1 %collective-permute-done.20.refs_16_ = bf16[256,2048]{1,0:T(8,128)(2,1)} collective-permute-done((bf16[256,2048]{1,0:T(8,128)(2,1)}, bf16[256,2048]{1,0:T(8,128)(2,1)}, u32[]{:S(2)}, u32[]{:S(2)}) %collective-permute-start.20) | collective-permute-done | bytes 1048608 | tf_op jit(solution)/shard_map/ppermute | solution.py:325
  263.9 17.9 %hidden_piece.5 = (bf16[256,1536]{1,0:T(8,128)(2,1)}, bf16[256,1536]{1,0:T(8,128)(2,1)}, bf16[256,1536]{1,0:T(8,128)(2,1)}, f32[256,2048]{1,0:T(8,128)}, f32[256,2048]{1,0:T(8,128)}) custom-call(bf16[256,1536]{1,0:T(8,128)(2,1)} %bitcast.62.refs_0_, bf16[256,1536]{1,0:T(8,128)(2,1)} %collective-permute-done.refs_1_, ...), custom_call_target="tpu_custom_call" | custom-call | flops 9663676416 | bytes 27525120 | tf_op jit(solution)/shard_map/hidden_piece/pallas_call | solution.py:187
  281.8 18.0 %hidden_piece.6 = (bf16[256,1536]{1,0:T(8,128)(2,1)}, bf16[256,1536]{1,0:T(8,128)(2,1)}, bf16[256,1536]{1,0:T(8,128)(2,1)}, f32[256,2048]{1,0:T(8,128)}, f32[256,2048]{1,0:T(8,128)}) custom-call(bf16[256,1536]{1,0:T(8,128)(2,1)} %bitcast.62.refs_0_, bf16[256,1536]{1,0:T(8,128)(2,1)} %collective-permute-done.refs_1_, ...), custom_call_target="tpu_custom_call" | custom-call | flops 9663676416 | bytes 27525120 | tf_op jit(solution)/shard_map/hidden_piece/pallas_call | solution.py:187
  299.7 6.8 collective-permute-done.21.refs_16_
  306.6 18.2 %hidden_piece.7 = (bf16[256,1536]{1,0:T(8,128)(2,1)}, bf16[256,1536]{1,0:T(8,128)(2,1)}, bf16[256,1536]{1,0:T(8,128)(2,1)}, f32[256,2048]{1,0:T(8,128)}, f32[256,2048]{1,0:T(8,128)}) custom-call(bf16[256,1536]{1,0:T(8,128)(2,1)} %bitcast.62.refs_0_, bf16[256,1536]{1,0:T(8,128)(2,1)} %collective-permute-done.refs_1_, ...), custom_call_target="tpu_custom_call" | custom-call | flops 9663676416 | bytes 27525120 | tf_op jit(solution)/shard_map/hidden_piece/pallas_call | solution.py:187
  324.8 12.5 %convolution_convert_fusion.1 = bf16[1536,2048]{1,0:T(8,128)(2,1)} fusion(bf16[256,2048]{1,0:T(8,128)(2,1)} %collective-permute-done.22.refs_17_, bf16[256,2048]{1,0:T(8,128)(2,1)} %copy-done.57, bf16[256,2048]{1,0:T(8,128)(2,1)} %collective-permute-done.9.refs_17_, bf16[256,2048]{1,0:T(8,128)(2,1)} %refs_17_.1, bf16[256,1536]{1,0:T(8,128)(2,1)} %get-tuple-element.190, ...), kind=kOutput, calls=%fused_computation.2 | convolution fusion | flops 6474956800 | bytes 13631488 | tf_op jit(solution)/shard_map/dot_general | solution.py:29
  339.4 24.9 %collective-permute-done.23 = bf16[256,2048]{1,0:T(8,128)(2,1)S(1)} collective-permute-done((bf16[256,2048]{1,0:T(8,128)(2,1)S(1)}, bf16[256,2048]{1,0:T(8,128)(2,1)S(1)}, u32[]{:S(2)}, u32[]{:S(2)}) %collective-permute-start.23) | collective-permute-done | bytes 1048608 | tf_op jit(solution)/shard_map/ppermute | solution.py:325
  364.7 24.0 %collective-permute-done.24 = bf16[256,2048]{1,0:T(8,128)(2,1)S(1)} collective-permute-done((bf16[256,2048]{1,0:T(8,128)(2,1)S(1)}, bf16[256,2048]{1,0:T(8,128)(2,1)S(1)}, u32[]{:S(2)}, u32[]{:S(2)}) %collective-permute-start.24) | collective-permute-done | bytes 1048608 | tf_op jit(solution)/shard_map/ppermute | solution.py:325
  391.3 22.3 %collective-permute-done.25 = bf16[256,2048]{1,0:T(8,128)(2,1)} collective-permute-done((bf16[256,2048]{1,0:T(8,128)(2,1)}, bf16[256,2048]{1,0:T(8,128)(2,1)}, u32[]{:S(2)}, u32[]{:S(2)}) %collective-permute-start.25) | collective-permute-done | bytes 1048608 | tf_op jit(solution)/shard_map/ppermute | solution.py:325
  424.1 5.7 convolution_convert_fusion.7
  431.4 5.7 convolution_convert_fusion
  483.4 21.5 %collective-permute-done.26 = bf16[256,2048]{1,0:T(8,128)(2,1)} collective-permute-done((bf16[256,2048]{1,0:T(8,128)(2,1)S(1)}, bf16[256,2048]{1,0:T(8,128)(2,1)}, u32[]{:S(2)}, u32[]{:S(2)}) %collective-permute-start.26) | collective-permute-done | bytes 1048608 | tf_op jit(solution)/shard_map/ppermute | solution.py:325
  515.0 18.3 %attention_backward.1 = (bf16[1024,1024]{1,0:T(8,128)(2,1)}, f32[2,128]{1,0:T(2,128)}) custom-call(f32[1024,1024]{1,0:T(8,128)} %convolution_dynamic-update-slice_fusion.q_ref.k_ref.v_ref, f32[1024,1024]{1,0:T(8,128)} %convolution_dynamic-update-slice_fusion.q_ref.k_ref.v_ref, f32[1024,1024]{1,0:T(8,128)} %convolution_dynamic-update-slice_fusion.q_ref.k_ref.v_ref, ...), custom_call_target="tpu_custom_call" | custom-call | flops 5368709120 | bytes 7340032 | tf_op jit(solution)/shard_map/attention_backward/pallas_call | solution.py:266
  534.1 9.4 %convolution_convert_fusion.6 = bf16[2048,1024]{1,0:T(8,128)(2,1)} fusion(bf16[1024,2048]{1,0:T(8,128)(2,1)} %fusion.59, bf16[1024,1024]{1,0:T(8,128)(2,1)} %get-tuple-element.211), kind=kOutput, calls=%fused_computation.17 | convolution fusion | flops 4297064448 | bytes 10485760 | tf_op jit(solution)/shard_map/dot_general | solution.py:29
  560.4 52.0 %collective-permute-done.35 = f32[34,128]{1,0:T(8,128)S(1)} collective-permute-done((f32[34,128]{1,0:T(8,128)S(1)}, f32[34,128]{1,0:T(8,128)S(1)}, u32[]{:S(2)}, u32[]{:S(2)}) %collective-permute-start.35) | collective-permute-done | bytes 17440 | tf_op jit(solution)/shard_map/ppermute | solution.py:383
  619.4 42.8 %collective-permute-done.37 = f32[34,128]{1,0:T(8,128)S(1)} collective-permute-done((f32[34,128]{1,0:T(8,128)S(1)}, f32[34,128]{1,0:T(8,128)S(1)}, u32[]{:S(2)}, u32[]{:S(2)}) %collective-permute-start.37) | collective-permute-done | bytes 17440 | tf_op jit(solution)/shard_map/ppermute | solution.py:383
  675.8 7.8 %collective-permute-done.40 = bf16[256,1536]{1,0:T(8,128)(2,1)S(1)} collective-permute-done((bf16[256,1536]{1,0:T(8,128)(2,1)}, bf16[256,1536]{1,0:T(8,128)(2,1)S(1)}, u32[]{:S(2)}, u32[]{:S(2)}) %collective-permute-start.40) | collective-permute-done | bytes 786464 | tf_op jit(solution)/shard_map/ppermute | solution.py:354
  687.9 10.0 %collective-permute-done.33 = bf16[256,2048]{1,0:T(8,128)(2,1)S(1)} collective-permute-done((bf16[256,2048]{1,0:T(8,128)(2,1)S(1)}, bf16[256,2048]{1,0:T(8,128)(2,1)S(1)}, u32[]{:S(2)}, u32[]{:S(2)}) %collective-permute-start.33) | collective-permute-done | bytes 1048608 | tf_op jit(solution)/shard_map/ppermute | solution.py:325
  697.8 18.4 %collective-permute-done.39 = bf16[256,2048]{1,0:T(8,128)(2,1)} collective-permute-done((bf16[256,2048]{1,0:T(8,128)(2,1)S(1)}, bf16[256,2048]{1,0:T(8,128)(2,1)}, u32[]{:S(2)}, u32[]{:S(2)}) %collective-permute-start.39) | collective-permute-done | bytes 1048608 | tf_op jit(solution)/shard_map/ppermute | solution.py:325
  727.0 28.4 %collective-permute-done.42 = bf16[256,2048]{1,0:T(8,128)(2,1)} collective-permute-done((bf16[256,2048]{1,0:T(8,128)(2,1)}, bf16[256,2048]{1,0:T(8,128)(2,1)}, u32[]{:S(2)}, u32[]{:S(2)}) %collective-permute-start.42) | collective-permute-done | bytes 1048608 | tf_op jit(solution)/shard_map/ppermute | solution.py:325
  (315 shorter events, 208.9 us)
Async XLA Ops:
  7.2 57.1 %all-gather.6.cloned.1.call-start = ((), (), s32[]{:S(2)}) async-start(), calls=%async_computation.6 | async-start | bytes 4718592 | tf_op jit(solution)/shard_map/all_gather | solution.py:390
  9.3 82.7 %all-gather.8.cloned.1.call-start = ((), (), s32[]{:S(2)}) async-start(), calls=%async_computation.7 | async-start | bytes 1310720 | tf_op jit(solution)/shard_map/all_gather | solution.py:405
  9.4 28.6 %collective-permute-start.2 = (bf16[256,2048]{1,0:T(8,128)(2,1)}, bf16[256,2048]{1,0:T(8,128)(2,1)}, u32[]{:S(2)}, u32[]{:S(2)}) collective-permute-start(bf16[256,2048]{1,0:T(8,128)(2,1)} %param.14), channel_id=1, source_target_pairs={{0,1},{1,2},{2,3},{3,0},{4,5},{5,6},{6,7},{7,4},{8,9},{9,10},{10,1... | collective-permute-start | bytes 3145736 | tf_op jit(solution)/shard_map/ppermute | solution.py:325
  15.7 40.7 %collective-permute-start = (bf16[256,1536]{1,0:T(8,128)(2,1)}, bf16[256,1536]{1,0:T(8,128)(2,1)}, u32[]{:S(2)}, u32[]{:S(2)}) collective-permute-start(bf16[256,1536]{1,0:T(8,128)(2,1)} %bitcast.62.refs_0_), channel_id=1, source_target_pairs={{0,8},{4,12},{8,0},{12,4},{16,24},{20,28},{24,16},{28,20},{1,9},{5... | collective-permute-start | bytes 2359304 | tf_op jit(solution)/shard_map/ppermute | solution.py:354
  18.2 38.2 %collective-permute-start.1 = (bf16[256,1536]{1,0:T(8,128)(2,1)}, bf16[256,1536]{1,0:T(8,128)(2,1)}, u32[]{:S(2)}, u32[]{:S(2)}) collective-permute-start(bf16[256,1536]{1,0:T(8,128)(2,1)} %bitcast.61.refs_8_), channel_id=1, source_target_pairs={{0,16},{4,20},{8,24},{12,28},{16,0},{20,4},{24,8},{28,12},{1,17},{... | collective-permute-start | bytes 2359304 | tf_op jit(solution)/shard_map/ppermute | solution.py:354
  48.4 149.4 %all-gather.10.cloned.1.call-start = ((), (), s32[]{:S(2)}) async-start(), calls=%async_computation.8 | async-start | bytes 9437184 | tf_op jit(solution)/shard_map/all_gather | solution.py:430
  74.2 34.3 %collective-permute-start.8 = (bf16[256,2048]{1,0:T(8,128)(2,1)S(1)}, bf16[256,2048]{1,0:T(8,128)(2,1)S(1)}, u32[]{:S(2)}, u32[]{:S(2)}) collective-permute-start(bf16[256,2048]{1,0:T(8,128)(2,1)S(1)} %collective-permute-done.3), channel_id=1, source_target_pairs={{0,1},{1,2},{2,3},{3,0},{4,5},{5,6},{6,7},{7,4},{8,9},{9,10},{10,1... | collective-permute-start | bytes 3145736 | tf_op jit(solution)/shard_map/ppermute | solution.py:325
  108.5 128.2 %all-gather.12.cloned.1.call-start = ((), (), s32[]{:S(2)}) async-start(), calls=%async_computation.9 | async-start | bytes 7077888 | tf_op jit(solution)/shard_map/all_gather | solution.py:432
  138.1 50.8 %all-to-all-start = ((bf16[4,256,512]{1,2,0:T(8,128)(2,1)}), bf16[4,256,512]{1,2,0:T(8,128)(2,1)S(1)}, u32[]{:S(2)}, u32[]{:S(2)}) async-start(bf16[4,256,512]{1,2,0:T(8,128)(2,1)} %copy.37), calls=%async_computation | async-start | bytes 2097152 | tf_op jit(solution)/shard_map/all_to_all | solution.py:438
  141.7 392.4 %reduce-scatter.5.cloned.1.call-start = ((), (), s32[]{:S(2)}) async-start(), calls=%async_computation.10 | async-start | bytes 7077888 | tf_op jit(solution)/shard_map/reduce_scatter | solution.py:349
  141.7 42.7 %collective-permute-start.10 = (bf16[256,2048]{1,0:T(8,128)(2,1)}, bf16[256,2048]{1,0:T(8,128)(2,1)S(1)}, u32[]{:S(2)}, u32[]{:S(2)}) collective-permute-start(bf16[256,2048]{1,0:T(8,128)(2,1)} %collective-permute-done.9.refs_17_), channel_id=1, source_target_pairs={{0,1},{1,2},{2,3},{3,0},{4,5},{5,6},{6,7},{7,4},{8,9},{9,10},{10,1... | collective-permute-start | bytes 3145736 | tf_op jit(solution)/shard_map/ppermute | solution.py:325
  143.7 45.3 %collective-permute-start.4 = (bf16[256,1536]{1,0:T(8,128)(2,1)}, bf16[256,1536]{1,0:T(8,128)(2,1)}, u32[]{:S(2)}, u32[]{:S(2)}) collective-permute-start(bf16[256,1536]{1,0:T(8,128)(2,1)} %bitcast.62.refs_0_), channel_id=1, source_target_pairs={{0,16},{4,20},{8,24},{12,28},{16,0},{20,4},{24,8},{28,12},{1,17},{... | collective-permute-start | bytes 2359304 | tf_op jit(solution)/shard_map/ppermute | solution.py:354
  145.1 51.1 %collective-permute-start.5 = (bf16[256,1536]{1,0:T(8,128)(2,1)}, bf16[256,1536]{1,0:T(8,128)(2,1)}, u32[]{:S(2)}, u32[]{:S(2)}) collective-permute-start(bf16[256,1536]{1,0:T(8,128)(2,1)} %collective-permute-done.refs_1_), channel_id=1, source_target_pairs={{0,16},{4,20},{8,24},{12,28},{16,0},{20,4},{24,8},{28,12},{1,17},{... | collective-permute-start | bytes 2359304 | tf_op jit(solution)/shard_map/ppermute | solution.py:354
  145.7 50.5 %collective-permute-start.6 = (bf16[256,1536]{1,0:T(8,128)(2,1)}, bf16[256,1536]{1,0:T(8,128)(2,1)}, u32[]{:S(2)}, u32[]{:S(2)}) collective-permute-start(bf16[256,1536]{1,0:T(8,128)(2,1)} %bitcast.61.refs_8_), channel_id=1, source_target_pairs={{0,8},{4,12},{8,0},{12,4},{16,24},{20,28},{24,16},{28,20},{1,9},{5... | collective-permute-start | bytes 2359304 | tf_op jit(solution)/shard_map/ppermute | solution.py:354
  147.1 49.7 %collective-permute-start.7 = (bf16[256,1536]{1,0:T(8,128)(2,1)}, bf16[256,1536]{1,0:T(8,128)(2,1)}, u32[]{:S(2)}, u32[]{:S(2)}) collective-permute-start(bf16[256,1536]{1,0:T(8,128)(2,1)} %collective-permute-done.1.refs_10_), channel_id=1, source_target_pairs={{0,8},{4,12},{8,0},{12,4},{16,24},{20,28},{24,16},{28,20},{1,9},{5... | collective-permute-start | bytes 2359304 | tf_op jit(solution)/shard_map/ppermute | solution.py:354
  235.5 28.1 %collective-permute-start.20 = (bf16[256,2048]{1,0:T(8,128)(2,1)}, bf16[256,2048]{1,0:T(8,128)(2,1)}, u32[]{:S(2)}, u32[]{:S(2)}) collective-permute-start(bf16[256,2048]{1,0:T(8,128)(2,1)} %collective-permute-done.19.refs_16_), channel_id=1, source_target_pairs={{0,1},{1,2},{2,3},{3,0},{4,5},{5,6},{6,7},{7,4},{8,9},{9,10},{10,1... | collective-permute-start | bytes 3145736 | tf_op jit(solution)/shard_map/ppermute | solution.py:325
  235.6 64.2 %collective-permute-start.22 = (bf16[256,2048]{1,0:T(8,128)(2,1)}, bf16[256,2048]{1,0:T(8,128)(2,1)}, u32[]{:S(2)}, u32[]{:S(2)}) collective-permute-start(bf16[256,2048]{1,0:T(8,128)(2,1)} %copy-done.57), channel_id=1, source_target_pairs={{0,1},{1,2},{2,3},{3,0},{4,5},{5,6},{6,7},{7,4},{8,9},{9,10},{10,1... | collective-permute-start | bytes 3145736 | tf_op jit(solution)/shard_map/ppermute | solution.py:325
  263.7 42.9 %collective-permute-start.21 = (bf16[256,2048]{1,0:T(8,128)(2,1)}, bf16[256,2048]{1,0:T(8,128)(2,1)}, u32[]{:S(2)}, u32[]{:S(2)}) collective-permute-start(bf16[256,2048]{1,0:T(8,128)(2,1)} %collective-permute-done.20.refs_16_), channel_id=1, source_target_pairs={{0,1},{1,2},{2,3},{3,0},{4,5},{5,6},{6,7},{7,4},{8,9},{9,10},{10,1... | collective-permute-start | bytes 3145736 | tf_op jit(solution)/shard_map/ppermute | solution.py:325
  337.4 329.6 %reduce-scatter.7.cloned.1.call-start = ((), (), s32[]{:S(2)}) async-start(), calls=%async_computation.11 | async-start | bytes 9437184 | tf_op jit(solution)/shard_map/reduce_scatter | solution.py:349
  456.5 53.0 %all-to-all-start.1 = ((bf16[4,256,512]{2,1,0:T(8,128)(2,1)}), bf16[4,256,512]{2,1,0:T(8,128)(2,1)}, u32[]{:S(2)}, u32[]{:S(2)}) async-start(bf16[4,256,512]{2,1,0:T(8,128)(2,1)} %bitcast.66), calls=%async_computation.1 | async-start | bytes 2097152 | tf_op jit(solution)/shard_map/all_to_all | solution.py:493
  460.8 294.7 %reduce-scatter.9.cloned.1.call-start = ((), (), s32[]{:S(2)}) async-start(), calls=%async_computation.12 | async-start | bytes 4718592 | tf_op jit(solution)/shard_map/reduce_scatter | solution.py:349
  462.8 42.1 %collective-permute-start.26 = (bf16[256,2048]{1,0:T(8,128)(2,1)S(1)}, bf16[256,2048]{1,0:T(8,128)(2,1)}, u32[]{:S(2)}, u32[]{:S(2)}) collective-permute-start(bf16[256,2048]{1,0:T(8,128)(2,1)S(1)} %convert_element_type.239), channel_id=1, source_target_pairs={{0,1},{1,2},{2,3},{3,0},{4,5},{5,6},{6,7},{7,4},{8,9},{9,10},{10,1... | collective-permute-start | bytes 3145736 | tf_op jit(solution)/shard_map/ppermute | solution.py:325
  512.1 104.2 %collective-permute-start.31 = (bf16[512,1536]{1,0:T(8,128)(2,1)}, bf16[512,1536]{1,0:T(8,128)(2,1)}, u32[]{:S(2)}, u32[]{:S(2)}) collective-permute-start(bf16[512,1536]{1,0:T(8,128)(2,1)} %pad_maximum_fusion.1), channel_id=1, source_target_pairs={{0,16},{4,20},{8,24},{12,28},{16,0},{20,4},{24,8},{28,12},{1,17},{... | collective-permute-start | bytes 4718600 | tf_op jit(solution)/shard_map/ppermute | solution.py:354
  543.5 221.5 %reduce-scatter.11.cloned.1.call-start = ((), (), s32[]{:S(2)}) async-start(), calls=%async_computation.13 | async-start | bytes 1310720 | tf_op jit(solution)/shard_map/reduce_scatter | solution.py:560
  558.2 105.9 %collective-permute-start.32 = (bf16[512,1536]{1,0:T(8,128)(2,1)S(1)}, bf16[512,1536]{1,0:T(8,128)(2,1)S(1)}, u32[]{:S(2)}, u32[]{:S(2)}) collective-permute-start(bf16[512,1536]{1,0:T(8,128)(2,1)S(1)} %pad_maximum_fusion.2), channel_id=1, source_target_pairs={{0,8},{4,12},{8,0},{12,4},{16,24},{20,28},{24,16},{28,20},{1,9},{5... | collective-permute-start | bytes 4718600 | tf_op jit(solution)/shard_map/ppermute | solution.py:354
  559.3 53.1 %collective-permute-start.35 = (f32[34,128]{1,0:T(8,128)S(1)}, f32[34,128]{1,0:T(8,128)S(1)}, u32[]{:S(2)}, u32[]{:S(2)}) collective-permute-start(f32[34,128]{1,0:T(8,128)S(1)} %fusion.75), channel_id=1, source_target_pairs={{0,8},{4,12},{8,0},{12,4},{16,24},{20,28},{24,16},{28,20},{1,9},{5... | collective-permute-start | bytes 52232 | tf_op jit(solution)/shard_map/ppermute | solution.py:383
  614.1 52.8 %collective-permute-start.30 = (bf16[256,2048]{1,0:T(8,128)(2,1)S(1)}, bf16[256,2048]{1,0:T(8,128)(2,1)}, u32[]{:S(2)}, u32[]{:S(2)}) collective-permute-start(bf16[256,2048]{1,0:T(8,128)(2,1)S(1)} %add_convert_fusion.6), channel_id=1, source_target_pairs={{0,1},{1,2},{2,3},{3,0},{4,5},{5,6},{6,7},{7,4},{8,9},{9,10},{10,1... | collective-permute-start | bytes 3145736 | tf_op jit(solution)/shard_map/ppermute | solution.py:325
  614.2 52.7 %collective-permute-start.29 = (bf16[256,2048]{1,0:T(8,128)(2,1)S(1)}, bf16[256,2048]{1,0:T(8,128)(2,1)}, u32[]{:S(2)}, u32[]{:S(2)}) collective-permute-start(bf16[256,2048]{1,0:T(8,128)(2,1)S(1)} %get-tuple-element.291), channel_id=1, source_target_pairs={{0,1},{1,2},{2,3},{3,0},{4,5},{5,6},{6,7},{7,4},{8,9},{9,10},{10,1... | collective-permute-start | bytes 3145736 | tf_op jit(solution)/shard_map/ppermute | solution.py:325
  616.2 46.0 %collective-permute-start.37 = (f32[34,128]{1,0:T(8,128)S(1)}, f32[34,128]{1,0:T(8,128)S(1)}, u32[]{:S(2)}, u32[]{:S(2)}) collective-permute-start(f32[34,128]{1,0:T(8,128)S(1)} %add.255), channel_id=1, source_target_pairs={{0,1},{1,0},{2,3},{3,2},{4,5},{5,4},{6,7},{7,6},{8,9},{9,8},{10,11... | collective-permute-start | bytes 52232 | tf_op jit(solution)/shard_map/ppermute | solution.py:383
  670.0 27.9 %collective-permute-start.33 = (bf16[256,2048]{1,0:T(8,128)(2,1)S(1)}, bf16[256,2048]{1,0:T(8,128)(2,1)S(1)}, u32[]{:S(2)}, u32[]{:S(2)}) collective-permute-start(bf16[256,2048]{1,0:T(8,128)(2,1)S(1)} %add_convert_fusion.5), channel_id=1, source_target_pairs={{0,1},{1,2},{2,3},{3,0},{4,5},{5,6},{6,7},{7,4},{8,9},{9,10},{10,1... | collective-permute-start | bytes 3145736 | tf_op jit(solution)/shard_map/ppermute | solution.py:325
  673.2 43.0 %collective-permute-start.39 = (bf16[256,2048]{1,0:T(8,128)(2,1)S(1)}, bf16[256,2048]{1,0:T(8,128)(2,1)}, u32[]{:S(2)}, u32[]{:S(2)}) collective-permute-start(bf16[256,2048]{1,0:T(8,128)(2,1)S(1)} %add_convert_fusion.4), channel_id=1, source_target_pairs={{0,1},{1,2},{2,3},{3,0},{4,5},{5,6},{6,7},{7,4},{8,9},{9,10},{10,1... | collective-permute-start | bytes 3145736 | tf_op jit(solution)/shard_map/ppermute | solution.py:325
  717.5 38.0 %collective-permute-start.42 = (bf16[256,2048]{1,0:T(8,128)(2,1)}, bf16[256,2048]{1,0:T(8,128)(2,1)}, u32[]{:S(2)}, u32[]{:S(2)}) collective-permute-start(bf16[256,2048]{1,0:T(8,128)(2,1)} %add_convert_fusion.2), channel_id=1, source_target_pairs={{0,1},{1,2},{2,3},{3,0},{4,5},{5,6},{6,7},{7,4},{8,9},{9,10},{10,1... | collective-permute-start | bytes 3145736 | tf_op jit(solution)/shard_map/ppermute | solution.py:325
  (80 other events, 947.1 us)
Sparse Core Ops, SparseCore 0:
  10.5 45.2 all-gather.5
  57.3 34.5 all-gather.7
  108.7 67.7 all-gather.9
  178.2 50.4 all-gather.11
  337.5 59.0 reduce-scatter.4
  437.2 69.6 reduce-scatter.6
  543.6 65.0 reduce-scatter.8
  720.2 38.2 reduce-scatter.10

commit v4 on v3

--- a/solution.py
+++ b/solution.py
@@ -424,7 +424,6 @@
         qkv = lax.dynamic_update_slice(qkv, dot(normed, w_qkv), at)
         if k == 1:
             xs[2] = double(xs[2])
-            qkv, normed_full, xs[2] = barrier((qkv, normed_full, xs[2]))
         if k == parts - 2:
             qkv, normed_full, xs[-1], output_w = barrier((qkv, normed_full, xs[-1], output_w))
             output_w = lax.all_gather(output_w, "dp", axis=1, tiled=True)
@@ -524,42 +523,37 @@
     moves = [down_move, held]
 
     def first_filler():
-        return part_qkv, moves, summed_output
+        return part_qkv, [moves[0], summed_output]
 
     def second_filler():
         return gain_filler(), moves
 
-    def step_moves(last):
-        at = len(moves_done) + 1
-        moves_done.append(last)
-        down_move, held = last
-        if 2 + at < parts:
-            down_move = around((late[2 + at] + down_move.astype(F32)).astype(BF16))
-        if at < bits - 1:
-            held = [halve(held[0], bits - 1 - at), halve(held[1], 1 + at)]
-        return [down_move, held]
-
-    moves_done, tied = [], []
-
-    def filler(make):
-        def run():
-            nonlocal moves
-            if tied:
-                moves = step_moves(tied[-1])
-            return make()
-
-        return run
-
-    grad_pre_in, made = scatter_ring(lambda k: grads_in[k], (filler(first_filler), filler(second_filler)), tied)
-    _, _, summed_output = made[0]
-    gain_sums, (down_move, held) = made[1]
-    for at in range(len(moves_done) + 1, max(bits - 1, parts - 2)):
-        down_move, held = step_moves([down_move, held])
+    def down_step(k, down_move):
+        return around((late[k] + down_move.astype(F32)).astype(BF16)) if k < parts else down_move
+
+    def first_step(tied):
+        down_move, summed = tied
+        moves[0] = down_step(3, down_move)
+        blocks = lax.all_to_all(
+            summed.reshape(parts, summed.shape[0] // parts, summed.shape[1]), "tensor", 0, 0, tiled=True
+        )
+        moves.append(blocks)
+
+    tied = []
+
+    def late_filler():
+        first_step(tied[0])
+        return second_filler()
+
+    grad_pre_in, made = scatter_ring(lambda k: grads_in[k], (first_filler, late_filler), tied)
+    gain_sums, (down_move, held, blocks) = made[1]
+    for k in range(4, parts):
+        down_move = down_step(k, down_move)
+    for at in range(1, bits - 1):
+        held = [halve(held[0], bits - 1 - at), halve(held[1], 1 + at)]
+    summed_output = jnp.sum(blocks.astype(F32), axis=0)
     summed_gate, summed_up = (h[0] for h in held)
     layer_out = (resid + late[0] + down_move.astype(F32)).astype(BF16)
-    summed_output = lax.psum_scatter(
-        summed_output, "tensor", scatter_dimension=0, tiled=True
-    ).astype(F32)
     summed_qkv = scattered(part_qkv, 0).astype(F32)
     scale_pre = normals[0][1]
     back_pre = rms_back(inputs_wide * scale_pre, scale_pre, pre_full, grad_pre_in)

time: 782 us -> 740 us (0.946)
  waiting for transfers between devices: 415 us -> 359 us
  starting transfers between devices: 40.1 us -> 48.2 us
    ppermute x18, waiting for transfers between devices: 275 us -> 205 us  [around(): return lax.ppermute(block, 'tensor', ring)]
    all_gather x1, waiting for transfers between devices: 13.8 us -> 25.4 us  [on_device(): output_w = lax.all_gather(w_output, 'tensor', axis=0, tiled=True)]
  transfers between devices with their start and end apart: 53 -> 53, of which waited for: 27 -> 23; matrix products, arithmetic and copies ran while one was open for 21% -> 23% of each run, Pallas kernels for 12% -> 12%
where the time goes in v4:
time: 740 us; the launch traced here: 732 us
  waiting for transfers between devices  359 us (49%)
  Pallas kernels  109 us (15%)
  matrix products  84.2 us (11%)
  other arithmetic  71.1 us (10%)
  starting transfers between devices  48.2 us (7%)
  local copies, waits for them, and re-layouts  35.5 us (5%)
  between operations  15.1 us (2%)
  blocking collectives  10.4 us (1%)
    ppermute x18, waiting for transfers between devices, around(): return lax.ppermute(block, 'tensor', ring)  205 us
    ppermute x5, waiting for transfers between devices, butterfly(): lax.ppermute(values, axis, [(i, i ^ 1 << bit) for i in range(size)])  102 us
    pallas_call x4, Pallas kernels, hidden_piece(): pl.pallas_call(functools.partial(hidden_kernel, blocks), grid=(units // t...  71.9 us
    dot_general x7, matrix products, contract_rows(): lax.dot_general(left, right, (((0,), (0,)), ((), ())), preferred_element_...  46.4 us
    all_gather x1, waiting for transfers between devices, on_device(): output_w = lax.all_gather(w_output, 'tensor', axis=0, tiled=True)  25.4 us
    dot_general x5, matrix products, dot(): return jnp.dot(left, right, preferred_element_type=F32)  19 us
    dot_general x5, matrix products, contract_cols(): lax.dot_general(left, right, (((1,), (1,)), ((), ())), preferred_element_...  18.9 us
    pallas_call x1, Pallas kernels, backward_heads(): pl.pallas_call(functools.partial(attention_backward, group, size, heads,...  18.7 us
  transfers between devices with their start and end apart: 53, of which 23 were waited for; matrix products, arithmetic and copies ran while one was open for 23% of the time, Pallas kernels for 12%

profile of v4, /device:TPU:0, one launch (start us, length us, event | category | flops | bytes accessed | tf_op | source)
XLA Modules:
  0.0 732.0 jit_solution(13370951332787155352)
XLA Ops:
  23.4 14.5 %collective-permute-done.2 = bf16[256,2048]{1,0:T(8,128)(2,1)} collective-permute-done((bf16[256,2048]{1,0:T(8,128)(2,1)}, bf16[256,2048]{1,0:T(8,128)(2,1)}, u32[]{:S(2)}, u32[]{:S(2)}) %collective-permute-start.2) | collective-permute-done | bytes 1048608 | tf_op jit(solution)/shard_map/ppermute | solution.py:325
  38.0 10.4 %all-gather = bf16[8,1,640]{2,1,0:T(2,128)(2,1)S(1)} all-gather(bf16[1,1,640]{2,1,0:T(2,128)(2,1)S(1)} %bitcast.89), channel_id=1, replica_groups=mesh['dp'=8,'tensor'=4] {'dp'}, dimensions={0}, use_global_device_ids=true | all-gather | bytes 11520 | tf_op jit(solution)/shard_map/all_gather | solution.py:406
  56.4 7.9 %collective-permute-done.3 = bf16[256,2048]{1,0:T(8,128)(2,1)S(1)} collective-permute-done((bf16[256,2048]{1,0:T(8,128)(2,1)}, bf16[256,2048]{1,0:T(8,128)(2,1)S(1)}, u32[]{:S(2)}, u32[]{:S(2)}) %collective-permute-start.3) | collective-permute-done | bytes 1048608 | tf_op jit(solution)/shard_map/ppermute | solution.py:325
  77.9 25.4 %all-gather.8.cloned.1.call-done = bf16[2048,256]{1,0:T(8,128)(2,1)} async-done(((bf16[512,256]{1,0:T(8,128)(2,1)}), bf16[2048,256]{1,0:T(8,128)(2,1)}) %all-gather.8.cloned.1.call-update) | async-done | bytes 1048592 | tf_op jit(solution)/shard_map/all_gather | solution.py:405
  113.9 11.2 %attention_forward.1 = (bf16[1024,512]{1,0:T(8,128)(2,1)}, f32[2,2,1024]{2,1,0:T(2,128)}) custom-call(f32[1024,1024]{1,0:T(8,128)} %convolution_dynamic-update-slice_fusion.q_ref.k_ref.v_ref, f32[1024,1024]{1,0:T(8,128)} %convolution_dynamic-update-slice_fusion.q_ref.k_ref.v_ref, f32[1024,1024]{1,0:T(8,128)} %convolution_dynamic-update-slice_fusion.q_ref.k_ref.v_ref, ...), custom_call_target="tpu_custom_call" | custom-call | flops 2147483648 | bytes 5242880 | tf_op jit(solution)/shard_map/attention_forward/pallas_call | solution.py:240
  125.0 7.9 %collective-permute-done.9.refs_17_ = bf16[256,2048]{1,0:T(8,128)(2,1)S(1)} collective-permute-done((bf16[256,2048]{1,0:T(8,128)(2,1)}, bf16[256,2048]{1,0:T(8,128)(2,1)S(1)}, u32[]{:S(2)}, u32[]{:S(2)}) %collective-permute-start.9) | collective-permute-done | bytes 1048608 | tf_op jit(solution)/shard_map/ppermute | solution.py:325
  145.7 34.7 %collective-permute-done.10.refs_17_ = bf16[256,2048]{1,0:T(8,128)(2,1)S(1)} collective-permute-done((bf16[256,2048]{1,0:T(8,128)(2,1)}, bf16[256,2048]{1,0:T(8,128)(2,1)S(1)}, u32[]{:S(2)}, u32[]{:S(2)}) %collective-permute-start.10) | collective-permute-done | bytes 1048608 | tf_op jit(solution)/shard_map/ppermute | solution.py:325
  185.0 6.2 collective-permute-done.5.refs_3_
  193.1 6.2 multiply_reduce_fusion.2
  206.1 24.7 %collective-permute-done.19.refs_16_ = bf16[256,2048]{1,0:T(8,128)(2,1)} collective-permute-done((bf16[256,2048]{1,0:T(8,128)(2,1)}, bf16[256,2048]{1,0:T(8,128)(2,1)}, u32[]{:S(2)}, u32[]{:S(2)}) %collective-permute-start.19) | collective-permute-done | bytes 1048608 | tf_op jit(solution)/shard_map/ppermute | solution.py:325
  232.0 18.0 %hidden_piece.4 = (bf16[256,1536]{1,0:T(8,128)(2,1)}, bf16[256,1536]{1,0:T(8,128)(2,1)}, bf16[256,1536]{1,0:T(8,128)(2,1)}, f32[256,2048]{1,0:T(8,128)}, f32[256,2048]{1,0:T(8,128)}) custom-call(bf16[256,1536]{1,0:T(8,128)(2,1)} %bitcast.65.refs_0_, bf16[256,1536]{1,0:T(8,128)(2,1)} %collective-permute-done.refs_1_, ...), custom_call_target="tpu_custom_call" | custom-call | flops 9663676416 | bytes 27525120 | tf_op jit(solution)/shard_map/hidden_piece/pallas_call | solution.py:187
  249.9 9.0 %collective-permute-done.20.refs_16_ = bf16[256,2048]{1,0:T(8,128)(2,1)} collective-permute-done((bf16[256,2048]{1,0:T(8,128)(2,1)}, bf16[256,2048]{1,0:T(8,128)(2,1)}, u32[]{:S(2)}, u32[]{:S(2)}) %collective-permute-start.20) | collective-permute-done | bytes 1048608 | tf_op jit(solution)/shard_map/ppermute | solution.py:325
  259.1 17.8 %hidden_piece.5 = (bf16[256,1536]{1,0:T(8,128)(2,1)}, bf16[256,1536]{1,0:T(8,128)(2,1)}, bf16[256,1536]{1,0:T(8,128)(2,1)}, f32[256,2048]{1,0:T(8,128)}, f32[256,2048]{1,0:T(8,128)}) custom-call(bf16[256,1536]{1,0:T(8,128)(2,1)} %bitcast.65.refs_0_, bf16[256,1536]{1,0:T(8,128)(2,1)} %collective-permute-done.refs_1_, ...), custom_call_target="tpu_custom_call" | custom-call | flops 9663676416 | bytes 27525120 | tf_op jit(solution)/shard_map/hidden_piece/pallas_call | solution.py:187
  276.9 17.9 %hidden_piece.6 = (bf16[256,1536]{1,0:T(8,128)(2,1)}, bf16[256,1536]{1,0:T(8,128)(2,1)}, bf16[256,1536]{1,0:T(8,128)(2,1)}, f32[256,2048]{1,0:T(8,128)}, f32[256,2048]{1,0:T(8,128)}) custom-call(bf16[256,1536]{1,0:T(8,128)(2,1)} %bitcast.65.refs_0_, bf16[256,1536]{1,0:T(8,128)(2,1)} %collective-permute-done.refs_1_, ...), custom_call_target="tpu_custom_call" | custom-call | flops 9663676416 | bytes 27525120 | tf_op jit(solution)/shard_map/hidden_piece/pallas_call | solution.py:187
  294.8 7.2 collective-permute-done.21.refs_16_
  302.0 18.2 %hidden_piece.7 = (bf16[256,1536]{1,0:T(8,128)(2,1)}, bf16[256,1536]{1,0:T(8,128)(2,1)}, bf16[256,1536]{1,0:T(8,128)(2,1)}, f32[256,2048]{1,0:T(8,128)}, f32[256,2048]{1,0:T(8,128)}) custom-call(bf16[256,1536]{1,0:T(8,128)(2,1)} %bitcast.65.refs_0_, bf16[256,1536]{1,0:T(8,128)(2,1)} %collective-permute-done.refs_1_, ...), custom_call_target="tpu_custom_call" | custom-call | flops 9663676416 | bytes 27525120 | tf_op jit(solution)/shard_map/hidden_piece/pallas_call | solution.py:187
  320.3 12.5 %convolution_convert_fusion.1 = bf16[1536,2048]{1,0:T(8,128)(2,1)} fusion(bf16[256,2048]{1,0:T(8,128)(2,1)} %collective-permute-done.22.refs_17_, bf16[256,2048]{1,0:T(8,128)(2,1)} %copy-done.55, bf16[256,2048]{1,0:T(8,128)(2,1)} %copy-done.54, bf16[256,2048]{1,0:T(8,128)(2,1)} %refs_17_.1, bf16[256,1536]{1,0:T(8,128)(2,1)} %get-tuple-element.183, ...), kind=kOutput, calls=%fused_computation.2 | convolution fusion | flops 6474956800 | bytes 13631488 | tf_op jit(solution)/shard_map/dot_general | solution.py:29
  334.9 25.1 %collective-permute-done.23 = bf16[256,2048]{1,0:T(8,128)(2,1)S(1)} collective-permute-done((bf16[256,2048]{1,0:T(8,128)(2,1)S(1)}, bf16[256,2048]{1,0:T(8,128)(2,1)S(1)}, u32[]{:S(2)}, u32[]{:S(2)}) %collective-permute-start.23) | collective-permute-done | bytes 1048608 | tf_op jit(solution)/shard_map/ppermute | solution.py:325
  360.4 24.3 %collective-permute-done.24 = bf16[256,2048]{1,0:T(8,128)(2,1)S(1)} collective-permute-done((bf16[256,2048]{1,0:T(8,128)(2,1)S(1)}, bf16[256,2048]{1,0:T(8,128)(2,1)S(1)}, u32[]{:S(2)}, u32[]{:S(2)}) %collective-permute-start.24) | collective-permute-done | bytes 1048608 | tf_op jit(solution)/shard_map/ppermute | solution.py:325
  387.3 22.6 %collective-permute-done.25 = bf16[256,2048]{1,0:T(8,128)(2,1)} collective-permute-done((bf16[256,2048]{1,0:T(8,128)(2,1)}, bf16[256,2048]{1,0:T(8,128)(2,1)}, u32[]{:S(2)}, u32[]{:S(2)}) %collective-permute-start.25) | collective-permute-done | bytes 1048608 | tf_op jit(solution)/shard_map/ppermute | solution.py:325
  420.3 5.7 convolution_convert_fusion.7
  427.7 5.6 convolution_convert_fusion
  441.2 4.9 convolution_convert_fusion.4
  446.2 4.8 convolution_convert_fusion.2
  461.3 5.4 convolution_convert_fusion.5
  479.7 21.6 %collective-permute-done.26 = bf16[256,2048]{1,0:T(8,128)(2,1)} collective-permute-done((bf16[256,2048]{1,0:T(8,128)(2,1)S(1)}, bf16[256,2048]{1,0:T(8,128)(2,1)}, u32[]{:S(2)}, u32[]{:S(2)}) %collective-permute-start.26) | collective-permute-done | bytes 1048608 | tf_op jit(solution)/shard_map/ppermute | solution.py:325
  509.0 18.7 %attention_backward.1 = (bf16[1024,1024]{1,0:T(8,128)(2,1)}, f32[2,128]{1,0:T(2,128)}) custom-call(f32[1024,1024]{1,0:T(8,128)} %convolution_dynamic-update-slice_fusion.q_ref.k_ref.v_ref, f32[1024,1024]{1,0:T(8,128)} %convolution_dynamic-update-slice_fusion.q_ref.k_ref.v_ref, f32[1024,1024]{1,0:T(8,128)} %convolution_dynamic-update-slice_fusion.q_ref.k_ref.v_ref, ...), custom_call_target="tpu_custom_call" | custom-call | flops 5368709120 | bytes 7340032 | tf_op jit(solution)/shard_map/attention_backward/pallas_call | solution.py:266
  528.5 9.4 %convolution_convert_fusion.6 = bf16[2048,1024]{1,0:T(8,128)(2,1)} fusion(bf16[1024,2048]{1,0:T(8,128)(2,1)} %fusion.61, bf16[1024,1024]{1,0:T(8,128)(2,1)} %get-tuple-element.204), kind=kOutput, calls=%fused_computation.17 | convolution fusion | flops 4297064448 | bytes 10485760 | tf_op jit(solution)/shard_map/dot_general | solution.py:29
  538.5 5.1 fusion.29
  562.2 49.1 %collective-permute-done.34 = f32[34,128]{1,0:T(8,128)S(1)} collective-permute-done((f32[34,128]{1,0:T(8,128)S(1)}, f32[34,128]{1,0:T(8,128)S(1)}, u32[]{:S(2)}, u32[]{:S(2)}) %collective-permute-start.34) | collective-permute-done | bytes 17440 | tf_op jit(solution)/shard_map/ppermute | solution.py:383
  635.1 52.2 %collective-permute-done.36 = f32[34,128]{1,0:T(8,128)S(1)} collective-permute-done((f32[34,128]{1,0:T(8,128)S(1)}, f32[34,128]{1,0:T(8,128)S(1)}, u32[]{:S(2)}, u32[]{:S(2)}) %collective-permute-start.36) | collective-permute-done | bytes 17440 | tf_op jit(solution)/shard_map/ppermute | solution.py:383
  700.8 6.3 collective-permute-done.42
  (310 shorter events, 206.4 us)
Async XLA Ops:
  7.2 58.8 %all-gather.6.cloned.1.call-start = ((), (), s32[]{:S(2)}) async-start(), calls=%async_computation.6 | async-start | bytes 4718592 | tf_op jit(solution)/shard_map/all_gather | solution.py:390
  9.3 93.9 %all-gather.8.cloned.1.call-start = ((), (), s32[]{:S(2)}) async-start(), calls=%async_computation.7 | async-start | bytes 1310720 | tf_op jit(solution)/shard_map/all_gather | solution.py:405
  9.4 28.6 %collective-permute-start.2 = (bf16[256,2048]{1,0:T(8,128)(2,1)}, bf16[256,2048]{1,0:T(8,128)(2,1)}, u32[]{:S(2)}, u32[]{:S(2)}) collective-permute-start(bf16[256,2048]{1,0:T(8,128)(2,1)} %param.14), channel_id=1, source_target_pairs={{0,1},{1,2},{2,3},{3,0},{4,5},{5,6},{6,7},{7,4},{8,9},{9,10},{10,1... | collective-permute-start | bytes 3145736 | tf_op jit(solution)/shard_map/ppermute | solution.py:325
  15.7 40.6 %collective-permute-start = (bf16[256,1536]{1,0:T(8,128)(2,1)}, bf16[256,1536]{1,0:T(8,128)(2,1)}, u32[]{:S(2)}, u32[]{:S(2)}) collective-permute-start(bf16[256,1536]{1,0:T(8,128)(2,1)} %bitcast.65.refs_0_), channel_id=1, source_target_pairs={{0,8},{4,12},{8,0},{12,4},{16,24},{20,28},{24,16},{28,20},{1,9},{5... | collective-permute-start | bytes 2359304 | tf_op jit(solution)/shard_map/ppermute | solution.py:354
  18.2 38.2 %collective-permute-start.1 = (bf16[256,1536]{1,0:T(8,128)(2,1)}, bf16[256,1536]{1,0:T(8,128)(2,1)}, u32[]{:S(2)}, u32[]{:S(2)}) collective-permute-start(bf16[256,1536]{1,0:T(8,128)(2,1)} %bitcast.64.refs_8_), channel_id=1, source_target_pairs={{0,16},{4,20},{8,24},{12,28},{16,0},{20,4},{24,8},{28,12},{1,17},{... | collective-permute-start | bytes 2359304 | tf_op jit(solution)/shard_map/ppermute | solution.py:354
  48.4 144.7 %all-gather.10.cloned.1.call-start = ((), (), s32[]{:S(2)}) async-start(), calls=%async_computation.8 | async-start | bytes 9437184 | tf_op jit(solution)/shard_map/all_gather | solution.py:429
  64.6 42.3 %collective-permute-start.8 = (bf16[256,2048]{1,0:T(8,128)(2,1)S(1)}, bf16[256,2048]{1,0:T(8,128)(2,1)S(1)}, u32[]{:S(2)}, u32[]{:S(2)}) collective-permute-start(bf16[256,2048]{1,0:T(8,128)(2,1)S(1)} %collective-permute-done.3), channel_id=1, source_target_pairs={{0,1},{1,2},{2,3},{3,0},{4,5},{5,6},{6,7},{7,4},{8,9},{9,10},{10,1... | collective-permute-start | bytes 3145736 | tf_op jit(solution)/shard_map/ppermute | solution.py:325
  106.9 125.1 %all-gather.12.cloned.1.call-start = ((), (), s32[]{:S(2)}) async-start(), calls=%async_computation.9 | async-start | bytes 7077888 | tf_op jit(solution)/shard_map/all_gather | solution.py:431
  135.6 49.4 %all-to-all-start = ((bf16[4,256,512]{1,2,0:T(8,128)(2,1)}), bf16[4,256,512]{1,2,0:T(8,128)(2,1)S(1)}, u32[]{:S(2)}, u32[]{:S(2)}) async-start(bf16[4,256,512]{1,2,0:T(8,128)(2,1)} %copy.37), calls=%async_computation | async-start | bytes 2097152 | tf_op jit(solution)/shard_map/all_to_all | solution.py:437
  139.1 389.4 %reduce-scatter.4.cloned.1.call-start = ((), (), s32[]{:S(2)}) async-start(), calls=%async_computation.10 | async-start | bytes 7077888 | tf_op jit(solution)/shard_map/reduce_scatter | solution.py:349
  139.2 41.2 %collective-permute-start.10 = (bf16[256,2048]{1,0:T(8,128)(2,1)}, bf16[256,2048]{1,0:T(8,128)(2,1)S(1)}, u32[]{:S(2)}, u32[]{:S(2)}) collective-permute-start(bf16[256,2048]{1,0:T(8,128)(2,1)} %copy-done.54), channel_id=1, source_target_pairs={{0,1},{1,2},{2,3},{3,0},{4,5},{5,6},{6,7},{7,4},{8,9},{9,10},{10,1... | collective-permute-start | bytes 3145736 | tf_op jit(solution)/shard_map/ppermute | solution.py:325
  141.1 43.9 %collective-permute-start.4 = (bf16[256,1536]{1,0:T(8,128)(2,1)}, bf16[256,1536]{1,0:T(8,128)(2,1)}, u32[]{:S(2)}, u32[]{:S(2)}) collective-permute-start(bf16[256,1536]{1,0:T(8,128)(2,1)} %bitcast.65.refs_0_), channel_id=1, source_target_pairs={{0,16},{4,20},{8,24},{12,28},{16,0},{20,4},{24,8},{28,12},{1,17},{... | collective-permute-start | bytes 2359304 | tf_op jit(solution)/shard_map/ppermute | solution.py:354
  142.0 49.2 %collective-permute-start.5 = (bf16[256,1536]{1,0:T(8,128)(2,1)}, bf16[256,1536]{1,0:T(8,128)(2,1)}, u32[]{:S(2)}, u32[]{:S(2)}) collective-permute-start(bf16[256,1536]{1,0:T(8,128)(2,1)} %collective-permute-done.refs_1_), channel_id=1, source_target_pairs={{0,16},{4,20},{8,24},{12,28},{16,0},{20,4},{24,8},{28,12},{1,17},{... | collective-permute-start | bytes 2359304 | tf_op jit(solution)/shard_map/ppermute | solution.py:354
  143.1 48.1 %collective-permute-start.6 = (bf16[256,1536]{1,0:T(8,128)(2,1)}, bf16[256,1536]{1,0:T(8,128)(2,1)}, u32[]{:S(2)}, u32[]{:S(2)}) collective-permute-start(bf16[256,1536]{1,0:T(8,128)(2,1)} %bitcast.64.refs_8_), channel_id=1, source_target_pairs={{0,8},{4,12},{8,0},{12,4},{16,24},{20,28},{24,16},{28,20},{1,9},{5... | collective-permute-start | bytes 2359304 | tf_op jit(solution)/shard_map/ppermute | solution.py:354
  144.0 48.1 %collective-permute-start.7 = (bf16[256,1536]{1,0:T(8,128)(2,1)}, bf16[256,1536]{1,0:T(8,128)(2,1)}, u32[]{:S(2)}, u32[]{:S(2)}) collective-permute-start(bf16[256,1536]{1,0:T(8,128)(2,1)} %collective-permute-done.1.refs_10_), channel_id=1, source_target_pairs={{0,8},{4,12},{8,0},{12,4},{16,24},{20,28},{24,16},{28,20},{1,9},{5... | collective-permute-start | bytes 2359304 | tf_op jit(solution)/shard_map/ppermute | solution.py:354
  203.6 27.2 %collective-permute-start.19 = (bf16[256,2048]{1,0:T(8,128)(2,1)}, bf16[256,2048]{1,0:T(8,128)(2,1)}, u32[]{:S(2)}, u32[]{:S(2)}) collective-permute-start(bf16[256,2048]{1,0:T(8,128)(2,1)} %shuffled.2.refs_16_), channel_id=1, source_target_pairs={{0,1},{1,2},{2,3},{3,0},{4,5},{5,6},{6,7},{7,4},{8,9},{9,10},{10,1... | collective-permute-start | bytes 3145736 | tf_op jit(solution)/shard_map/ppermute | solution.py:325
  230.8 28.1 %collective-permute-start.20 = (bf16[256,2048]{1,0:T(8,128)(2,1)}, bf16[256,2048]{1,0:T(8,128)(2,1)}, u32[]{:S(2)}, u32[]{:S(2)}) collective-permute-start(bf16[256,2048]{1,0:T(8,128)(2,1)} %collective-permute-done.19.refs_16_), channel_id=1, source_target_pairs={{0,1},{1,2},{2,3},{3,0},{4,5},{5,6},{6,7},{7,4},{8,9},{9,10},{10,1... | collective-permute-start | bytes 3145736 | tf_op jit(solution)/shard_map/ppermute | solution.py:325
  230.8 64.1 %collective-permute-start.22 = (bf16[256,2048]{1,0:T(8,128)(2,1)}, bf16[256,2048]{1,0:T(8,128)(2,1)}, u32[]{:S(2)}, u32[]{:S(2)}) collective-permute-start(bf16[256,2048]{1,0:T(8,128)(2,1)} %copy-done.55), channel_id=1, source_target_pairs={{0,1},{1,2},{2,3},{3,0},{4,5},{5,6},{6,7},{7,4},{8,9},{9,10},{10,1... | collective-permute-start | bytes 3145736 | tf_op jit(solution)/shard_map/ppermute | solution.py:325
  258.9 43.1 %collective-permute-start.21 = (bf16[256,2048]{1,0:T(8,128)(2,1)}, bf16[256,2048]{1,0:T(8,128)(2,1)}, u32[]{:S(2)}, u32[]{:S(2)}) collective-permute-start(bf16[256,2048]{1,0:T(8,128)(2,1)} %collective-permute-done.20.refs_16_), channel_id=1, source_target_pairs={{0,1},{1,2},{2,3},{3,0},{4,5},{5,6},{6,7},{7,4},{8,9},{9,10},{10,1... | collective-permute-start | bytes 3145736 | tf_op jit(solution)/shard_map/ppermute | solution.py:325
  332.8 278.5 %reduce-scatter.6.cloned.1.call-start = ((), (), s32[]{:S(2)}) async-start(), calls=%async_computation.11 | async-start | bytes 9437184 | tf_op jit(solution)/shard_map/reduce_scatter | solution.py:349
  452.9 53.0 %all-to-all-start.1 = ((bf16[4,256,512]{2,1,0:T(8,128)(2,1)}), bf16[4,256,512]{2,1,0:T(8,128)(2,1)}, u32[]{:S(2)}, u32[]{:S(2)}) async-start(bf16[4,256,512]{2,1,0:T(8,128)(2,1)} %bitcast.69), calls=%async_computation.1 | async-start | bytes 2097152 | tf_op jit(solution)/shard_map/all_to_all | solution.py:492
  457.2 239.9 %reduce-scatter.8.cloned.1.call-start = ((), (), s32[]{:S(2)}) async-start(), calls=%async_computation.12 | async-start | bytes 4718592 | tf_op jit(solution)/shard_map/reduce_scatter | solution.py:349
  459.1 42.2 %collective-permute-start.26 = (bf16[256,2048]{1,0:T(8,128)(2,1)S(1)}, bf16[256,2048]{1,0:T(8,128)(2,1)}, u32[]{:S(2)}, u32[]{:S(2)}) collective-permute-start(bf16[256,2048]{1,0:T(8,128)(2,1)S(1)} %convert_element_type.239), channel_id=1, source_target_pairs={{0,1},{1,2},{2,3},{3,0},{4,5},{5,6},{6,7},{7,4},{8,9},{9,10},{10,1... | collective-permute-start | bytes 3145736 | tf_op jit(solution)/shard_map/ppermute | solution.py:325
  509.0 102.4 %collective-permute-start.30 = (bf16[256,2048]{1,0:T(8,128)(2,1)}, bf16[256,2048]{1,0:T(8,128)(2,1)}, u32[]{:S(2)}, u32[]{:S(2)}) collective-permute-start(bf16[256,2048]{1,0:T(8,128)(2,1)} %add_convert_fusion.6), channel_id=1, source_target_pairs={{0,1},{1,2},{2,3},{3,0},{4,5},{5,6},{6,7},{7,4},{8,9},{9,10},{10,1... | collective-permute-start | bytes 3145736 | tf_op jit(solution)/shard_map/ppermute | solution.py:325
  543.6 67.7 %collective-permute-start.29 = (bf16[256,2048]{1,0:T(8,128)(2,1)}, bf16[256,2048]{1,0:T(8,128)(2,1)}, u32[]{:S(2)}, u32[]{:S(2)}) collective-permute-start(bf16[256,2048]{1,0:T(8,128)(2,1)} %get-tuple-element.283), channel_id=1, source_target_pairs={{0,1},{1,2},{2,3},{3,0},{4,5},{5,6},{6,7},{7,4},{8,9},{9,10},{10,1... | collective-permute-start | bytes 3145736 | tf_op jit(solution)/shard_map/ppermute | solution.py:325
  557.7 67.8 %collective-permute-start.38 = (bf16[512,1536]{1,0:T(8,128)(2,1)}, bf16[512,1536]{1,0:T(8,128)(2,1)}, u32[]{:S(2)}, u32[]{:S(2)}) collective-permute-start(bf16[512,1536]{1,0:T(8,128)(2,1)} %pad_maximum_fusion.1), channel_id=1, source_target_pairs={{0,16},{4,20},{8,24},{12,28},{16,0},{20,4},{24,8},{28,12},{1,17},{... | collective-permute-start | bytes 4718600 | tf_op jit(solution)/shard_map/ppermute | solution.py:354
  558.7 52.6 %collective-permute-start.34 = (f32[34,128]{1,0:T(8,128)S(1)}, f32[34,128]{1,0:T(8,128)S(1)}, u32[]{:S(2)}, u32[]{:S(2)}) collective-permute-start(f32[34,128]{1,0:T(8,128)S(1)} %fusion.106), channel_id=1, source_target_pairs={{0,16},{4,20},{8,24},{12,28},{16,0},{20,4},{24,8},{28,12},{1,17},{... | collective-permute-start | bytes 52232 | tf_op jit(solution)/shard_map/ppermute | solution.py:383
  561.1 69.8 %collective-permute-start.39 = (bf16[512,1536]{1,0:T(8,128)(2,1)}, bf16[512,1536]{1,0:T(8,128)(2,1)}, u32[]{:S(2)}, u32[]{:S(2)}) collective-permute-start(bf16[512,1536]{1,0:T(8,128)(2,1)} %pad_maximum_fusion.2), channel_id=1, source_target_pairs={{0,8},{4,12},{8,0},{12,4},{16,24},{20,28},{24,16},{28,20},{1,9},{5... | collective-permute-start | bytes 4718600 | tf_op jit(solution)/shard_map/ppermute | solution.py:354
  614.5 72.8 %collective-permute-start.31 = (bf16[256,2048]{1,0:T(8,128)(2,1)}, bf16[256,2048]{1,0:T(8,128)(2,1)}, u32[]{:S(2)}, u32[]{:S(2)}) collective-permute-start(bf16[256,2048]{1,0:T(8,128)(2,1)} %add_convert_fusion.5), channel_id=1, source_target_pairs={{0,1},{1,2},{2,3},{3,0},{4,5},{5,6},{6,7},{7,4},{8,9},{9,10},{10,1... | collective-permute-start | bytes 3145736 | tf_op jit(solution)/shard_map/ppermute | solution.py:325
  616.4 70.8 %all-to-all-start.2 = ((bf16[4,512,256]{2,1,0:T(8,128)(2,1)}), bf16[4,512,256]{2,1,0:T(8,128)(2,1)}, u32[]{:S(2)}, u32[]{:S(2)}) async-start(bf16[4,512,256]{2,1,0:T(8,128)(2,1)} %bitcast.70), calls=%async_computation.4 | async-start | bytes 2097152 | tf_op jit(solution)/shard_map/all_to_all | solution.py:537
  623.2 64.0 %collective-permute-start.37 = (bf16[256,2048]{1,0:T(8,128)(2,1)S(1)}, bf16[256,2048]{1,0:T(8,128)(2,1)}, u32[]{:S(2)}, u32[]{:S(2)}) collective-permute-start(bf16[256,2048]{1,0:T(8,128)(2,1)S(1)} %add_convert_fusion.4), channel_id=1, source_target_pairs={{0,1},{1,2},{2,3},{3,0},{4,5},{5,6},{6,7},{7,4},{8,9},{9,10},{10,1... | collective-permute-start | bytes 3145736 | tf_op jit(solution)/shard_map/ppermute | solution.py:325
  628.5 58.8 %collective-permute-start.36 = (f32[34,128]{1,0:T(8,128)S(1)}, f32[34,128]{1,0:T(8,128)S(1)}, u32[]{:S(2)}, u32[]{:S(2)}) collective-permute-start(f32[34,128]{1,0:T(8,128)S(1)} %add.250), channel_id=1, source_target_pairs={{0,2},{1,3},{2,0},{3,1},{4,6},{5,7},{6,4},{7,5},{8,10},{9,11},{10,... | collective-permute-start | bytes 52232 | tf_op jit(solution)/shard_map/ppermute | solution.py:383
  (78 other events, 810.1 us)
Sparse Core Ops, SparseCore 0:
  10.5 45.2 all-gather.5
  57.3 45.8 all-gather.7
  107.0 68.8 all-gather.9
  177.6 49.0 all-gather.11
  333.0 58.8 reduce-scatter.3
  433.5 68.8 reduce-scatter.5
  538.0 69.0 reduce-scatter.7

commit v5 on v4

--- a/solution.py
+++ b/solution.py
@@ -478,6 +478,10 @@
     mid_rows, grad_gates, grad_ups = rows_of(mids), column(1), column(2)
     gives = [contract_rows(mid_rows[:, half:], grads).astype(BF16) for grads in (grad_gates, grad_ups)]
     back_order = [relative.index(r) for r in range(dp)]
+    late = [pieces[k][4] for k in range(parts)]
+    down_move, grad_mid_in = barrier((late[1].astype(BF16), grad_mid_in))
+    down_move = around(down_move)
+    late = barrier((late, grad_mid_in))[0]
     grad_mid_in = shuffled(
         grad_mid_in, jnp.asarray(back_order, jnp.int32)[mine ^ jnp.arange(dp, dtype=jnp.int32)]
     )
@@ -485,8 +489,6 @@
     part_mid = jnp.sum(grad_mid_in * normal_mid, axis=0)
     grad_resid_b = grad_resid.astype(BF16)
 
-    late = barrier(([pieces[k][4] for k in range(parts)], grad_resid_b))[0]
-    down_move = around(late[1].astype(BF16))
     grad_mixed = contract_cols(grad_resid_b, output_w).astype(BF16)
     grad_mixed = grad_mixed.reshape(rows, parts, heads * head_size).transpose(1, 0, 2)
     grad_attn = lax.all_to_all(grad_mixed, "tensor", 0, 0, tiled=True)
@@ -517,6 +519,7 @@
 
     def gain_filler():
         packed = jnp.concatenate([part_pre, part_mid, gain_parts[0], gain_parts[1]])
+        packed = barrier((packed, tied[0][0]))[0]
         return butterfly(packed.reshape(-1, 128)).reshape(-1)
 
     part_qkv = contract_rows(normed_full, grad_qkv).astype(BF16)

time: 740 us -> 708 us (0.957)
  waiting for transfers between devices: 359 us -> 333 us
  starting transfers between devices: 48.2 us -> 40.6 us
    ppermute x5, waiting for transfers between devices: 102 us -> 61.2 us  [butterfly(): lax.ppermute(values, axis, [(i, i ^ 1 << bit) for i in range(size)])]
    ppermute x18, waiting for transfers between devices: 205 us -> 220 us  [around(): return lax.ppermute(block, 'tensor', ring)]
  transfers between devices with their start and end apart: 53 -> 53, of which waited for: 23 -> 25; matrix products, arithmetic and copies ran while one was open for 23% -> 24% of each run, Pallas kernels for 12% -> 13%
where the time goes in v5:
time: 708 us; the launch traced here: 699 us
  waiting for transfers between devices  333 us (47%)
  Pallas kernels  108 us (15%)
  matrix products  84 us (12%)
  other arithmetic  72.3 us (10%)
  starting transfers between devices  40.6 us (6%)
  local copies, waits for them, and re-layouts  34.8 us (5%)
  between operations  15.1 us (2%)
  blocking collectives  10.5 us (1%)
    ppermute x18, waiting for transfers between devices, around(): return lax.ppermute(block, 'tensor', ring)  220 us
    pallas_call x4, Pallas kernels, hidden_piece(): pl.pallas_call(functools.partial(hidden_kernel, blocks), grid=(units // t...  71.8 us
    ppermute x5, waiting for transfers between devices, butterfly(): lax.ppermute(values, axis, [(i, i ^ 1 << bit) for i in range(size)])  61.2 us
    dot_general x7, matrix products, contract_rows(): lax.dot_general(left, right, (((0,), (0,)), ((), ())), preferred_element_...  47.1 us
    all_gather x1, waiting for transfers between devices, on_device(): output_w = lax.all_gather(w_output, 'tensor', axis=0, tiled=True)  25.3 us
    dot_general x5, matrix products, dot(): return jnp.dot(left, right, preferred_element_type=F32)  19 us
    pallas_call x1, Pallas kernels, backward_heads(): pl.pallas_call(functools.partial(attention_backward, group, size, heads,...  18.7 us
    dot_general x5, matrix products, contract_cols(): lax.dot_general(left, right, (((1,), (1,)), ((), ())), preferred_element_...  17.9 us
  transfers between devices with their start and end apart: 53, of which 25 were waited for; matrix products, arithmetic and copies ran while one was open for 24% of the time, Pallas kernels for 13%

profile of v5, /device:TPU:0, one launch (start us, length us, event | category | flops | bytes accessed | tf_op | source)
XLA Modules:
  0.0 699.2 jit_solution(16638567772111797156)
XLA Ops:
  23.4 14.5 %collective-permute-done.2 = bf16[256,2048]{1,0:T(8,128)(2,1)} collective-permute-done((bf16[256,2048]{1,0:T(8,128)(2,1)}, bf16[256,2048]{1,0:T(8,128)(2,1)}, u32[]{:S(2)}, u32[]{:S(2)}) %collective-permute-start.2) | collective-permute-done | bytes 1048608 | tf_op jit(solution)/shard_map/ppermute | solution.py:325
  38.0 10.5 %all-gather = bf16[8,1,640]{2,1,0:T(2,128)(2,1)S(1)} all-gather(bf16[1,1,640]{2,1,0:T(2,128)(2,1)S(1)} %bitcast.88), channel_id=1, replica_groups=mesh['dp'=8,'tensor'=4] {'dp'}, dimensions={0}, use_global_device_ids=true | all-gather | bytes 11520 | tf_op jit(solution)/shard_map/all_gather | solution.py:406
  56.5 7.8 %collective-permute-done.3 = bf16[256,2048]{1,0:T(8,128)(2,1)S(1)} collective-permute-done((bf16[256,2048]{1,0:T(8,128)(2,1)}, bf16[256,2048]{1,0:T(8,128)(2,1)S(1)}, u32[]{:S(2)}, u32[]{:S(2)}) %collective-permute-start.3) | collective-permute-done | bytes 1048608 | tf_op jit(solution)/shard_map/ppermute | solution.py:325
  77.9 25.3 %all-gather.8.cloned.1.call-done = bf16[2048,256]{1,0:T(8,128)(2,1)} async-done(((bf16[512,256]{1,0:T(8,128)(2,1)}), bf16[2048,256]{1,0:T(8,128)(2,1)}) %all-gather.8.cloned.1.call-update) | async-done | bytes 1048592 | tf_op jit(solution)/shard_map/all_gather | solution.py:405
  113.8 11.2 %attention_forward.1 = (bf16[1024,512]{1,0:T(8,128)(2,1)}, f32[2,2,1024]{2,1,0:T(2,128)}) custom-call(f32[1024,1024]{1,0:T(8,128)} %convolution_dynamic-update-slice_fusion.q_ref.k_ref.v_ref, f32[1024,1024]{1,0:T(8,128)} %convolution_dynamic-update-slice_fusion.q_ref.k_ref.v_ref, f32[1024,1024]{1,0:T(8,128)} %convolution_dynamic-update-slice_fusion.q_ref.k_ref.v_ref, ...), custom_call_target="tpu_custom_call" | custom-call | flops 2147483648 | bytes 5242880 | tf_op jit(solution)/shard_map/attention_forward/pallas_call | solution.py:240
  125.0 7.9 %collective-permute-done.9.refs_17_ = bf16[256,2048]{1,0:T(8,128)(2,1)S(1)} collective-permute-done((bf16[256,2048]{1,0:T(8,128)(2,1)}, bf16[256,2048]{1,0:T(8,128)(2,1)S(1)}, u32[]{:S(2)}, u32[]{:S(2)}) %collective-permute-start.9) | collective-permute-done | bytes 1048608 | tf_op jit(solution)/shard_map/ppermute | solution.py:325
  145.7 34.7 %collective-permute-done.10.refs_17_ = bf16[256,2048]{1,0:T(8,128)(2,1)S(1)} collective-permute-done((bf16[256,2048]{1,0:T(8,128)(2,1)}, bf16[256,2048]{1,0:T(8,128)(2,1)S(1)}, u32[]{:S(2)}, u32[]{:S(2)}) %collective-permute-start.10) | collective-permute-done | bytes 1048608 | tf_op jit(solution)/shard_map/ppermute | solution.py:325
  185.0 6.2 collective-permute-done.5.refs_3_
  193.2 6.2 multiply_reduce_fusion.2
  206.1 24.7 %collective-permute-done.19.refs_16_ = bf16[256,2048]{1,0:T(8,128)(2,1)} collective-permute-done((bf16[256,2048]{1,0:T(8,128)(2,1)}, bf16[256,2048]{1,0:T(8,128)(2,1)}, u32[]{:S(2)}, u32[]{:S(2)}) %collective-permute-start.19) | collective-permute-done | bytes 1048608 | tf_op jit(solution)/shard_map/ppermute | solution.py:325
  232.0 17.9 %hidden_piece.4 = (bf16[256,1536]{1,0:T(8,128)(2,1)}, bf16[256,1536]{1,0:T(8,128)(2,1)}, bf16[256,1536]{1,0:T(8,128)(2,1)}, f32[256,2048]{1,0:T(8,128)}, f32[256,2048]{1,0:T(8,128)}) custom-call(bf16[256,1536]{1,0:T(8,128)(2,1)} %bitcast.63.refs_0_, bf16[256,1536]{1,0:T(8,128)(2,1)} %collective-permute-done.refs_1_, ...), custom_call_target="tpu_custom_call" | custom-call | flops 9663676416 | bytes 27525120 | tf_op jit(solution)/shard_map/hidden_piece/pallas_call | solution.py:187
  249.9 9.0 %collective-permute-done.20.refs_16_ = bf16[256,2048]{1,0:T(8,128)(2,1)} collective-permute-done((bf16[256,2048]{1,0:T(8,128)(2,1)}, bf16[256,2048]{1,0:T(8,128)(2,1)}, u32[]{:S(2)}, u32[]{:S(2)}) %collective-permute-start.20) | collective-permute-done | bytes 1048608 | tf_op jit(solution)/shard_map/ppermute | solution.py:325
  259.1 17.8 %hidden_piece.5 = (bf16[256,1536]{1,0:T(8,128)(2,1)}, bf16[256,1536]{1,0:T(8,128)(2,1)}, bf16[256,1536]{1,0:T(8,128)(2,1)}, f32[256,2048]{1,0:T(8,128)}, f32[256,2048]{1,0:T(8,128)}) custom-call(bf16[256,1536]{1,0:T(8,128)(2,1)} %bitcast.63.refs_0_, bf16[256,1536]{1,0:T(8,128)(2,1)} %collective-permute-done.refs_1_, ...), custom_call_target="tpu_custom_call" | custom-call | flops 9663676416 | bytes 27525120 | tf_op jit(solution)/shard_map/hidden_piece/pallas_call | solution.py:187
  276.9 17.9 %hidden_piece.6 = (bf16[256,1536]{1,0:T(8,128)(2,1)}, bf16[256,1536]{1,0:T(8,128)(2,1)}, bf16[256,1536]{1,0:T(8,128)(2,1)}, f32[256,2048]{1,0:T(8,128)}, f32[256,2048]{1,0:T(8,128)}) custom-call(bf16[256,1536]{1,0:T(8,128)(2,1)} %bitcast.63.refs_0_, bf16[256,1536]{1,0:T(8,128)(2,1)} %collective-permute-done.refs_1_, ...), custom_call_target="tpu_custom_call" | custom-call | flops 9663676416 | bytes 27525120 | tf_op jit(solution)/shard_map/hidden_piece/pallas_call | solution.py:187
  294.8 7.3 %collective-permute-done.21.refs_16_ = bf16[256,2048]{1,0:T(8,128)(2,1)} collective-permute-done((bf16[256,2048]{1,0:T(8,128)(2,1)}, bf16[256,2048]{1,0:T(8,128)(2,1)}, u32[]{:S(2)}, u32[]{:S(2)}) %collective-permute-start.21) | collective-permute-done | bytes 1048608 | tf_op jit(solution)/shard_map/ppermute | solution.py:325
  302.1 18.2 %hidden_piece.7 = (bf16[256,1536]{1,0:T(8,128)(2,1)}, bf16[256,1536]{1,0:T(8,128)(2,1)}, bf16[256,1536]{1,0:T(8,128)(2,1)}, f32[256,2048]{1,0:T(8,128)}, f32[256,2048]{1,0:T(8,128)}) custom-call(bf16[256,1536]{1,0:T(8,128)(2,1)} %bitcast.63.refs_0_, bf16[256,1536]{1,0:T(8,128)(2,1)} %collective-permute-done.refs_1_, ...), custom_call_target="tpu_custom_call" | custom-call | flops 9663676416 | bytes 27525120 | tf_op jit(solution)/shard_map/hidden_piece/pallas_call | solution.py:187
  320.3 12.5 %convolution_convert_fusion.1 = bf16[1536,2048]{1,0:T(8,128)(2,1)} fusion(bf16[256,2048]{1,0:T(8,128)(2,1)} %collective-permute-done.22.refs_17_, bf16[256,2048]{1,0:T(8,128)(2,1)} %copy-done.56, bf16[256,2048]{1,0:T(8,128)(2,1)} %copy-done.55, bf16[256,2048]{1,0:T(8,128)(2,1)} %refs_17_.1, bf16[256,1536]{1,0:T(8,128)(2,1)} %get-tuple-element.185, ...), kind=kOutput, calls=%fused_computation.2 | convolution fusion | flops 6474956800 | bytes 13631488 | tf_op jit(solution)/shard_map/dot_general | solution.py:29
  334.8 25.2 %collective-permute-done.23 = bf16[256,2048]{1,0:T(8,128)(2,1)S(1)} collective-permute-done((bf16[256,2048]{1,0:T(8,128)(2,1)S(1)}, bf16[256,2048]{1,0:T(8,128)(2,1)S(1)}, u32[]{:S(2)}, u32[]{:S(2)}) %collective-permute-start.23) | collective-permute-done | bytes 1048608 | tf_op jit(solution)/shard_map/ppermute | solution.py:325
  360.3 24.3 %collective-permute-done.24 = bf16[256,2048]{1,0:T(8,128)(2,1)S(1)} collective-permute-done((bf16[256,2048]{1,0:T(8,128)(2,1)S(1)}, bf16[256,2048]{1,0:T(8,128)(2,1)S(1)}, u32[]{:S(2)}, u32[]{:S(2)}) %collective-permute-start.24) | collective-permute-done | bytes 1048608 | tf_op jit(solution)/shard_map/ppermute | solution.py:325
  390.1 19.6 %collective-permute-done.25 = bf16[256,2048]{1,0:T(8,128)(2,1)} collective-permute-done((bf16[256,2048]{1,0:T(8,128)(2,1)}, bf16[256,2048]{1,0:T(8,128)(2,1)}, u32[]{:S(2)}, u32[]{:S(2)}) %collective-permute-start.25) | collective-permute-done | bytes 1048608 | tf_op jit(solution)/shard_map/ppermute | solution.py:325
  419.6 5.7 convolution_convert_fusion.7
  426.9 5.7 convolution_convert_fusion
  440.5 4.8 convolution_convert_fusion.4
  459.8 6.2 convolution_convert_fusion.5
  479.0 22.8 %collective-permute-done.26 = bf16[256,2048]{1,0:T(8,128)(2,1)} collective-permute-done((bf16[256,2048]{1,0:T(8,128)(2,1)}, bf16[256,2048]{1,0:T(8,128)(2,1)}, u32[]{:S(2)}, u32[]{:S(2)}) %collective-permute-start.26) | collective-permute-done | bytes 1048608 | tf_op jit(solution)/shard_map/ppermute | solution.py:325
  510.9 18.7 %attention_backward.1 = (bf16[1024,1024]{1,0:T(8,128)(2,1)}, f32[2,128]{1,0:T(2,128)}) custom-call(f32[1024,1024]{1,0:T(8,128)} %convolution_dynamic-update-slice_fusion.q_ref.k_ref.v_ref, f32[1024,1024]{1,0:T(8,128)} %convolution_dynamic-update-slice_fusion.q_ref.k_ref.v_ref, f32[1024,1024]{1,0:T(8,128)} %convolution_dynamic-update-slice_fusion.q_ref.k_ref.v_ref, ...), custom_call_target="tpu_custom_call" | custom-call | flops 5368709120 | bytes 7340032 | tf_op jit(solution)/shard_map/attention_backward/pallas_call | solution.py:266
  529.6 9.4 %convolution_convert_fusion.6 = bf16[2048,1024]{1,0:T(8,128)(2,1)} fusion(bf16[1024,2048]{1,0:T(8,128)(2,1)} %fusion.61, bf16[1024,1024]{1,0:T(8,128)(2,1)} %get-tuple-element.207), kind=kOutput, calls=%fused_computation.17 | convolution fusion | flops 4297064448 | bytes 10485760 | tf_op jit(solution)/shard_map/dot_general | solution.py:29
  555.0 17.0 %collective-permute-done.29 = bf16[256,2048]{1,0:T(8,128)(2,1)} collective-permute-done((bf16[256,2048]{1,0:T(8,128)(2,1)S(1)}, bf16[256,2048]{1,0:T(8,128)(2,1)}, u32[]{:S(2)}, u32[]{:S(2)}) %collective-permute-start.29) | collective-permute-done | bytes 1048608 | tf_op jit(solution)/shard_map/ppermute | solution.py:325
  579.4 5.1 all-to-all-start.2
  584.5 33.2 %collective-permute-done.33 = f32[34,128]{1,0:T(8,128)S(1)} collective-permute-done((f32[34,128]{1,0:T(8,128)S(1)}, f32[34,128]{1,0:T(8,128)S(1)}, u32[]{:S(2)}, u32[]{:S(2)}) %collective-permute-start.33) | collective-permute-done | bytes 17440 | tf_op jit(solution)/shard_map/ppermute | solution.py:383
  625.1 26.6 %collective-permute-done.35 = f32[34,128]{1,0:T(8,128)S(1)} collective-permute-done((f32[34,128]{1,0:T(8,128)S(1)}, f32[34,128]{1,0:T(8,128)S(1)}, u32[]{:S(2)}, u32[]{:S(2)}) %collective-permute-start.35) | collective-permute-done | bytes 17440 | tf_op jit(solution)/shard_map/ppermute | solution.py:383
  667.6 6.5 collective-permute-done.42
  (312 shorter events, 203.7 us)
Async XLA Ops:
  7.2 58.8 %all-gather.6.cloned.1.call-start = ((), (), s32[]{:S(2)}) async-start(), calls=%async_computation.6 | async-start | bytes 4718592 | tf_op jit(solution)/shard_map/all_gather | solution.py:390
  9.3 93.9 %all-gather.8.cloned.1.call-start = ((), (), s32[]{:S(2)}) async-start(), calls=%async_computation.7 | async-start | bytes 1310720 | tf_op jit(solution)/shard_map/all_gather | solution.py:405
  9.4 28.6 %collective-permute-start.2 = (bf16[256,2048]{1,0:T(8,128)(2,1)}, bf16[256,2048]{1,0:T(8,128)(2,1)}, u32[]{:S(2)}, u32[]{:S(2)}) collective-permute-start(bf16[256,2048]{1,0:T(8,128)(2,1)} %param.14), channel_id=1, source_target_pairs={{0,1},{1,2},{2,3},{3,0},{4,5},{5,6},{6,7},{7,4},{8,9},{9,10},{10,1... | collective-permute-start | bytes 3145736 | tf_op jit(solution)/shard_map/ppermute | solution.py:325
  15.8 40.7 %collective-permute-start = (bf16[256,1536]{1,0:T(8,128)(2,1)}, bf16[256,1536]{1,0:T(8,128)(2,1)}, u32[]{:S(2)}, u32[]{:S(2)}) collective-permute-start(bf16[256,1536]{1,0:T(8,128)(2,1)} %bitcast.63.refs_0_), channel_id=1, source_target_pairs={{0,8},{4,12},{8,0},{12,4},{16,24},{20,28},{24,16},{28,20},{1,9},{5... | collective-permute-start | bytes 2359304 | tf_op jit(solution)/shard_map/ppermute | solution.py:354
  18.2 38.2 %collective-permute-start.1 = (bf16[256,1536]{1,0:T(8,128)(2,1)}, bf16[256,1536]{1,0:T(8,128)(2,1)}, u32[]{:S(2)}, u32[]{:S(2)}) collective-permute-start(bf16[256,1536]{1,0:T(8,128)(2,1)} %bitcast.62.refs_8_), channel_id=1, source_target_pairs={{0,16},{4,20},{8,24},{12,28},{16,0},{20,4},{24,8},{28,12},{1,17},{... | collective-permute-start | bytes 2359304 | tf_op jit(solution)/shard_map/ppermute | solution.py:354
  48.5 144.7 %all-gather.10.cloned.1.call-start = ((), (), s32[]{:S(2)}) async-start(), calls=%async_computation.8 | async-start | bytes 9437184 | tf_op jit(solution)/shard_map/all_gather | solution.py:429
  64.6 42.3 %collective-permute-start.8 = (bf16[256,2048]{1,0:T(8,128)(2,1)S(1)}, bf16[256,2048]{1,0:T(8,128)(2,1)S(1)}, u32[]{:S(2)}, u32[]{:S(2)}) collective-permute-start(bf16[256,2048]{1,0:T(8,128)(2,1)S(1)} %collective-permute-done.3), channel_id=1, source_target_pairs={{0,1},{1,2},{2,3},{3,0},{4,5},{5,6},{6,7},{7,4},{8,9},{9,10},{10,1... | collective-permute-start | bytes 3145736 | tf_op jit(solution)/shard_map/ppermute | solution.py:325
  106.9 125.1 %all-gather.12.cloned.1.call-start = ((), (), s32[]{:S(2)}) async-start(), calls=%async_computation.9 | async-start | bytes 7077888 | tf_op jit(solution)/shard_map/all_gather | solution.py:431
  135.6 49.4 %all-to-all-start = ((bf16[4,256,512]{1,2,0:T(8,128)(2,1)}), bf16[4,256,512]{1,2,0:T(8,128)(2,1)S(1)}, u32[]{:S(2)}, u32[]{:S(2)}) async-start(bf16[4,256,512]{1,2,0:T(8,128)(2,1)} %copy.37), calls=%async_computation | async-start | bytes 2097152 | tf_op jit(solution)/shard_map/all_to_all | solution.py:437
  139.1 390.5 %reduce-scatter.4.cloned.1.call-start = ((), (), s32[]{:S(2)}) async-start(), calls=%async_computation.10 | async-start | bytes 7077888 | tf_op jit(solution)/shard_map/reduce_scatter | solution.py:349
  139.2 41.2 %collective-permute-start.10 = (bf16[256,2048]{1,0:T(8,128)(2,1)}, bf16[256,2048]{1,0:T(8,128)(2,1)S(1)}, u32[]{:S(2)}, u32[]{:S(2)}) collective-permute-start(bf16[256,2048]{1,0:T(8,128)(2,1)} %copy-done.55), channel_id=1, source_target_pairs={{0,1},{1,2},{2,3},{3,0},{4,5},{5,6},{6,7},{7,4},{8,9},{9,10},{10,1... | collective-permute-start | bytes 3145736 | tf_op jit(solution)/shard_map/ppermute | solution.py:325
  141.1 43.9 %collective-permute-start.4 = (bf16[256,1536]{1,0:T(8,128)(2,1)}, bf16[256,1536]{1,0:T(8,128)(2,1)}, u32[]{:S(2)}, u32[]{:S(2)}) collective-permute-start(bf16[256,1536]{1,0:T(8,128)(2,1)} %bitcast.63.refs_0_), channel_id=1, source_target_pairs={{0,16},{4,20},{8,24},{12,28},{16,0},{20,4},{24,8},{28,12},{1,17},{... | collective-permute-start | bytes 2359304 | tf_op jit(solution)/shard_map/ppermute | solution.py:354
  142.0 49.2 %collective-permute-start.5 = (bf16[256,1536]{1,0:T(8,128)(2,1)}, bf16[256,1536]{1,0:T(8,128)(2,1)}, u32[]{:S(2)}, u32[]{:S(2)}) collective-permute-start(bf16[256,1536]{1,0:T(8,128)(2,1)} %collective-permute-done.refs_1_), channel_id=1, source_target_pairs={{0,16},{4,20},{8,24},{12,28},{16,0},{20,4},{24,8},{28,12},{1,17},{... | collective-permute-start | bytes 2359304 | tf_op jit(solution)/shard_map/ppermute | solution.py:354
  143.1 48.1 %collective-permute-start.6 = (bf16[256,1536]{1,0:T(8,128)(2,1)}, bf16[256,1536]{1,0:T(8,128)(2,1)}, u32[]{:S(2)}, u32[]{:S(2)}) collective-permute-start(bf16[256,1536]{1,0:T(8,128)(2,1)} %bitcast.62.refs_8_), channel_id=1, source_target_pairs={{0,8},{4,12},{8,0},{12,4},{16,24},{20,28},{24,16},{28,20},{1,9},{5... | collective-permute-start | bytes 2359304 | tf_op jit(solution)/shard_map/ppermute | solution.py:354
  144.0 48.1 %collective-permute-start.7 = (bf16[256,1536]{1,0:T(8,128)(2,1)}, bf16[256,1536]{1,0:T(8,128)(2,1)}, u32[]{:S(2)}, u32[]{:S(2)}) collective-permute-start(bf16[256,1536]{1,0:T(8,128)(2,1)} %collective-permute-done.1.refs_10_), channel_id=1, source_target_pairs={{0,8},{4,12},{8,0},{12,4},{16,24},{20,28},{24,16},{28,20},{1,9},{5... | collective-permute-start | bytes 2359304 | tf_op jit(solution)/shard_map/ppermute | solution.py:354
  203.6 27.2 %collective-permute-start.19 = (bf16[256,2048]{1,0:T(8,128)(2,1)}, bf16[256,2048]{1,0:T(8,128)(2,1)}, u32[]{:S(2)}, u32[]{:S(2)}) collective-permute-start(bf16[256,2048]{1,0:T(8,128)(2,1)} %shuffled.2.refs_16_), channel_id=1, source_target_pairs={{0,1},{1,2},{2,3},{3,0},{4,5},{5,6},{6,7},{7,4},{8,9},{9,10},{10,1... | collective-permute-start | bytes 3145736 | tf_op jit(solution)/shard_map/ppermute | solution.py:325
  205.1 26.9 %collective-permute-start.16 = (bf16[256,1536]{1,0:T(8,128)(2,1)}, bf16[256,1536]{1,0:T(8,128)(2,1)}, u32[]{:S(2)}, u32[]{:S(2)}) collective-permute-start(bf16[256,1536]{1,0:T(8,128)(2,1)} %collective-permute-done.6.refs_9_), channel_id=1, source_target_pairs={{0,4},{4,0},{8,12},{12,8},{16,20},{20,16},{24,28},{28,24},{1,5},{5... | collective-permute-start | bytes 2359304 | tf_op jit(solution)/shard_map/ppermute | solution.py:354
  230.8 28.1 %collective-permute-start.20 = (bf16[256,2048]{1,0:T(8,128)(2,1)}, bf16[256,2048]{1,0:T(8,128)(2,1)}, u32[]{:S(2)}, u32[]{:S(2)}) collective-permute-start(bf16[256,2048]{1,0:T(8,128)(2,1)} %collective-permute-done.19.refs_16_), channel_id=1, source_target_pairs={{0,1},{1,2},{2,3},{3,0},{4,5},{5,6},{6,7},{7,4},{8,9},{9,10},{10,1... | collective-permute-start | bytes 3145736 | tf_op jit(solution)/shard_map/ppermute | solution.py:325
  230.8 64.0 %collective-permute-start.22 = (bf16[256,2048]{1,0:T(8,128)(2,1)}, bf16[256,2048]{1,0:T(8,128)(2,1)}, u32[]{:S(2)}, u32[]{:S(2)}) collective-permute-start(bf16[256,2048]{1,0:T(8,128)(2,1)} %copy-done.56), channel_id=1, source_target_pairs={{0,1},{1,2},{2,3},{3,0},{4,5},{5,6},{6,7},{7,4},{8,9},{9,10},{10,1... | collective-permute-start | bytes 3145736 | tf_op jit(solution)/shard_map/ppermute | solution.py:325
  258.9 43.1 %collective-permute-start.21 = (bf16[256,2048]{1,0:T(8,128)(2,1)}, bf16[256,2048]{1,0:T(8,128)(2,1)}, u32[]{:S(2)}, u32[]{:S(2)}) collective-permute-start(bf16[256,2048]{1,0:T(8,128)(2,1)} %collective-permute-done.20.refs_16_), channel_id=1, source_target_pairs={{0,1},{1,2},{2,3},{3,0},{4,5},{5,6},{6,7},{7,4},{8,9},{9,10},{10,1... | collective-permute-start | bytes 3145736 | tf_op jit(solution)/shard_map/ppermute | solution.py:325
  332.8 239.2 %reduce-scatter.6.cloned.1.call-start = ((), (), s32[]{:S(2)}) async-start(), calls=%async_computation.11 | async-start | bytes 9437184 | tf_op jit(solution)/shard_map/reduce_scatter | solution.py:349
  453.3 53.0 %all-to-all-start.1 = ((bf16[4,256,512]{2,1,0:T(8,128)(2,1)}), bf16[4,256,512]{2,1,0:T(8,128)(2,1)}, u32[]{:S(2)}, u32[]{:S(2)}) async-start(bf16[4,256,512]{2,1,0:T(8,128)(2,1)} %bitcast.67), calls=%async_computation.1 | async-start | bytes 2097152 | tf_op jit(solution)/shard_map/all_to_all | solution.py:494
  457.6 206.2 %reduce-scatter.8.cloned.1.call-start = ((), (), s32[]{:S(2)}) async-start(), calls=%async_computation.12 | async-start | bytes 4718592 | tf_op jit(solution)/shard_map/reduce_scatter | solution.py:349
  457.7 44.1 %collective-permute-start.26 = (bf16[256,2048]{1,0:T(8,128)(2,1)}, bf16[256,2048]{1,0:T(8,128)(2,1)}, u32[]{:S(2)}, u32[]{:S(2)}) collective-permute-start(bf16[256,2048]{1,0:T(8,128)(2,1)} %convert_element_type.229), channel_id=1, source_target_pairs={{0,1},{1,2},{2,3},{3,0},{4,5},{5,6},{6,7},{7,4},{8,9},{9,10},{10,1... | collective-permute-start | bytes 3145736 | tf_op jit(solution)/shard_map/ppermute | solution.py:325
  509.6 45.5 %collective-permute-start.30 = (bf16[256,2048]{1,0:T(8,128)(2,1)}, bf16[256,2048]{1,0:T(8,128)(2,1)}, u32[]{:S(2)}, u32[]{:S(2)}) collective-permute-start(bf16[256,2048]{1,0:T(8,128)(2,1)} %add_convert_fusion.6), channel_id=1, source_target_pairs={{0,1},{1,2},{2,3},{3,0},{4,5},{5,6},{6,7},{7,4},{8,9},{9,10},{10,1... | collective-permute-start | bytes 3145736 | tf_op jit(solution)/shard_map/ppermute | solution.py:325
  539.7 82.5 %collective-permute-start.38 = (bf16[512,1536]{1,0:T(8,128)(2,1)}, bf16[512,1536]{1,0:T(8,128)(2,1)}, u32[]{:S(2)}, u32[]{:S(2)}) collective-permute-start(bf16[512,1536]{1,0:T(8,128)(2,1)} %pad_maximum_fusion.1), channel_id=1, source_target_pairs={{0,16},{4,20},{8,24},{12,28},{16,0},{20,4},{24,8},{28,12},{1,17},{... | collective-permute-start | bytes 4718600 | tf_op jit(solution)/shard_map/ppermute | solution.py:354
  574.8 76.9 %collective-permute-start.39 = (bf16[512,1536]{1,0:T(8,128)(2,1)}, bf16[512,1536]{1,0:T(8,128)(2,1)}, u32[]{:S(2)}, u32[]{:S(2)}) collective-permute-start(bf16[512,1536]{1,0:T(8,128)(2,1)} %pad_maximum_fusion.2), channel_id=1, source_target_pairs={{0,8},{4,12},{8,0},{12,4},{16,24},{20,28},{24,16},{28,20},{1,9},{5... | collective-permute-start | bytes 4718600 | tf_op jit(solution)/shard_map/ppermute | solution.py:354
  574.8 42.9 %collective-permute-start.33 = (f32[34,128]{1,0:T(8,128)S(1)}, f32[34,128]{1,0:T(8,128)S(1)}, u32[]{:S(2)}, u32[]{:S(2)}) collective-permute-start(f32[34,128]{1,0:T(8,128)S(1)} %bitcast_add_fusion), channel_id=1, source_target_pairs={{0,8},{4,12},{8,0},{12,4},{16,24},{20,28},{24,16},{28,20},{1,9},{5... | collective-permute-start | bytes 52232 | tf_op jit(solution)/shard_map/ppermute | solution.py:383
  579.4 77.0 %collective-permute-start.31 = (bf16[256,2048]{1,0:T(8,128)(2,1)}, bf16[256,2048]{1,0:T(8,128)(2,1)}, u32[]{:S(2)}, u32[]{:S(2)}) collective-permute-start(bf16[256,2048]{1,0:T(8,128)(2,1)} %add_convert_fusion.5), channel_id=1, source_target_pairs={{0,1},{1,2},{2,3},{3,0},{4,5},{5,6},{6,7},{7,4},{8,9},{9,10},{10,1... | collective-permute-start | bytes 3145736 | tf_op jit(solution)/shard_map/ppermute | solution.py:325
  579.4 77.0 %all-to-all-start.2 = ((bf16[4,512,256]{2,1,0:T(8,128)(2,1)}), bf16[4,512,256]{2,1,0:T(8,128)(2,1)}, u32[]{:S(2)}, u32[]{:S(2)}) async-start(bf16[4,512,256]{2,1,0:T(8,128)(2,1)} %bitcast.68), calls=%async_computation.4 | async-start | bytes 2097152 | tf_op jit(solution)/shard_map/all_to_all | solution.py:540
  620.1 36.3 %collective-permute-start.37 = (bf16[256,2048]{1,0:T(8,128)(2,1)S(1)}, bf16[256,2048]{1,0:T(8,128)(2,1)}, u32[]{:S(2)}, u32[]{:S(2)}) collective-permute-start(bf16[256,2048]{1,0:T(8,128)(2,1)S(1)} %add_convert_fusion.4), channel_id=1, source_target_pairs={{0,1},{1,2},{2,3},{3,0},{4,5},{5,6},{6,7},{7,4},{8,9},{9,10},{10,1... | collective-permute-start | bytes 3145736 | tf_op jit(solution)/shard_map/ppermute | solution.py:325
  621.6 30.1 %collective-permute-start.35 = (f32[34,128]{1,0:T(8,128)S(1)}, f32[34,128]{1,0:T(8,128)S(1)}, u32[]{:S(2)}, u32[]{:S(2)}) collective-permute-start(f32[34,128]{1,0:T(8,128)S(1)} %add.249), channel_id=1, source_target_pairs={{0,1},{1,0},{2,3},{3,2},{4,5},{5,4},{6,7},{7,6},{8,9},{9,8},{10,11... | collective-permute-start | bytes 52232 | tf_op jit(solution)/shard_map/ppermute | solution.py:383
  (79 other events, 852.9 us)
Sparse Core Ops, SparseCore 0:
  10.5 45.2 all-gather.5
  57.3 45.8 all-gather.7
  107.0 68.8 all-gather.9
  177.6 49.0 all-gather.11
  332.9 58.8 reduce-scatter.3
  432.7 68.8 reduce-scatter.5
  539.2 67.7 reduce-scatter.7

commit v6 on v5

--- a/solution.py
+++ b/solution.py
@@ -526,7 +526,7 @@
     moves = [down_move, held]
 
     def first_filler():
-        return part_qkv, [moves[0], summed_output]
+        return part_qkv, [moves[0]]
 
     def second_filler():
         return gain_filler(), moves
@@ -534,22 +534,17 @@
     def down_step(k, down_move):
         return around((late[k] + down_move.astype(F32)).astype(BF16)) if k < parts else down_move
 
-    def first_step(tied):
-        down_move, summed = tied
-        moves[0] = down_step(3, down_move)
-        blocks = lax.all_to_all(
-            summed.reshape(parts, summed.shape[0] // parts, summed.shape[1]), "tensor", 0, 0, tiled=True
-        )
-        moves.append(blocks)
-
     tied = []
 
     def late_filler():
-        first_step(tied[0])
+        moves[0] = down_step(3, tied[0][0])
+        moves.append(summed_output)
         return second_filler()
 
     grad_pre_in, made = scatter_ring(lambda k: grads_in[k], (first_filler, late_filler), tied)
-    gain_sums, (down_move, held, blocks) = made[1]
+    gain_sums, (down_move, held, summed_output) = made[1]
+    blocks = summed_output.reshape(parts, summed_output.shape[0] // parts, summed_output.shape[1])
+    blocks = lax.all_to_all(blocks, "tensor", 0, 0, tiled=True)
     for k in range(4, parts):
         down_move = down_step(k, down_move)
     for at in range(1, bits - 1):

time: 708 us -> 723 us (1.021)
  waiting for transfers between devices: 333 us -> 347 us
    all_to_all x1, waiting for transfers between devices: 0.01 us -> 13 us  [on_device(): blocks = lax.all_to_all(blocks, 'tensor', 0, 0, tiled=True)]
  transfers between devices with their start and end apart: 53 -> 53, of which waited for: 25 -> 25; matrix products, arithmetic and copies ran while one was open for 24% -> 23% of each run, Pallas kernels for 13% -> 13%
where the time goes in v6:
time: 723 us; the launch traced here: 715 us
  waiting for transfers between devices  347 us (48%)
  Pallas kernels  108 us (15%)
  matrix products  83.8 us (12%)
  other arithmetic  69 us (10%)
  starting transfers between devices  44 us (6%)
  local copies, waits for them, and re-layouts  37.9 us (5%)
  between operations  15.1 us (2%)
  blocking collectives  10.6 us (1%)
    ppermute x18, waiting for transfers between devices, around(): return lax.ppermute(block, 'tensor', ring)  219 us
    pallas_call x4, Pallas kernels, hidden_piece(): pl.pallas_call(functools.partial(hidden_kernel, blocks), grid=(units // t...  71.6 us
    ppermute x5, waiting for transfers between devices, butterfly(): lax.ppermute(values, axis, [(i, i ^ 1 << bit) for i in range(size)])  66.5 us
    dot_general x7, matrix products, contract_rows(): lax.dot_general(left, right, (((0,), (0,)), ((), ())), preferred_element_...  46 us
    all_gather x1, waiting for transfers between devices, on_device(): output_w = lax.all_gather(w_output, 'tensor', axis=0, tiled=True)  25.3 us
    dot_general x5, matrix products, dot(): return jnp.dot(left, right, preferred_element_type=F32)  19.1 us
    dot_general x5, matrix products, contract_cols(): lax.dot_general(left, right, (((1,), (1,)), ((), ())), preferred_element_...  18.7 us
    pallas_call x1, Pallas kernels, backward_heads(): pl.pallas_call(functools.partial(attention_backward, group, size, heads,...  18.3 us
  transfers between devices with their start and end apart: 53, of which 25 were waited for; matrix products, arithmetic and copies ran while one was open for 23% of the time, Pallas kernels for 13%

profile of v6, /device:TPU:0, one launch (start us, length us, event | category | flops | bytes accessed | tf_op | source)
XLA Modules:
  0.0 714.9 jit_solution(13915025761794170373)
XLA Ops:
  23.5 14.4 %collective-permute-done.2 = bf16[256,2048]{1,0:T(8,128)(2,1)} collective-permute-done((bf16[256,2048]{1,0:T(8,128)(2,1)}, bf16[256,2048]{1,0:T(8,128)(2,1)}, u32[]{:S(2)}, u32[]{:S(2)}) %collective-permute-start.2) | collective-permute-done | bytes 1048608 | tf_op jit(solution)/shard_map/ppermute | solution.py:325
  38.0 10.6 %all-gather = bf16[8,1,640]{2,1,0:T(2,128)(2,1)S(1)} all-gather(bf16[1,1,640]{2,1,0:T(2,128)(2,1)S(1)} %bitcast.88), channel_id=1, replica_groups=mesh['dp'=8,'tensor'=4] {'dp'}, dimensions={0}, use_global_device_ids=true | all-gather | bytes 11520 | tf_op jit(solution)/shard_map/all_gather | solution.py:406
  56.5 7.8 %collective-permute-done.3 = bf16[256,2048]{1,0:T(8,128)(2,1)S(1)} collective-permute-done((bf16[256,2048]{1,0:T(8,128)(2,1)}, bf16[256,2048]{1,0:T(8,128)(2,1)S(1)}, u32[]{:S(2)}, u32[]{:S(2)}) %collective-permute-start.3) | collective-permute-done | bytes 1048608 | tf_op jit(solution)/shard_map/ppermute | solution.py:325
  77.9 25.3 %all-gather.8.cloned.1.call-done = bf16[2048,256]{1,0:T(8,128)(2,1)} async-done(((bf16[512,256]{1,0:T(8,128)(2,1)}), bf16[2048,256]{1,0:T(8,128)(2,1)}) %all-gather.8.cloned.1.call-update) | async-done | bytes 1048592 | tf_op jit(solution)/shard_map/all_gather | solution.py:405
  113.9 11.2 %attention_forward.1 = (bf16[1024,512]{1,0:T(8,128)(2,1)}, f32[2,2,1024]{2,1,0:T(2,128)}) custom-call(f32[1024,1024]{1,0:T(8,128)} %convolution_dynamic-update-slice_fusion.q_ref.k_ref.v_ref, f32[1024,1024]{1,0:T(8,128)} %convolution_dynamic-update-slice_fusion.q_ref.k_ref.v_ref, f32[1024,1024]{1,0:T(8,128)} %convolution_dynamic-update-slice_fusion.q_ref.k_ref.v_ref, ...), custom_call_target="tpu_custom_call" | custom-call | flops 2147483648 | bytes 5242880 | tf_op jit(solution)/shard_map/attention_forward/pallas_call | solution.py:240
  125.1 7.9 %collective-permute-done.9.refs_17_ = bf16[256,2048]{1,0:T(8,128)(2,1)} collective-permute-done((bf16[256,2048]{1,0:T(8,128)(2,1)}, bf16[256,2048]{1,0:T(8,128)(2,1)}, u32[]{:S(2)}, u32[]{:S(2)}) %collective-permute-start.9) | collective-permute-done | bytes 1048608 | tf_op jit(solution)/shard_map/ppermute | solution.py:325
  145.4 34.7 %collective-permute-done.10.refs_17_ = bf16[256,2048]{1,0:T(8,128)(2,1)S(1)} collective-permute-done((bf16[256,2048]{1,0:T(8,128)(2,1)}, bf16[256,2048]{1,0:T(8,128)(2,1)S(1)}, u32[]{:S(2)}, u32[]{:S(2)}) %collective-permute-start.10) | collective-permute-done | bytes 1048608 | tf_op jit(solution)/shard_map/ppermute | solution.py:325
  184.7 6.1 collective-permute-done.5.refs_3_
  192.7 6.2 multiply_reduce_fusion.2
  205.6 24.7 %collective-permute-done.19.refs_16_ = bf16[256,2048]{1,0:T(8,128)(2,1)} collective-permute-done((bf16[256,2048]{1,0:T(8,128)(2,1)}, bf16[256,2048]{1,0:T(8,128)(2,1)}, u32[]{:S(2)}, u32[]{:S(2)}) %collective-permute-start.19) | collective-permute-done | bytes 1048608 | tf_op jit(solution)/shard_map/ppermute | solution.py:325
  231.5 17.9 %hidden_piece.4 = (bf16[256,1536]{1,0:T(8,128)(2,1)}, bf16[256,1536]{1,0:T(8,128)(2,1)}, bf16[256,1536]{1,0:T(8,128)(2,1)}, f32[256,2048]{1,0:T(8,128)}, f32[256,2048]{1,0:T(8,128)}) custom-call(bf16[256,1536]{1,0:T(8,128)(2,1)} %bitcast.63.refs_0_, bf16[256,1536]{1,0:T(8,128)(2,1)} %collective-permute-done.refs_1_, ...), custom_call_target="tpu_custom_call" | custom-call | flops 9663676416 | bytes 27525120 | tf_op jit(solution)/shard_map/hidden_piece/pallas_call | solution.py:187
  249.4 9.0 %collective-permute-done.20.refs_16_ = bf16[256,2048]{1,0:T(8,128)(2,1)} collective-permute-done((bf16[256,2048]{1,0:T(8,128)(2,1)}, bf16[256,2048]{1,0:T(8,128)(2,1)}, u32[]{:S(2)}, u32[]{:S(2)}) %collective-permute-start.20) | collective-permute-done | bytes 1048608 | tf_op jit(solution)/shard_map/ppermute | solution.py:325
  258.7 17.8 %hidden_piece.5 = (bf16[256,1536]{1,0:T(8,128)(2,1)}, bf16[256,1536]{1,0:T(8,128)(2,1)}, bf16[256,1536]{1,0:T(8,128)(2,1)}, f32[256,2048]{1,0:T(8,128)}, f32[256,2048]{1,0:T(8,128)}) custom-call(bf16[256,1536]{1,0:T(8,128)(2,1)} %bitcast.63.refs_0_, bf16[256,1536]{1,0:T(8,128)(2,1)} %collective-permute-done.refs_1_, ...), custom_call_target="tpu_custom_call" | custom-call | flops 9663676416 | bytes 27525120 | tf_op jit(solution)/shard_map/hidden_piece/pallas_call | solution.py:187
  276.5 17.7 %hidden_piece.6 = (bf16[256,1536]{1,0:T(8,128)(2,1)}, bf16[256,1536]{1,0:T(8,128)(2,1)}, bf16[256,1536]{1,0:T(8,128)(2,1)}, f32[256,2048]{1,0:T(8,128)}, f32[256,2048]{1,0:T(8,128)}) custom-call(bf16[256,1536]{1,0:T(8,128)(2,1)} %bitcast.63.refs_0_, bf16[256,1536]{1,0:T(8,128)(2,1)} %collective-permute-done.refs_1_, ...), custom_call_target="tpu_custom_call" | custom-call | flops 9663676416 | bytes 27525120 | tf_op jit(solution)/shard_map/hidden_piece/pallas_call | solution.py:187
  294.2 7.4 %collective-permute-done.21.refs_16_ = bf16[256,2048]{1,0:T(8,128)(2,1)} collective-permute-done((bf16[256,2048]{1,0:T(8,128)(2,1)}, bf16[256,2048]{1,0:T(8,128)(2,1)}, u32[]{:S(2)}, u32[]{:S(2)}) %collective-permute-start.21) | collective-permute-done | bytes 1048608 | tf_op jit(solution)/shard_map/ppermute | solution.py:325
  301.6 18.2 %hidden_piece.7 = (bf16[256,1536]{1,0:T(8,128)(2,1)}, bf16[256,1536]{1,0:T(8,128)(2,1)}, bf16[256,1536]{1,0:T(8,128)(2,1)}, f32[256,2048]{1,0:T(8,128)}, f32[256,2048]{1,0:T(8,128)}) custom-call(bf16[256,1536]{1,0:T(8,128)(2,1)} %bitcast.63.refs_0_, bf16[256,1536]{1,0:T(8,128)(2,1)} %collective-permute-done.refs_1_, ...), custom_call_target="tpu_custom_call" | custom-call | flops 9663676416 | bytes 27525120 | tf_op jit(solution)/shard_map/hidden_piece/pallas_call | solution.py:187
  319.8 12.5 %convolution_convert_fusion.1 = bf16[1536,2048]{1,0:T(8,128)(2,1)} fusion(bf16[256,2048]{1,0:T(8,128)(2,1)} %collective-permute-done.22.refs_17_, bf16[256,2048]{1,0:T(8,128)(2,1)} %copy-done.52, bf16[256,2048]{1,0:T(8,128)(2,1)} %collective-permute-done.9.refs_17_, bf16[256,2048]{1,0:T(8,128)(2,1)} %refs_17_.1, bf16[256,1536]{1,0:T(8,128)(2,1)} %get-tuple-element.184, ...), kind=kOutput, calls=%fused_computation.2 | convolution fusion | flops 6474956800 | bytes 13631488 | tf_op jit(solution)/shard_map/dot_general | solution.py:29
  334.3 25.2 %collective-permute-done.23 = bf16[256,2048]{1,0:T(8,128)(2,1)S(1)} collective-permute-done((bf16[256,2048]{1,0:T(8,128)(2,1)S(1)}, bf16[256,2048]{1,0:T(8,128)(2,1)S(1)}, u32[]{:S(2)}, u32[]{:S(2)}) %collective-permute-start.23) | collective-permute-done | bytes 1048608 | tf_op jit(solution)/shard_map/ppermute | solution.py:325
  361.9 23.4 %collective-permute-done.24 = bf16[256,2048]{1,0:T(8,128)(2,1)} collective-permute-done((bf16[256,2048]{1,0:T(8,128)(2,1)}, bf16[256,2048]{1,0:T(8,128)(2,1)}, u32[]{:S(2)}, u32[]{:S(2)}) %collective-permute-start.24) | collective-permute-done | bytes 1048608 | tf_op jit(solution)/shard_map/ppermute | solution.py:325
  390.8 20.5 %collective-permute-done.25 = bf16[256,2048]{1,0:T(8,128)(2,1)S(1)} collective-permute-done((bf16[256,2048]{1,0:T(8,128)(2,1)S(1)}, bf16[256,2048]{1,0:T(8,128)(2,1)S(1)}, u32[]{:S(2)}, u32[]{:S(2)}) %collective-permute-start.25) | collective-permute-done | bytes 1048608 | tf_op jit(solution)/shard_map/ppermute | solution.py:325
  419.8 5.7 convolution_convert_fusion.7
  427.2 5.7 convolution_convert_fusion
  459.7 6.1 convolution_convert_fusion.5
  478.7 22.9 %collective-permute-done.26 = bf16[256,2048]{1,0:T(8,128)(2,1)} collective-permute-done((bf16[256,2048]{1,0:T(8,128)(2,1)}, bf16[256,2048]{1,0:T(8,128)(2,1)}, u32[]{:S(2)}, u32[]{:S(2)}) %collective-permute-start.26) | collective-permute-done | bytes 1048608 | tf_op jit(solution)/shard_map/ppermute | solution.py:325
  512.8 18.3 %attention_backward.1 = (bf16[1024,1024]{1,0:T(8,128)(2,1)}, f32[2,128]{1,0:T(2,128)}) custom-call(f32[1024,1024]{1,0:T(8,128)} %convolution_dynamic-update-slice_fusion.q_ref.k_ref.v_ref, f32[1024,1024]{1,0:T(8,128)} %convolution_dynamic-update-slice_fusion.q_ref.k_ref.v_ref, f32[1024,1024]{1,0:T(8,128)} %convolution_dynamic-update-slice_fusion.q_ref.k_ref.v_ref, ...), custom_call_target="tpu_custom_call" | custom-call | flops 5368709120 | bytes 7340032 | tf_op jit(solution)/shard_map/attention_backward/pallas_call | solution.py:266
  546.5 8.3 %convolution_convert_fusion.6 = bf16[2048,1024]{1,0:T(8,128)(2,1)} fusion(bf16[1024,2048]{1,0:T(8,128)(2,1)} %fusion.61, bf16[1024,1024]{1,0:T(8,128)(2,1)S(1)} %copy-done.33), kind=kOutput, calls=%fused_computation.17 | convolution fusion | flops 4297064448 | bytes 10485760 | tf_op jit(solution)/shard_map/dot_general | solution.py:29
  554.8 8.9 %collective-permute-done.29 = bf16[256,2048]{1,0:T(8,128)(2,1)} collective-permute-done((bf16[256,2048]{1,0:T(8,128)(2,1)}, bf16[256,2048]{1,0:T(8,128)(2,1)}, u32[]{:S(2)}, u32[]{:S(2)}) %collective-permute-start.29) | collective-permute-done | bytes 1048608 | tf_op jit(solution)/shard_map/ppermute | solution.py:325
  570.7 44.3 %collective-permute-done.33 = f32[34,128]{1,0:T(8,128)S(1)} collective-permute-done((f32[34,128]{1,0:T(8,128)S(1)}, f32[34,128]{1,0:T(8,128)S(1)}, u32[]{:S(2)}, u32[]{:S(2)}) %collective-permute-start.33) | collective-permute-done | bytes 17440 | tf_op jit(solution)/shard_map/ppermute | solution.py:383
  622.1 20.4 %collective-permute-done.35 = f32[34,128]{1,0:T(8,128)S(1)} collective-permute-done((f32[34,128]{1,0:T(8,128)S(1)}, f32[34,128]{1,0:T(8,128)S(1)}, u32[]{:S(2)}, u32[]{:S(2)}) %collective-permute-start.35) | collective-permute-done | bytes 17440 | tf_op jit(solution)/shard_map/ppermute | solution.py:383
  654.7 5.3 all-to-all-start.2
  674.9 8.0 %collective-permute-done.40 = bf16[256,2048]{1,0:T(8,128)(2,1)} collective-permute-done((bf16[256,2048]{1,0:T(8,128)(2,1)}, bf16[256,2048]{1,0:T(8,128)(2,1)}, u32[]{:S(2)}, u32[]{:S(2)}) %collective-permute-start.40) | collective-permute-done | bytes 1048608 | tf_op jit(solution)/shard_map/ppermute | solution.py:325
  689.0 13.0 %all-to-all-done.2 = bf16[4,512,256]{2,1,0:T(8,128)(2,1)} async-done(((bf16[4,512,256]{2,1,0:T(8,128)(2,1)}), bf16[4,512,256]{2,1,0:T(8,128)(2,1)}, u32[]{:S(2)}, u32[]{:S(2)}) %all-to-all-start.2) | async-done | bytes 1048608 | tf_op jit(solution)/shard_map/all_to_all | solution.py:547
  (304 shorter events, 214.2 us)
Async XLA Ops:
  7.2 58.8 %all-gather.6.cloned.1.call-start = ((), (), s32[]{:S(2)}) async-start(), calls=%async_computation.6 | async-start | bytes 4718592 | tf_op jit(solution)/shard_map/all_gather | solution.py:390
  9.3 93.9 %all-gather.8.cloned.1.call-start = ((), (), s32[]{:S(2)}) async-start(), calls=%async_computation.7 | async-start | bytes 1310720 | tf_op jit(solution)/shard_map/all_gather | solution.py:405
  9.4 28.6 %collective-permute-start.2 = (bf16[256,2048]{1,0:T(8,128)(2,1)}, bf16[256,2048]{1,0:T(8,128)(2,1)}, u32[]{:S(2)}, u32[]{:S(2)}) collective-permute-start(bf16[256,2048]{1,0:T(8,128)(2,1)} %param.14), channel_id=1, source_target_pairs={{0,1},{1,2},{2,3},{3,0},{4,5},{5,6},{6,7},{7,4},{8,9},{9,10},{10,1... | collective-permute-start | bytes 3145736 | tf_op jit(solution)/shard_map/ppermute | solution.py:325
  15.8 40.7 %collective-permute-start = (bf16[256,1536]{1,0:T(8,128)(2,1)}, bf16[256,1536]{1,0:T(8,128)(2,1)}, u32[]{:S(2)}, u32[]{:S(2)}) collective-permute-start(bf16[256,1536]{1,0:T(8,128)(2,1)} %bitcast.63.refs_0_), channel_id=1, source_target_pairs={{0,8},{4,12},{8,0},{12,4},{16,24},{20,28},{24,16},{28,20},{1,9},{5... | collective-permute-start | bytes 2359304 | tf_op jit(solution)/shard_map/ppermute | solution.py:354
  18.3 38.2 %collective-permute-start.1 = (bf16[256,1536]{1,0:T(8,128)(2,1)}, bf16[256,1536]{1,0:T(8,128)(2,1)}, u32[]{:S(2)}, u32[]{:S(2)}) collective-permute-start(bf16[256,1536]{1,0:T(8,128)(2,1)} %bitcast.62.refs_8_), channel_id=1, source_target_pairs={{0,16},{4,20},{8,24},{12,28},{16,0},{20,4},{24,8},{28,12},{1,17},{... | collective-permute-start | bytes 2359304 | tf_op jit(solution)/shard_map/ppermute | solution.py:354
  48.6 144.1 %all-gather.10.cloned.1.call-start = ((), (), s32[]{:S(2)}) async-start(), calls=%async_computation.8 | async-start | bytes 9437184 | tf_op jit(solution)/shard_map/all_gather | solution.py:429
  64.6 42.3 %collective-permute-start.8 = (bf16[256,2048]{1,0:T(8,128)(2,1)S(1)}, bf16[256,2048]{1,0:T(8,128)(2,1)S(1)}, u32[]{:S(2)}, u32[]{:S(2)}) collective-permute-start(bf16[256,2048]{1,0:T(8,128)(2,1)S(1)} %collective-permute-done.3), channel_id=1, source_target_pairs={{0,1},{1,2},{2,3},{3,0},{4,5},{5,6},{6,7},{7,4},{8,9},{9,10},{10,1... | collective-permute-start | bytes 3145736 | tf_op jit(solution)/shard_map/ppermute | solution.py:325
  106.9 124.7 %all-gather.12.cloned.1.call-start = ((), (), s32[]{:S(2)}) async-start(), calls=%async_computation.9 | async-start | bytes 7077888 | tf_op jit(solution)/shard_map/all_gather | solution.py:431
  135.3 49.4 %all-to-all-start = ((bf16[4,256,512]{1,2,0:T(8,128)(2,1)}), bf16[4,256,512]{1,2,0:T(8,128)(2,1)S(1)}, u32[]{:S(2)}, u32[]{:S(2)}) async-start(bf16[4,256,512]{1,2,0:T(8,128)(2,1)} %copy.37), calls=%async_computation | async-start | bytes 2097152 | tf_op jit(solution)/shard_map/all_to_all | solution.py:437
  138.8 393.0 %reduce-scatter.4.cloned.1.call-start = ((), (), s32[]{:S(2)}) async-start(), calls=%async_computation.10 | async-start | bytes 7077888 | tf_op jit(solution)/shard_map/reduce_scatter | solution.py:349
  138.9 41.2 %collective-permute-start.10 = (bf16[256,2048]{1,0:T(8,128)(2,1)}, bf16[256,2048]{1,0:T(8,128)(2,1)S(1)}, u32[]{:S(2)}, u32[]{:S(2)}) collective-permute-start(bf16[256,2048]{1,0:T(8,128)(2,1)} %collective-permute-done.9.refs_17_), channel_id=1, source_target_pairs={{0,1},{1,2},{2,3},{3,0},{4,5},{5,6},{6,7},{7,4},{8,9},{9,10},{10,1... | collective-permute-start | bytes 3145736 | tf_op jit(solution)/shard_map/ppermute | solution.py:325
  140.8 43.9 %collective-permute-start.4 = (bf16[256,1536]{1,0:T(8,128)(2,1)}, bf16[256,1536]{1,0:T(8,128)(2,1)}, u32[]{:S(2)}, u32[]{:S(2)}) collective-permute-start(bf16[256,1536]{1,0:T(8,128)(2,1)} %bitcast.63.refs_0_), channel_id=1, source_target_pairs={{0,16},{4,20},{8,24},{12,28},{16,0},{20,4},{24,8},{28,12},{1,17},{... | collective-permute-start | bytes 2359304 | tf_op jit(solution)/shard_map/ppermute | solution.py:354
  141.8 49.0 %collective-permute-start.5 = (bf16[256,1536]{1,0:T(8,128)(2,1)}, bf16[256,1536]{1,0:T(8,128)(2,1)}, u32[]{:S(2)}, u32[]{:S(2)}) collective-permute-start(bf16[256,1536]{1,0:T(8,128)(2,1)} %collective-permute-done.refs_1_), channel_id=1, source_target_pairs={{0,16},{4,20},{8,24},{12,28},{16,0},{20,4},{24,8},{28,12},{1,17},{... | collective-permute-start | bytes 2359304 | tf_op jit(solution)/shard_map/ppermute | solution.py:354
  142.9 48.0 %collective-permute-start.6 = (bf16[256,1536]{1,0:T(8,128)(2,1)}, bf16[256,1536]{1,0:T(8,128)(2,1)}, u32[]{:S(2)}, u32[]{:S(2)}) collective-permute-start(bf16[256,1536]{1,0:T(8,128)(2,1)} %bitcast.62.refs_8_), channel_id=1, source_target_pairs={{0,8},{4,12},{8,0},{12,4},{16,24},{20,28},{24,16},{28,20},{1,9},{5... | collective-permute-start | bytes 2359304 | tf_op jit(solution)/shard_map/ppermute | solution.py:354
  143.8 47.8 %collective-permute-start.7 = (bf16[256,1536]{1,0:T(8,128)(2,1)}, bf16[256,1536]{1,0:T(8,128)(2,1)}, u32[]{:S(2)}, u32[]{:S(2)}) collective-permute-start(bf16[256,1536]{1,0:T(8,128)(2,1)} %collective-permute-done.1.refs_10_), channel_id=1, source_target_pairs={{0,8},{4,12},{8,0},{12,4},{16,24},{20,28},{24,16},{28,20},{1,9},{5... | collective-permute-start | bytes 2359304 | tf_op jit(solution)/shard_map/ppermute | solution.py:354
  203.1 27.2 %collective-permute-start.19 = (bf16[256,2048]{1,0:T(8,128)(2,1)}, bf16[256,2048]{1,0:T(8,128)(2,1)}, u32[]{:S(2)}, u32[]{:S(2)}) collective-permute-start(bf16[256,2048]{1,0:T(8,128)(2,1)} %shuffled.2.refs_16_), channel_id=1, source_target_pairs={{0,1},{1,2},{2,3},{3,0},{4,5},{5,6},{6,7},{7,4},{8,9},{9,10},{10,1... | collective-permute-start | bytes 3145736 | tf_op jit(solution)/shard_map/ppermute | solution.py:325
  204.6 26.9 %collective-permute-start.16 = (bf16[256,1536]{1,0:T(8,128)(2,1)}, bf16[256,1536]{1,0:T(8,128)(2,1)}, u32[]{:S(2)}, u32[]{:S(2)}) collective-permute-start(bf16[256,1536]{1,0:T(8,128)(2,1)} %collective-permute-done.6.refs_9_), channel_id=1, source_target_pairs={{0,4},{4,0},{8,12},{12,8},{16,20},{20,16},{24,28},{28,24},{1,5},{5... | collective-permute-start | bytes 2359304 | tf_op jit(solution)/shard_map/ppermute | solution.py:354
  230.3 28.1 %collective-permute-start.20 = (bf16[256,2048]{1,0:T(8,128)(2,1)}, bf16[256,2048]{1,0:T(8,128)(2,1)}, u32[]{:S(2)}, u32[]{:S(2)}) collective-permute-start(bf16[256,2048]{1,0:T(8,128)(2,1)} %collective-permute-done.19.refs_16_), channel_id=1, source_target_pairs={{0,1},{1,2},{2,3},{3,0},{4,5},{5,6},{6,7},{7,4},{8,9},{9,10},{10,1... | collective-permute-start | bytes 3145736 | tf_op jit(solution)/shard_map/ppermute | solution.py:325
  230.3 63.9 %collective-permute-start.22 = (bf16[256,2048]{1,0:T(8,128)(2,1)}, bf16[256,2048]{1,0:T(8,128)(2,1)}, u32[]{:S(2)}, u32[]{:S(2)}) collective-permute-start(bf16[256,2048]{1,0:T(8,128)(2,1)} %copy-done.52), channel_id=1, source_target_pairs={{0,1},{1,2},{2,3},{3,0},{4,5},{5,6},{6,7},{7,4},{8,9},{9,10},{10,1... | collective-permute-start | bytes 3145736 | tf_op jit(solution)/shard_map/ppermute | solution.py:325
  258.5 43.1 %collective-permute-start.21 = (bf16[256,2048]{1,0:T(8,128)(2,1)}, bf16[256,2048]{1,0:T(8,128)(2,1)}, u32[]{:S(2)}, u32[]{:S(2)}) collective-permute-start(bf16[256,2048]{1,0:T(8,128)(2,1)} %collective-permute-done.20.refs_16_), channel_id=1, source_target_pairs={{0,1},{1,2},{2,3},{3,0},{4,5},{5,6},{6,7},{7,4},{8,9},{9,10},{10,1... | collective-permute-start | bytes 3145736 | tf_op jit(solution)/shard_map/ppermute | solution.py:325
  332.3 315.2 %reduce-scatter.6.cloned.1.call-start = ((), (), s32[]{:S(2)}) async-start(), calls=%async_computation.11 | async-start | bytes 9437184 | tf_op jit(solution)/shard_map/reduce_scatter | solution.py:349
  453.2 53.0 %all-to-all-start.1 = ((bf16[4,256,512]{2,1,0:T(8,128)(2,1)}), bf16[4,256,512]{2,1,0:T(8,128)(2,1)}, u32[]{:S(2)}, u32[]{:S(2)}) async-start(bf16[4,256,512]{2,1,0:T(8,128)(2,1)} %bitcast.67), calls=%async_computation.1 | async-start | bytes 2097152 | tf_op jit(solution)/shard_map/all_to_all | solution.py:494
  457.5 246.8 %reduce-scatter.8.cloned.1.call-start = ((), (), s32[]{:S(2)}) async-start(), calls=%async_computation.12 | async-start | bytes 4718592 | tf_op jit(solution)/shard_map/reduce_scatter | solution.py:349
  457.5 44.1 %collective-permute-start.26 = (bf16[256,2048]{1,0:T(8,128)(2,1)}, bf16[256,2048]{1,0:T(8,128)(2,1)}, u32[]{:S(2)}, u32[]{:S(2)}) collective-permute-start(bf16[256,2048]{1,0:T(8,128)(2,1)} %convert_element_type.229), channel_id=1, source_target_pairs={{0,1},{1,2},{2,3},{3,0},{4,5},{5,6},{6,7},{7,4},{8,9},{9,10},{10,1... | collective-permute-start | bytes 3145736 | tf_op jit(solution)/shard_map/ppermute | solution.py:325
  509.4 45.4 %collective-permute-start.30 = (bf16[256,2048]{1,0:T(8,128)(2,1)}, bf16[256,2048]{1,0:T(8,128)(2,1)}, u32[]{:S(2)}, u32[]{:S(2)}) collective-permute-start(bf16[256,2048]{1,0:T(8,128)(2,1)} %add_convert_fusion.6), channel_id=1, source_target_pairs={{0,1},{1,2},{2,3},{3,0},{4,5},{5,6},{6,7},{7,4},{8,9},{9,10},{10,1... | collective-permute-start | bytes 3145736 | tf_op jit(solution)/shard_map/ppermute | solution.py:325
  511.0 108.0 %collective-permute-start.38 = (bf16[512,1536]{1,0:T(8,128)(2,1)}, bf16[512,1536]{1,0:T(8,128)(2,1)}, u32[]{:S(2)}, u32[]{:S(2)}) collective-permute-start(bf16[512,1536]{1,0:T(8,128)(2,1)} %pad_maximum_fusion.1), channel_id=1, source_target_pairs={{0,16},{4,20},{8,24},{12,28},{16,0},{20,4},{24,8},{28,12},{1,17},{... | collective-permute-start | bytes 4718600 | tf_op jit(solution)/shard_map/ppermute | solution.py:354
  566.4 78.1 %collective-permute-start.39 = (bf16[512,1536]{1,0:T(8,128)(2,1)}, bf16[512,1536]{1,0:T(8,128)(2,1)}, u32[]{:S(2)}, u32[]{:S(2)}) collective-permute-start(bf16[512,1536]{1,0:T(8,128)(2,1)} %pad_maximum_fusion.2), channel_id=1, source_target_pairs={{0,8},{4,12},{8,0},{12,4},{16,24},{20,28},{24,16},{28,20},{1,9},{5... | collective-permute-start | bytes 4718600 | tf_op jit(solution)/shard_map/ppermute | solution.py:354
  566.4 48.6 %collective-permute-start.33 = (f32[34,128]{1,0:T(8,128)S(1)}, f32[34,128]{1,0:T(8,128)S(1)}, u32[]{:S(2)}, u32[]{:S(2)}) collective-permute-start(f32[34,128]{1,0:T(8,128)S(1)} %bitcast_add_fusion), channel_id=1, source_target_pairs={{0,8},{4,12},{8,0},{12,4},{16,24},{20,28},{24,16},{28,20},{1,9},{5... | collective-permute-start | bytes 52232 | tf_op jit(solution)/shard_map/ppermute | solution.py:383
  570.7 76.8 %collective-permute-start.31 = (bf16[256,2048]{1,0:T(8,128)(2,1)S(1)}, bf16[256,2048]{1,0:T(8,128)(2,1)}, u32[]{:S(2)}, u32[]{:S(2)}) collective-permute-start(bf16[256,2048]{1,0:T(8,128)(2,1)S(1)} %add_convert_fusion.5), channel_id=1, source_target_pairs={{0,1},{1,2},{2,3},{3,0},{4,5},{5,6},{6,7},{7,4},{8,9},{9,10},{10,1... | collective-permute-start | bytes 3145736 | tf_op jit(solution)/shard_map/ppermute | solution.py:325
  617.1 30.3 %collective-permute-start.37 = (bf16[256,2048]{1,0:T(8,128)(2,1)S(1)}, bf16[256,2048]{1,0:T(8,128)(2,1)}, u32[]{:S(2)}, u32[]{:S(2)}) collective-permute-start(bf16[256,2048]{1,0:T(8,128)(2,1)S(1)} %add_convert_fusion.4), channel_id=1, source_target_pairs={{0,1},{1,2},{2,3},{3,0},{4,5},{5,6},{6,7},{7,4},{8,9},{9,10},{10,1... | collective-permute-start | bytes 3145736 | tf_op jit(solution)/shard_map/ppermute | solution.py:325
  654.7 28.2 %collective-permute-start.40 = (bf16[256,2048]{1,0:T(8,128)(2,1)}, bf16[256,2048]{1,0:T(8,128)(2,1)}, u32[]{:S(2)}, u32[]{:S(2)}) collective-permute-start(bf16[256,2048]{1,0:T(8,128)(2,1)} %add_convert_fusion.2), channel_id=1, source_target_pairs={{0,1},{1,2},{2,3},{3,0},{4,5},{5,6},{6,7},{7,4},{8,9},{9,10},{10,1... | collective-permute-start | bytes 3145736 | tf_op jit(solution)/shard_map/ppermute | solution.py:325
  654.7 47.3 %all-to-all-start.2 = ((bf16[4,512,256]{2,1,0:T(8,128)(2,1)}), bf16[4,512,256]{2,1,0:T(8,128)(2,1)}, u32[]{:S(2)}, u32[]{:S(2)}) async-start(bf16[4,512,256]{2,1,0:T(8,128)(2,1)} %bitcast.68), calls=%async_computation.5 | async-start | bytes 2097152 | tf_op jit(solution)/shard_map/all_to_all | solution.py:547
  (75 other events, 864.9 us)
Sparse Core Ops, SparseCore 0:
  10.5 45.3 all-gather.5
  57.4 45.8 all-gather.7
  107.0 69.0 all-gather.9
  177.9 48.7 all-gather.11
  332.4 58.8 reduce-scatter.3
  433.0 68.8 reduce-scatter.5
  566.5 61.1 reduce-scatter.7
